TPU v7x, 512 devices: a whole 4x8x8 slice. The times are simulated.
512 devices in a mesh: space: 64 (over z_lo, x, y), tm: 8 (over z_hi, core).
Axes of the slice: x: 4, y: 8, z: 8 (z_hi: 4, z_lo: 2; z = z_hi * 2 + z_lo), core: 2. Of those that a mesh axis runs over, the one named last changes fastest.
Arguments:
- source: bfloat16 [16, 128, 4, 2, 3, 16, 128], P('tm', 'space'), may hold values from -6 to 6
- gauge_links: bfloat16 [16, 128, 4, 2, 3, 3, 128], P('tm', 'space'), may hold values from -2.5 to 2.5
- clover: bfloat16 [16, 128, 2, 2, 6, 6, 128], P('tm', 'space'), may hold values from -0.3984375 to 0.3984375
- eigenvectors: bfloat16 [16, 128, 2, 3, 256, 128], P('tm', 'space'), may hold values from -4 to 4
- elemental: bfloat16 [16, 2, 256, 256], P('tm'), may hold values from -0.25 to 0.25
Outputs:
- sink_field: bfloat16 [16, 128, 4, 2, 3, 16, 128], P('tm', 'space')
All inputs are finite; a program needn't handle non-finite values.
Results may differ from a plain program's by a relative error of at most 0.0057.
Values may be sent and summed in bfloat16 or wider, within the bound.
No kernel may reach another device: no remote copies, remote signals or barrier semaphores. Data moves between devices by JAX's collectives and lax.ppermute only.
A program may use at most 64 MiB of HBM per device.

v0:
```python
import jax
import jax.numpy as jnp
from jax import lax
from jax.sharding import PartitionSpec as P

X = 16
Y = 8


HOPPING = 0.125
HALF_MAP = (
    ((1, 0.0, -1.0), (0, 0.0, -1.0)),
    ((1, -1.0, 0.0), (0, 1.0, 0.0)),
    ((0, 0.0, -1.0), (1, 0.0, 1.0)),
    ((0, 1.0, 0.0), (1, 1.0, 0.0)),
)


def passed_along(value, axis, by):
    count = lax.axis_size(axis)
    return lax.ppermute(value, axis, [(i, (i + by) % count) for i in range(count)])


def extended(cells, sides, width):
    for axis, dim in sides:
        count = lax.axis_size(axis)
        head = lax.slice_in_dim(cells, 0, width, axis=dim)
        tail = lax.slice_in_dim(cells, cells.shape[dim] - width, cells.shape[dim], axis=dim)
        cells = jnp.concatenate(
            [
                lax.ppermute(tail, axis, [(i, (i + 1) % count) for i in range(count)]),
                cells,
                lax.ppermute(head, axis, [((i + 1) % count, i) for i in range(count)]),
            ],
            axis=dim,
        )
    return cells


def dagger_map(forward_map):
    result = [None, None]
    for row_number in range(2):
        column, real_coef, imag_coef = forward_map[row_number]
        result[column] = (row_number, real_coef, -imag_coef)
    return tuple(result)


def apply_half(spin_map, half_spinor):
    outputs = []
    for column, real_coef, imag_coef in spin_map:
        picked = half_spinor[:, :, column]
        real_in = picked[:, :, 0]
        imag_in = picked[:, :, 1]
        outputs.append(
            jnp.stack(
                [
                    real_coef * real_in - imag_coef * imag_in,
                    real_coef * imag_in + imag_coef * real_in,
                ],
                axis=2,
            )
        )
    return jnp.stack(outputs, axis=2)


def project(spinor, spin_map, sign_value):
    return spinor[:, :, 0:2] + sign_value * apply_half(spin_map, spinor[:, :, 2:4])


def colour_apply(matrix, spinor):
    real_out = 0.0
    imag_out = 0.0
    for colour in range(3):
        left_real = matrix[:, :, 0, :, colour][:, :, None, :, None, :]
        left_imag = matrix[:, :, 1, :, colour][:, :, None, :, None, :]
        right_real = spinor[:, :, :, 0, colour][:, :, :, None]
        right_imag = spinor[:, :, :, 1, colour][:, :, :, None]
        real_out = real_out + left_real * right_real - left_imag * right_imag
        imag_out = imag_out + left_real * right_imag + left_imag * right_real
    return jnp.stack([real_out, imag_out], axis=3)


def adjoint(matrix):
    return jnp.stack(
        [jnp.swapaxes(matrix[:, :, 0], 2, 3), -jnp.swapaxes(matrix[:, :, 1], 2, 3)], axis=2
    )


def clover_apply(clover, spinor):
    block_list = []
    for chiral in range(2):
        clover_block = clover[:, :, chiral]
        new_shape = clover_block.shape[:2] + (2, 3, 6, clover_block.shape[-1])
        rows_real = clover_block[:, :, 0].reshape(new_shape)
        rows_imag = clover_block[:, :, 1].reshape(new_shape)
        real_out = 0.0
        imag_out = 0.0
        for source_index in range(6):
            spin_in = 2 * chiral + source_index // 3
            colour_in = source_index % 3
            left_real = rows_real[:, :, :, :, source_index][:, :, :, :, None, :]
            left_imag = rows_imag[:, :, :, :, source_index][:, :, :, :, None, :]
            right_real = spinor[:, :, spin_in, 0, colour_in][:, :, None, None]
            right_imag = spinor[:, :, spin_in, 1, colour_in][:, :, None, None]
            real_out = real_out + left_real * right_real - left_imag * right_imag
            imag_out = imag_out + left_real * right_imag + left_imag * right_real
        block_list.append(jnp.stack([real_out, imag_out], axis=3))
    return jnp.concatenate(block_list, axis=2)


def roll_plane(array_in, offset, hop_direction):
    sites = array_in.shape[-1]
    period = X if hop_direction == 0 else Y
    stride = 1 if hop_direction == 0 else X
    position = jnp.arange(sites) // stride % period
    if offset < 0:
        at_edge = position == period - 1
        wrapped = jnp.roll(array_in, (period - 1) * stride, axis=-1)
        plain = jnp.roll(array_in, -stride, axis=-1)
    else:
        at_edge = position == 0
        wrapped = jnp.roll(array_in, -(period - 1) * stride, axis=-1)
        plain = jnp.roll(array_in, stride, axis=-1)
    return jnp.where(at_edge, wrapped, plain)


def dirac_region(padded, centre_links, back_z, back_t, clover):
    centre = padded[1:-1, 1:-1]
    hopping = 0.0
    for hop_direction in range(4):
        forward_map = HALF_MAP[hop_direction]
        backward_map = dagger_map(forward_map)
        here_links = centre_links[:, :, hop_direction]
        if hop_direction < 2:
            ahead = roll_plane(project(centre, forward_map, -1.0), -1, hop_direction)
            behind = roll_plane(
                colour_apply(adjoint(here_links), project(centre, forward_map, 1.0)),
                1,
                hop_direction,
            )
        else:
            if hop_direction == 2:
                ahead_full = padded[1:-1, 2:]
                behind_full = padded[1:-1, :-2]
                behind_links = back_z
            else:
                ahead_full = padded[2:, 1:-1]
                behind_full = padded[:-2, 1:-1]
                behind_links = back_t
            ahead = project(ahead_full, forward_map, -1.0)
            behind = colour_apply(adjoint(behind_links), project(behind_full, forward_map, 1.0))
        forward_part = colour_apply(here_links, ahead)
        hopping = hopping + jnp.concatenate(
            [forward_part + behind, apply_half(backward_map, behind - forward_part)], axis=2
        )
    return centre + clover_apply(clover, centre) - HOPPING * hopping


def reverse_time(padded, depth_rows, position, tm_count):
    slices = padded.shape[0]
    slice_ids = jnp.arange(slices)
    negate = jnp.logical_or(
        jnp.logical_and(slice_ids < depth_rows, position == 0),
        jnp.logical_and(slice_ids >= slices - depth_rows, position == tm_count - 1),
    )
    factor = jnp.where(negate, -1.0, 1.0).astype(jnp.float32)
    return padded * factor.reshape((slices,) + (1,) * (padded.ndim - 1))


def mix_coefficients(elemental, coefficients):
    slices = coefficients.shape[0]
    eigen_count = coefficients.shape[1]
    complex_pairs = coefficients.reshape(slices, eigen_count, -1, 2)
    elemental_f32 = elemental.astype(jnp.float32)

    def product(left_factor, right_factor):
        return jnp.einsum(
            "ogs,osq->ogq", left_factor, right_factor, precision=lax.Precision.HIGHEST
        )

    mixed_real = product(elemental_f32[:, 0], complex_pairs[..., 0]) - product(
        elemental_f32[:, 1], complex_pairs[..., 1]
    )
    mixed_imag = product(elemental_f32[:, 0], complex_pairs[..., 1]) + product(
        elemental_f32[:, 1], complex_pairs[..., 0]
    )
    return (
        jnp.stack([mixed_real, mixed_imag], axis=-1)
        .reshape(slices, eigen_count, -1)
        .astype(jnp.bfloat16)
    )


def on_device(source, gauge_links, clover, eigenvectors, elemental):
    slices = source.shape[0]
    layers = source.shape[1]
    column_list = source.shape[5]
    eigen_count = eigenvectors.shape[4]
    tm_position = lax.axis_index("tm")
    tm_count = lax.axis_size("tm")
    links_f32 = gauge_links.astype(jnp.float32)
    clover_f32 = clover.astype(jnp.float32)
    edge_z = passed_along(gauge_links[:, -1:, 2], "space", 1)
    edge_t = passed_along(gauge_links[-1:, :, 3], "tm", 1)
    back_z = jnp.concatenate([edge_z, gauge_links[:, :-1, 2]], axis=1).astype(jnp.float32)
    back_t = jnp.concatenate([edge_t, gauge_links[:-1, :, 3]], axis=0).astype(jnp.float32)

    def apply_once(spinor_in):
        padded = extended(spinor_in, (("space", 1), ("tm", 0)), 1)
        padded = reverse_time(padded, 1, tm_position, tm_count)
        return dirac_region(padded, links_f32, back_z, back_t, clover_f32)

    def apply_twice(spinor_in):
        return apply_once(apply_once(spinor_in))

    forward = apply_twice(source.astype(jnp.float32))
    rounded = forward.astype(jnp.bfloat16)
    normaliser = (3.0 * X * Y * layers * lax.axis_size("space")) ** (-0.5)
    products = 0.0
    for colour in range(3):
        products = products + lax.dot_general(
            eigenvectors[:, :, :, colour],
            rounded[:, :, :, :, colour],
            (((1, 4), (1, 5)), ((0,), (0,))),
            preferred_element_type=jnp.float32,
        )
    real_part = products[:, 0, :, :, 0] + products[:, 1, :, :, 1]
    imag_part = products[:, 0, :, :, 1] - products[:, 1, :, :, 0]
    partial_sums = (
        jnp.stack([real_part, imag_part], axis=-1).reshape(slices, eigen_count, 8 * column_list)
        * normaliser
    )
    share_sums = lax.psum_scatter(partial_sums, "space", scatter_dimension=2, tiled=True)
    mixed_coef = lax.all_gather(
        mix_coefficients(elemental, share_sums), "space", axis=2, tiled=True
    )
    complex_pairs = mixed_coef.reshape(slices, eigen_count, 4, column_list, 2)
    mixed_real = complex_pairs[..., 0]
    mixed_imag = complex_pairs[..., 1]
    first_row = jnp.stack([mixed_real, mixed_imag], axis=3)
    second_row = jnp.stack([-mixed_imag, mixed_real], axis=3)
    left_operand = jnp.stack([first_row, second_row], axis=1)
    colour_parts = [
        lax.dot_general(
            left_operand,
            eigenvectors[:, :, :, colour],
            (((1, 2), (2, 3)), ((0,), (0,))),
            preferred_element_type=jnp.float32,
        )
        for colour in range(3)
    ]
    expanded = jnp.moveaxis(jnp.stack(colour_parts, axis=3), 5, 1) * eigen_count ** (-0.5)
    return apply_twice(expanded).astype(jnp.bfloat16)


def solution(mesh):
    placed = (
        P("tm", "space", None, None, None, None, None),
        P("tm", "space", None, None, None, None, None),
        P("tm", "space", None, None, None, None, None),
        P("tm", "space", None, None, None, None),
        P("tm", None, None, None),
    )
    return jax.shard_map(
        on_device,
        mesh=mesh,
        in_specs=placed,
        out_specs=P("tm", "space", None, None, None, None, None),
        check_vma=False,
    )
```

profile of v0, /device:TPU:1, one launch (start us, length us, event | category | flops | bytes accessed | tf_op | source)
XLA Modules:
  0.0 960.1 jit_solution(2014216765966501170)
XLA Ops:
  7.8 4.0 collective-permute-start
  11.8 7.8 collective-permute-start.1
  20.4 6.6 collective-permute-start.5
  28.4 1.9 collective-permute-start.4
  34.0 1.9 collective-permute-start.2
  35.9 2.4 collective-permute-start.3
  39.3 11.1 %collective-permute-done.2 = f32[1,4,4,2,3,16,128]{6,5,1,3,0,4,2:T(8,128)S(1)} collective-permute-done((f32[1,4,4,2,3,16,128]{6,5,1,3,0,4,2:T(8,128)S(1)}, f32[1,4,4,2,3,16,128]{6,5,1,3,0,4,2:T(8,128)S(1)}, u32[]{:S(2)}, u32[]{:S(2)}) %collective-permute-start.2) | collective-permute-done | bytes 786464 | tf_op jit(solution)/shard_map/ppermute | solution.py:31
  50.3 10.2 %collective-permute-done.3 = f32[1,4,4,2,3,16,128]{6,5,1,3,0,4,2:T(8,128)S(1)} collective-permute-done((f32[1,4,4,2,3,16,128]{6,5,1,3,0,4,2:T(8,128)S(1)}, f32[1,4,4,2,3,16,128]{6,5,1,3,0,4,2:T(8,128)S(1)}, u32[]{:S(2)}, u32[]{:S(2)}) %collective-permute-start.3) | collective-permute-done | bytes 786464 | tf_op jit(solution)/shard_map/ppermute | solution.py:33
  68.5 1.9 collective-permute-start.6
  70.5 7.6 collective-permute-start.7
  78.0 6.9 collective-permute-done.6
  88.1 1.9 collective-permute-start.8
  90.0 2.6 collective-permute-start.9
  96.0 11.3 %collective-permute-done.8 = f32[1,4,4,2,3,16,128]{6,5,1,3,0,4,2:T(8,128)} collective-permute-done((f32[1,4,4,2,3,16,128]{6,5,1,3,0,4,2:T(8,128)}, f32[1,4,4,2,3,16,128]{6,5,1,3,0,4,2:T(8,128)}, u32[]{:S(2)}, u32[]{:S(2)}) %collective-permute-start.8) | collective-permute-done | bytes 786464 | tf_op jit(solution)/shard_map/ppermute | solution.py:31
  107.4 5.4 collective-permute-done.9
  125.0 532.2 %all-reduce.3.cloned.1.call-done = f32[2,256,128]{1,0,2:T(2,128)} async-done(((f32[2,256,128]{1,0,2:T(2,128)}), f32[2,256,128]{1,0,2:T(2,128)}) %all-reduce.3.cloned.1.call-update) | async-done | bytes 262160
  659.2 126.4 %all-gather = bf16[2,256,1,128]{1,0,2,3:T(2,128)(2,1)S(1)} all-gather(bf16[2,256,1,2]{1,0,2,3:T(2,128)(2,1)S(1)} %pad_maximum_fusion.50), channel_id=2, replica_groups=mesh['space'=64,'tm'=8] {'space'}, dimensions={3}, use_global_device_ids=true | all-gather | bytes 133120 | tf_op jit(solution)/shard_map/all_gather | solution.py:234
  786.8 1.9 collective-permute-start.10
  788.7 7.6 collective-permute-start.11
  796.3 3.2 collective-permute-done.10
  801.4 63.4 %collective-permute-start.12 = (f32[1,4,4,2,3,16,128]{6,5,1,3,0,4,2:T(8,128)S(1)}, f32[1,4,4,2,3,16,128]{6,5,1,3,0,4,2:T(8,128)S(1)}, u32[]{:S(2)}, u32[]{:S(2)}) collective-permute-start(f32[1,4,4,2,3,16,128]{6,5,1,3,0,4,2:T(8,128)S(1)} %get-tuple-element.180), channel_id=1, source_target_pairs={{0,1},{1,2},{2,3},{3,4},{4,5},{5,6},{6,7},{7,0},{8,9},{9,10},{10,1... | collective-permute-start | bytes 2359304 | tf_op jit(solution)/shard_map/ppermute | solution.py:31
  864.8 2.1 collective-permute-start.13
  866.9 15.2 %collective-permute-done.12 = f32[1,4,4,2,3,16,128]{6,5,1,3,0,4,2:T(8,128)S(1)} collective-permute-done((f32[1,4,4,2,3,16,128]{6,5,1,3,0,4,2:T(8,128)S(1)}, f32[1,4,4,2,3,16,128]{6,5,1,3,0,4,2:T(8,128)S(1)}, u32[]{:S(2)}, u32[]{:S(2)}) %collective-permute-start.12) | collective-permute-done | bytes 786464 | tf_op jit(solution)/shard_map/ppermute | solution.py:31
  882.2 5.4 collective-permute-done.13
  896.7 1.9 collective-permute-start.14
  898.6 7.6 collective-permute-start.15
  906.2 4.8 collective-permute-done.14
  911.1 3.5 collective-permute-done.15
  914.9 1.9 collective-permute-start.16
  916.9 2.7 collective-permute-start.17
  919.5 14.7 %collective-permute-done.16 = f32[1,4,4,2,3,16,128]{6,5,1,3,2,0,4:T(8,128)S(1)} collective-permute-done((f32[1,4,4,2,3,16,128]{6,5,1,3,2,0,4:T(8,128)S(1)}, f32[1,4,4,2,3,16,128]{6,5,1,3,2,0,4:T(8,128)S(1)}, u32[]{:S(2)}, u32[]{:S(2)}) %collective-permute-start.16) | collective-permute-done | bytes 786464 | tf_op jit(solution)/shard_map/ppermute | solution.py:31
  934.2 10.3 %collective-permute-done.17 = f32[1,4,4,2,3,16,128]{6,5,1,3,2,0,4:T(8,128)S(1)} collective-permute-done((f32[1,4,4,2,3,16,128]{6,5,1,3,2,0,4:T(8,128)S(1)}, f32[1,4,4,2,3,16,128]{6,5,1,3,2,0,4:T(8,128)S(1)}, u32[]{:S(2)}, u32[]{:S(2)}) %collective-permute-start.17) | collective-permute-done | bytes 786464 | tf_op jit(solution)/shard_map/ppermute | solution.py:33
  (636 shorter events, 52.9 us)
Async XLA Ops:
  6.5 650.7 %all-reduce.3.cloned.1.call-start = ((), (), s32[]{:S(2)}) async-start(), calls=%async_computation | async-start | bytes 524288
  7.8 26.0 %collective-permute-start = (f32[2,1,4,2,3,16,128]{6,5,1,3,0,4,2:T(8,128)S(1)}, f32[2,1,4,2,3,16,128]{6,5,1,3,0,4,2:T(8,128)S(1)}, u32[]{:S(2)}, u32[]{:S(2)}) collective-permute-start(f32[2,1,4,2,3,16,128]{6,5,1,3,0,4,2:T(8,128)S(1)} %get-tuple-element.247), channel_id=1, source_target_pairs={{0,8},{8,16},{16,24},{24,32},{32,40},{40,48},{48,56},{56,64},{64,7... | collective-permute-start | bytes 1179656 | tf_op jit(solution)/shard_map/ppermute | solution.py:31
  11.8 21.9 %collective-permute-start.1 = (f32[2,1,4,2,3,16,128]{6,5,1,3,0,4,2:T(8,128)S(1)}, f32[2,1,4,2,3,16,128]{6,5,1,3,0,4,2:T(8,128)S(1)}, u32[]{:S(2)}, u32[]{:S(2)}) collective-permute-start(f32[2,1,4,2,3,16,128]{6,5,1,3,0,4,2:T(8,128)S(1)} %get-tuple-element.248), channel_id=1, source_target_pairs={{8,0},{16,8},{24,16},{32,24},{40,32},{48,40},{56,48},{64,56},{72,6... | collective-permute-start | bytes 1179656 | tf_op jit(solution)/shard_map/ppermute | solution.py:33
  20.4 13.3 %collective-permute-start.5 = (bf16[1,2,2,3,3,128]{5,1,4,3,2,0:T(2,128)(2,1)S(1)}, bf16[1,2,2,3,3,128]{5,1,4,3,2,0:T(2,128)(2,1)S(1)}, u32[]{:S(2)}, u32[]{:S(2)}) collective-permute-start(bf16[1,2,2,3,3,128]{5,1,4,3,2,0:T(2,128)(2,1)S(1)} %bitcast.1310), channel_id=1, source_target_pairs={{0,1},{1,2},{2,3},{3,4},{4,5},{5,6},{6,7},{7,0},{8,9},{9,10},{10,1... | collective-permute-start | bytes 27656 | tf_op jit(solution)/shard_map/ppermute | solution.py:21
  28.4 9.9 %collective-permute-start.4 = (bf16[2,1,2,3,3,128]{5,1,4,3,2,0:T(2,128)(2,1)}, bf16[2,1,2,3,3,128]{5,1,4,3,2,0:T(2,128)(2,1)}, u32[]{:S(2)}, u32[]{:S(2)}) collective-permute-start(bf16[2,1,2,3,3,128]{5,1,4,3,2,0:T(2,128)(2,1)} %copy.764), channel_id=1, source_target_pairs={{0,8},{8,16},{16,24},{24,32},{32,40},{40,48},{48,56},{56,64},{64,7... | collective-permute-start | bytes 27656 | tf_op jit(solution)/shard_map/ppermute | solution.py:21
  32.6 33.2 %copy-start.31 = (f32[2,2,3,128]{3,1,2,0:T(2,128)}, f32[2,2,3,128]{3,1,2,0:T(2,128)S(1)}, u32[]{:S(2)}) copy-start(f32[2,2,3,128]{3,1,2,0:T(2,128)S(1)} %get-tuple-element.761) | copy-start | bytes 18436
  32.6 33.2 %copy-start.34 = (f32[2,2,3,128]{3,1,2,0:T(2,128)}, f32[2,2,3,128]{3,1,2,0:T(2,128)S(1)}, u32[]{:S(2)}) copy-start(f32[2,2,3,128]{3,1,2,0:T(2,128)S(1)} %get-tuple-element.762) | copy-start | bytes 18436
  32.6 33.2 %copy-start.37 = (f32[2,2,3,128]{3,1,2,0:T(2,128)}, f32[2,2,3,128]{3,1,2,0:T(2,128)S(1)}, u32[]{:S(2)}) copy-start(f32[2,2,3,128]{3,1,2,0:T(2,128)S(1)} %get-tuple-element.763) | copy-start | bytes 18436
  32.6 33.2 %copy-start.40 = (f32[2,2,3,128]{3,1,2,0:T(2,128)}, f32[2,2,3,128]{3,1,2,0:T(2,128)S(1)}, u32[]{:S(2)}) copy-start(f32[2,2,3,128]{3,1,2,0:T(2,128)S(1)} %get-tuple-element.764) | copy-start | bytes 18436
  32.6 33.2 %copy-start.43 = (f32[2,2,3,128]{3,1,2,0:T(2,128)}, f32[2,2,3,128]{3,1,2,0:T(2,128)S(1)}, u32[]{:S(2)}) copy-start(f32[2,2,3,128]{3,1,2,0:T(2,128)S(1)} %get-tuple-element.765) | copy-start | bytes 18436
  32.6 33.2 %copy-start.46 = (f32[2,2,3,128]{3,1,2,0:T(2,128)}, f32[2,2,3,128]{3,1,2,0:T(2,128)S(1)}, u32[]{:S(2)}) copy-start(f32[2,2,3,128]{3,1,2,0:T(2,128)S(1)} %get-tuple-element.766) | copy-start | bytes 18436
  33.5 30.6 %copy-start.13 = (f32[2,2,3,128]{3,1,2,0:T(2,128)}, f32[2,2,3,128]{3,1,2,0:T(2,128)S(1)}, u32[]{:S(2)}) copy-start(f32[2,2,3,128]{3,1,2,0:T(2,128)S(1)} %get-tuple-element.717) | copy-start | bytes 18436
  33.6 31.3 %copy-start.1 = (f32[2,2,3,128]{3,1,2,0:T(2,128)}, f32[2,2,3,128]{3,1,2,0:T(2,128)S(1)}, u32[]{:S(2)}) copy-start(f32[2,2,3,128]{3,1,2,0:T(2,128)S(1)} %get-tuple-element.795) | copy-start | bytes 18436
  33.6 31.3 %copy-start.4 = (f32[2,2,3,128]{3,1,2,0:T(2,128)}, f32[2,2,3,128]{3,1,2,0:T(2,128)S(1)}, u32[]{:S(2)}) copy-start(f32[2,2,3,128]{3,1,2,0:T(2,128)S(1)} %get-tuple-element.796) | copy-start | bytes 18436
  33.6 31.3 %copy-start.7 = (f32[2,2,3,128]{3,1,2,0:T(2,128)}, f32[2,2,3,128]{3,1,2,0:T(2,128)S(1)}, u32[]{:S(2)}) copy-start(f32[2,2,3,128]{3,1,2,0:T(2,128)S(1)} %get-tuple-element.797) | copy-start | bytes 18436
  33.6 31.3 %copy-start.10 = (f32[2,2,3,128]{3,1,2,0:T(2,128)}, f32[2,2,3,128]{3,1,2,0:T(2,128)S(1)}, u32[]{:S(2)}) copy-start(f32[2,2,3,128]{3,1,2,0:T(2,128)S(1)} %get-tuple-element.798) | copy-start | bytes 18436
  34.0 16.4 %collective-permute-start.2 = (f32[1,4,4,2,3,16,128]{6,5,1,3,0,4,2:T(8,128)S(1)}, f32[1,4,4,2,3,16,128]{6,5,1,3,0,4,2:T(8,128)S(1)}, u32[]{:S(2)}, u32[]{:S(2)}) collective-permute-start(f32[1,4,4,2,3,16,128]{6,5,1,3,0,4,2:T(8,128)S(1)} %get-tuple-element.187), channel_id=1, source_target_pairs={{0,1},{1,2},{2,3},{3,4},{4,5},{5,6},{6,7},{7,0},{8,9},{9,10},{10,1... | collective-permute-start | bytes 2359304 | tf_op jit(solution)/shard_map/ppermute | solution.py:31
  35.9 24.6 %collective-permute-start.3 = (f32[1,4,4,2,3,16,128]{6,5,1,3,0,4,2:T(8,128)S(1)}, f32[1,4,4,2,3,16,128]{6,5,1,3,0,4,2:T(8,128)S(1)}, u32[]{:S(2)}, u32[]{:S(2)}) collective-permute-start(f32[1,4,4,2,3,16,128]{6,5,1,3,0,4,2:T(8,128)S(1)} %get-tuple-element.188), channel_id=1, source_target_pairs={{1,0},{2,1},{3,2},{4,3},{5,4},{6,5},{7,6},{0,7},{9,8},{10,9},{11,1... | collective-permute-start | bytes 2359304 | tf_op jit(solution)/shard_map/ppermute | solution.py:33
  68.5 16.4 %collective-permute-start.6 = (f32[2,1,4,2,3,16,128]{6,5,1,3,0,4,2:T(8,128)S(1)}, f32[2,1,4,2,3,16,128]{6,5,1,3,0,4,2:T(8,128)S(1)}, u32[]{:S(2)}, u32[]{:S(2)}) collective-permute-start(f32[2,1,4,2,3,16,128]{6,5,1,3,0,4,2:T(8,128)S(1)} %get-tuple-element.235), channel_id=1, source_target_pairs={{0,8},{8,16},{16,24},{24,32},{32,40},{40,48},{48,56},{56,64},{64,7... | collective-permute-start | bytes 1179656 | tf_op jit(solution)/shard_map/ppermute | solution.py:31
  70.5 16.3 %collective-permute-start.7 = (f32[2,1,4,2,3,16,128]{6,5,1,3,0,4,2:T(8,128)S(1)}, f32[2,1,4,2,3,16,128]{6,5,1,3,0,4,2:T(8,128)S(1)}, u32[]{:S(2)}, u32[]{:S(2)}) collective-permute-start(f32[2,1,4,2,3,16,128]{6,5,1,3,0,4,2:T(8,128)S(1)} %get-tuple-element.236), channel_id=1, source_target_pairs={{8,0},{16,8},{24,16},{32,24},{40,32},{48,40},{56,48},{64,56},{72,6... | collective-permute-start | bytes 1179656 | tf_op jit(solution)/shard_map/ppermute | solution.py:33
  88.1 19.2 %collective-permute-start.8 = (f32[1,4,4,2,3,16,128]{6,5,1,3,0,4,2:T(8,128)}, f32[1,4,4,2,3,16,128]{6,5,1,3,0,4,2:T(8,128)}, u32[]{:S(2)}, u32[]{:S(2)}) collective-permute-start(f32[1,4,4,2,3,16,128]{6,5,1,3,0,4,2:T(8,128)} %get-tuple-element.185), channel_id=1, source_target_pairs={{0,1},{1,2},{2,3},{3,4},{4,5},{5,6},{6,7},{7,0},{8,9},{9,10},{10,1... | collective-permute-start | bytes 2359304 | tf_op jit(solution)/shard_map/ppermute | solution.py:31
  90.0 22.7 %collective-permute-start.9 = (f32[1,4,4,2,3,16,128]{6,5,1,3,0,4,2:T(8,128)}, f32[1,4,4,2,3,16,128]{6,5,1,3,0,4,2:T(8,128)}, u32[]{:S(2)}, u32[]{:S(2)}) collective-permute-start(f32[1,4,4,2,3,16,128]{6,5,1,3,0,4,2:T(8,128)} %get-tuple-element.186), channel_id=1, source_target_pairs={{1,0},{2,1},{3,2},{4,3},{5,4},{6,5},{7,6},{0,7},{9,8},{10,9},{11,1... | collective-permute-start | bytes 2359304 | tf_op jit(solution)/shard_map/ppermute | solution.py:33
  123.6 534.4 %copy-start = (bf16[2,2,256,256]{3,2,1,0:T(8,128)(2,1)S(1)}, bf16[2,2,256,256]{3,2,1,0:T(8,128)(2,1)}, u32[]{:S(2)}) copy-start(bf16[2,2,256,256]{3,2,1,0:T(8,128)(2,1)} %param.9) | copy-start | bytes 1572868
  786.8 12.7 %collective-permute-start.10 = (f32[2,1,4,2,3,16,128]{6,5,1,3,0,4,2:T(8,128)S(1)}, f32[2,1,4,2,3,16,128]{6,5,1,3,0,4,2:T(8,128)S(1)}, u32[]{:S(2)}, u32[]{:S(2)}) collective-permute-start(f32[2,1,4,2,3,16,128]{6,5,1,3,0,4,2:T(8,128)S(1)} %get-tuple-element.223), channel_id=1, source_target_pairs={{0,8},{8,16},{16,24},{24,32},{32,40},{40,48},{48,56},{56,64},{64,7... | collective-permute-start | bytes 1179656 | tf_op jit(solution)/shard_map/ppermute | solution.py:31
  788.7 98.9 %copy-start.111 = (f32[4]{0:T(128)S(1)}, f32[4]{0:T(128)}, u32[]{:S(2)}) copy-start(f32[4]{0:T(128)} %copy-done.110) | copy-start | bytes 52
  788.7 12.3 %collective-permute-start.11 = (f32[2,1,4,2,3,16,128]{6,5,1,3,0,4,2:T(8,128)S(1)}, f32[2,1,4,2,3,16,128]{6,5,1,3,0,4,2:T(8,128)S(1)}, u32[]{:S(2)}, u32[]{:S(2)}) collective-permute-start(f32[2,1,4,2,3,16,128]{6,5,1,3,0,4,2:T(8,128)S(1)} %get-tuple-element.224), channel_id=1, source_target_pairs={{8,0},{16,8},{24,16},{32,24},{40,32},{48,40},{56,48},{64,56},{72,6... | collective-permute-start | bytes 1179656 | tf_op jit(solution)/shard_map/ppermute | solution.py:33
  801.4 80.8 %collective-permute-start.12 = (f32[1,4,4,2,3,16,128]{6,5,1,3,0,4,2:T(8,128)S(1)}, f32[1,4,4,2,3,16,128]{6,5,1,3,0,4,2:T(8,128)S(1)}, u32[]{:S(2)}, u32[]{:S(2)}) collective-permute-start(f32[1,4,4,2,3,16,128]{6,5,1,3,0,4,2:T(8,128)S(1)} %get-tuple-element.180), channel_id=1, source_target_pairs={{0,1},{1,2},{2,3},{3,4},{4,5},{5,6},{6,7},{7,0},{8,9},{9,10},{10,1... | collective-permute-start | bytes 2359304 | tf_op jit(solution)/shard_map/ppermute | solution.py:31
  864.8 22.8 %collective-permute-start.13 = (f32[1,4,4,2,3,16,128]{6,5,1,3,0,4,2:T(8,128)S(1)}, f32[1,4,4,2,3,16,128]{6,5,1,3,0,4,2:T(8,128)S(1)}, u32[]{:S(2)}, u32[]{:S(2)}) collective-permute-start(f32[1,4,4,2,3,16,128]{6,5,1,3,0,4,2:T(8,128)S(1)} %get-tuple-element.181), channel_id=1, source_target_pairs={{1,0},{2,1},{3,2},{4,3},{5,4},{6,5},{7,6},{0,7},{9,8},{10,9},{11,1... | collective-permute-start | bytes 2359304 | tf_op jit(solution)/shard_map/ppermute | solution.py:33
  896.7 14.4 %collective-permute-start.14 = (f32[2,1,4,2,3,16,128]{6,5,1,3,2,0,4:T(8,128)S(1)}, f32[2,1,4,2,3,16,128]{6,5,1,3,2,0,4:T(8,128)S(1)}, u32[]{:S(2)}, u32[]{:S(2)}) collective-permute-start(f32[2,1,4,2,3,16,128]{6,5,1,3,2,0,4:T(8,128)S(1)} %get-tuple-element.211), channel_id=1, source_target_pairs={{0,8},{8,16},{16,24},{24,32},{32,40},{40,48},{48,56},{56,64},{64,7... | collective-permute-start | bytes 1179656 | tf_op jit(solution)/shard_map/ppermute | solution.py:31
  898.6 16.0 %collective-permute-start.15 = (f32[2,1,4,2,3,16,128]{6,5,1,3,2,0,4:T(8,128)S(1)}, f32[2,1,4,2,3,16,128]{6,5,1,3,2,0,4:T(8,128)S(1)}, u32[]{:S(2)}, u32[]{:S(2)}) collective-permute-start(f32[2,1,4,2,3,16,128]{6,5,1,3,2,0,4:T(8,128)S(1)} %get-tuple-element.212), channel_id=1, source_target_pairs={{8,0},{16,8},{24,16},{32,24},{40,32},{48,40},{56,48},{64,56},{72,6... | collective-permute-start | bytes 1179656 | tf_op jit(solution)/shard_map/ppermute | solution.py:33
  914.9 19.3 %collective-permute-start.16 = (f32[1,4,4,2,3,16,128]{6,5,1,3,2,0,4:T(8,128)S(1)}, f32[1,4,4,2,3,16,128]{6,5,1,3,2,0,4:T(8,128)S(1)}, u32[]{:S(2)}, u32[]{:S(2)}) collective-permute-start(f32[1,4,4,2,3,16,128]{6,5,1,3,2,0,4:T(8,128)S(1)} %get-tuple-element.178), channel_id=1, source_target_pairs={{0,1},{1,2},{2,3},{3,4},{4,5},{5,6},{6,7},{7,0},{8,9},{9,10},{10,1... | collective-permute-start | bytes 2359304 | tf_op jit(solution)/shard_map/ppermute | solution.py:31
  916.9 27.7 %collective-permute-start.17 = (f32[1,4,4,2,3,16,128]{6,5,1,3,2,0,4:T(8,128)S(1)}, f32[1,4,4,2,3,16,128]{6,5,1,3,2,0,4:T(8,128)S(1)}, u32[]{:S(2)}, u32[]{:S(2)}) collective-permute-start(f32[1,4,4,2,3,16,128]{6,5,1,3,2,0,4:T(8,128)S(1)} %get-tuple-element.179), channel_id=1, source_target_pairs={{1,0},{2,1},{3,2},{4,3},{5,4},{6,5},{7,6},{0,7},{9,8},{10,9},{11,1... | collective-permute-start | bytes 2359304 | tf_op jit(solution)/shard_map/ppermute | solution.py:33
  (99 other events, 753.8 us)
Sparse Core Ops, SparseCore 0:
  125.0 532.1 all-reduce.2
where the time goes:
time: 964 us; the launch traced here: 960 us
  waiting for transfers between devices  638 us (66%)
  starting transfers between devices  128 us (13%)
  blocking collectives  126 us (13%)
  other arithmetic  30.5 us (3%)
  between operations  18.4 us (2%)
  local copies, waits for them, and re-layouts  16.3 us (2%)
    unnamed x2, waiting for transfers between devices  532 us
    all_gather x1, blocking collectives, on_device(): lax.all_gather(mix_coefficients(elemental, share_sums), 'space', axis=2,...  126 us
    ppermute x8, starting transfers between devices, extended(): lax.ppermute(tail, axis, [(i, (i + 1) % count) for i in range(count)])  79 us
    ppermute x8, waiting for transfers between devices, extended(): lax.ppermute(tail, axis, [(i, (i + 1) % count) for i in range(count)])  67.3 us
    ppermute x8, starting transfers between devices, extended(): lax.ppermute(head, axis, [((i + 1) % count, i) for i in range(count)])  40.4 us
    ppermute x8, waiting for transfers between devices, extended(): lax.ppermute(head, axis, [((i + 1) % count, i) for i in range(count)])  38.1 us
  transfers between devices with their start and end apart: 19, of which 15 were waited for; matrix products, arithmetic and copies ran while one was open for 1% of the time, Pallas kernels for 0%

commit v1 on v0

v1 whole, which is shorter than its diff:
```python
import jax
import jax.numpy as jnp
from jax import lax
from jax.sharding import PartitionSpec as P

X = 16
Y = 8


HOPPING = 0.125
HALF_MAP = (
    ((1, 0.0, -1.0), (0, 0.0, -1.0)),
    ((1, -1.0, 0.0), (0, 1.0, 0.0)),
    ((0, 0.0, -1.0), (1, 0.0, 1.0)),
    ((0, 1.0, 0.0), (1, 1.0, 0.0)),
)


def passed_along(value, axis, by):
    count = lax.axis_size(axis)
    return lax.ppermute(value, axis, [(i, (i + by) % count) for i in range(count)])


def dagger_map(forward_map):
    result = [None, None]
    for row_number in range(2):
        column, real_coef, imag_coef = forward_map[row_number]
        result[column] = (row_number, real_coef, -imag_coef)
    return tuple(result)


def apply_half(spin_map, half_spinor):
    outputs = []
    for column, real_coef, imag_coef in spin_map:
        picked = half_spinor[:, :, column]
        real_in = picked[:, :, 0]
        imag_in = picked[:, :, 1]
        outputs.append(
            jnp.stack(
                [
                    real_coef * real_in - imag_coef * imag_in,
                    real_coef * imag_in + imag_coef * real_in,
                ],
                axis=2,
            )
        )
    return jnp.stack(outputs, axis=2)


def project(spinor, spin_map, sign_value):
    return spinor[:, :, 0:2] + sign_value * apply_half(spin_map, spinor[:, :, 2:4])


def colour_apply(matrix, spinor):
    real_out = 0.0
    imag_out = 0.0
    for colour in range(3):
        left_real = matrix[:, :, 0, :, colour][:, :, None, :, None, :]
        left_imag = matrix[:, :, 1, :, colour][:, :, None, :, None, :]
        right_real = spinor[:, :, :, 0, colour][:, :, :, None]
        right_imag = spinor[:, :, :, 1, colour][:, :, :, None]
        real_out = real_out + left_real * right_real - left_imag * right_imag
        imag_out = imag_out + left_real * right_imag + left_imag * right_real
    return jnp.stack([real_out, imag_out], axis=3)


def adjoint(matrix):
    return jnp.stack(
        [jnp.swapaxes(matrix[:, :, 0], 2, 3), -jnp.swapaxes(matrix[:, :, 1], 2, 3)], axis=2
    )


def clover_apply(clover, spinor):
    block_list = []
    for chiral in range(2):
        clover_block = clover[:, :, chiral]
        new_shape = clover_block.shape[:2] + (2, 3, 6, clover_block.shape[-1])
        rows_real = clover_block[:, :, 0].reshape(new_shape)
        rows_imag = clover_block[:, :, 1].reshape(new_shape)
        real_out = 0.0
        imag_out = 0.0
        for source_index in range(6):
            spin_in = 2 * chiral + source_index // 3
            colour_in = source_index % 3
            left_real = rows_real[:, :, :, :, source_index][:, :, :, :, None, :]
            left_imag = rows_imag[:, :, :, :, source_index][:, :, :, :, None, :]
            right_real = spinor[:, :, spin_in, 0, colour_in][:, :, None, None]
            right_imag = spinor[:, :, spin_in, 1, colour_in][:, :, None, None]
            real_out = real_out + left_real * right_real - left_imag * right_imag
            imag_out = imag_out + left_real * right_imag + left_imag * right_real
        block_list.append(jnp.stack([real_out, imag_out], axis=3))
    return jnp.concatenate(block_list, axis=2)


def roll_plane(array_in, offset, hop_direction):
    sites = array_in.shape[-1]
    period = X if hop_direction == 0 else Y
    stride = 1 if hop_direction == 0 else X
    position = jnp.arange(sites) // stride % period
    if offset < 0:
        at_edge = position == period - 1
        wrapped = jnp.roll(array_in, (period - 1) * stride, axis=-1)
        plain = jnp.roll(array_in, -stride, axis=-1)
    else:
        at_edge = position == 0
        wrapped = jnp.roll(array_in, -(period - 1) * stride, axis=-1)
        plain = jnp.roll(array_in, stride, axis=-1)
    return jnp.where(at_edge, wrapped, plain)


def dirac(centre, links, clover, first_sign, last_sign):
    halves = {}
    for hop_direction, (axis, dim, before_sign, after_sign) in (
        (2, ("space", 1, None, None)),
        (3, ("tm", 0, first_sign, last_sign)),
    ):
        size = centre.shape[dim]
        here_links = links[:, :, hop_direction]
        forward_map = HALF_MAP[hop_direction]
        ahead_own = project(centre, forward_map, -1.0)
        behind_own = colour_apply(adjoint(here_links), project(centre, forward_map, 1.0))
        low = lax.slice_in_dim(ahead_own, 0, 1, axis=dim)
        high = lax.slice_in_dim(behind_own, size - 1, size, axis=dim)
        after = passed_along(low.astype(jnp.bfloat16), axis, -1).astype(jnp.float32)
        before = passed_along(high.astype(jnp.bfloat16), axis, 1).astype(jnp.float32)
        if after_sign is not None:
            after = after * after_sign
            before = before * before_sign
        ahead = jnp.concatenate([lax.slice_in_dim(ahead_own, 1, size, axis=dim), after], axis=dim)
        behind = jnp.concatenate(
            [before, lax.slice_in_dim(behind_own, 0, size - 1, axis=dim)], axis=dim
        )
        halves[hop_direction] = (ahead, behind)
    hopping = 0.0
    for hop_direction in range(4):
        forward_map = HALF_MAP[hop_direction]
        backward_map = dagger_map(forward_map)
        here_links = links[:, :, hop_direction]
        if hop_direction < 2:
            ahead = roll_plane(project(centre, forward_map, -1.0), -1, hop_direction)
            behind = roll_plane(
                colour_apply(adjoint(here_links), project(centre, forward_map, 1.0)),
                1,
                hop_direction,
            )
        else:
            ahead, behind = halves[hop_direction]
        forward_part = colour_apply(here_links, ahead)
        hopping = hopping + jnp.concatenate(
            [forward_part + behind, apply_half(backward_map, behind - forward_part)], axis=2
        )
    return centre + clover_apply(clover, centre) - HOPPING * hopping


def mix_coefficients(elemental, shares):
    weights = elemental.astype(jnp.float32)

    def product(component, values):
        return jnp.einsum(
            "okj,oj->ok", weights[:, component], values, precision=lax.Precision.HIGHEST
        )

    real = product(0, shares[:, 0]) - product(1, shares[:, 1])
    imag = product(0, shares[:, 1]) + product(1, shares[:, 0])
    return jnp.stack([real, imag], axis=1).astype(jnp.bfloat16)


def on_device(source, gauge_links, clover, eigenvectors, elemental):
    slices = source.shape[0]
    layers = source.shape[1]
    columns = source.shape[5]
    eigen_count = eigenvectors.shape[4]
    space_count = lax.axis_size("space")
    tm_position = lax.axis_index("tm")
    tm_count = lax.axis_size("tm")
    first_sign = jnp.where(tm_position == 0, -1.0, 1.0)
    last_sign = jnp.where(tm_position == tm_count - 1, -1.0, 1.0)
    links_f32 = gauge_links.astype(jnp.float32)
    clover_f32 = clover.astype(jnp.float32)

    def apply_twice(spinor):
        for _ in range(2):
            spinor = dirac(spinor, links_f32, clover_f32, first_sign, last_sign)
        return spinor

    rounded = apply_twice(source.astype(jnp.float32)).astype(jnp.bfloat16)
    normaliser = (3.0 * X * Y * layers * space_count) ** (-0.5)
    products = 0.0
    for colour in range(3):
        products = products + lax.dot_general(
            rounded[:, :, :, :, colour],
            eigenvectors[:, :, :, colour],
            (((1, 5), (1, 4)), ((0,), (0,))),
            preferred_element_type=jnp.float32,
        )
    real_part = products[:, :, 0, :, 0] + products[:, :, 1, :, 1]
    imag_part = products[:, :, 1, :, 0] - products[:, :, 0, :, 1]
    partial_sums = jnp.stack([real_part, imag_part], axis=3) * normaliser
    partial_sums = jnp.moveaxis(partial_sums, 0, 2).reshape(
        4 * columns, slices, 2, eigen_count
    )
    gathered = lax.all_to_all(partial_sums, "space", 0, 0, tiled=True)
    per_device = 4 * columns // space_count
    shares = gathered.reshape(space_count, per_device, slices, 2, eigen_count).sum(0)
    mixed = jnp.stack([mix_coefficients(elemental, shares[i]) for i in range(per_device)])
    everywhere = jnp.broadcast_to(mixed[None], (space_count,) + mixed.shape)
    everywhere = everywhere.reshape((space_count * per_device,) + mixed.shape[1:])
    mixed_coef = lax.all_to_all(everywhere, "space", 0, 0, tiled=True)
    parts = jnp.moveaxis(
        mixed_coef.reshape(4, columns, slices, 2, eigen_count), 2, 0
    )
    mixed_real = parts[:, :, :, 0]
    mixed_imag = parts[:, :, :, 1]
    left_operand = jnp.stack(
        [
            jnp.stack([mixed_real, mixed_imag], axis=2),
            jnp.stack([-mixed_imag, mixed_real], axis=2),
        ],
        axis=4,
    )
    colour_parts = [
        lax.dot_general(
            left_operand,
            eigenvectors[:, :, :, colour],
            (((4, 5), (2, 3)), ((0,), (0,))),
            preferred_element_type=jnp.float32,
        )
        for colour in range(3)
    ]
    expanded = jnp.moveaxis(jnp.stack(colour_parts, axis=3), 5, 1) * eigen_count ** (-0.5)
    return apply_twice(expanded).astype(jnp.bfloat16)


def solution(mesh):
    placed = (
        P("tm", "space", None, None, None, None, None),
        P("tm", "space", None, None, None, None, None),
        P("tm", "space", None, None, None, None, None),
        P("tm", "space", None, None, None, None),
        P("tm", None, None, None),
    )
    return jax.shard_map(
        on_device,
        mesh=mesh,
        in_specs=placed,
        out_specs=P("tm", "space", None, None, None, None, None),
        check_vma=False,
    )
```

time: 964 us -> 176 us (0.18)
  waiting for transfers between devices: 638 us -> 19 us
  blocking collectives: 126 us -> 18.7 us
  starting transfers between devices: 128 us -> 78.4 us
  between operations: 18.4 us -> 4.25 us
    unnamed x2 -> x0, waiting for transfers between devices: 532 us -> none
    all_gather x1 -> x0, blocking collectives: 126 us -> none  [on_device(): lax.all_gather(mix_coefficients(elemental, share_sums), 'space', axis=2,...]
    ppermute x16 -> x0, starting transfers between devices: 119 us -> none  [the longest x8 79 us: extended(): lax.ppermute(tail, axis, [(i, (i + 1) % count) for i in range(count)])]
    ppermute x16 -> x0, waiting for transfers between devices: 105 us -> none  [the longest x8 67.3 us: extended(): lax.ppermute(tail, axis, [(i, (i + 1) % count) for i in range(count)])]
    ppermute x2 -> x16, starting transfers between devices: 8.56 us -> 73.8 us  [passed_along(): lax.ppermute(value, axis, [(i, (i + by) % count) for i in range(count)])]
    all_to_all x0 -> x1, blocking collectives: none -> 18.7 us  [on_device(): gathered = lax.all_to_all(partial_sums, 'space', 0, 0, tiled=True)]
    all_to_all x0 -> x1, waiting for transfers between devices: none -> 9.91 us  [on_device(): mixed_coef = lax.all_to_all(everywhere, 'space', 0, 0, tiled=True)]
  transfers between devices with their start and end apart: 19 -> 17, of which waited for: 15 -> 3; matrix products, arithmetic and copies ran while one was open for 1% -> 17% of each run, Pallas kernels for 0% -> 0%
where the time goes in v1:
time: 176 us; the launch traced here: 175 us
  starting transfers between devices  78.4 us (45%)
  other arithmetic  35.2 us (20%)
  waiting for transfers between devices  19 us (11%)
  blocking collectives  18.7 us (11%)
  local copies, waits for them, and re-layouts  16.4 us (9%)
  between operations  4.25 us (2%)
  matrix products  2.89 us (2%)
    ppermute x16, starting transfers between devices, passed_along(): lax.ppermute(value, axis, [(i, (i + by) % count) for i in range(count)])  73.8 us
    all_to_all x1, blocking collectives, on_device(): gathered = lax.all_to_all(partial_sums, 'space', 0, 0, tiled=True)  18.7 us
    all_to_all x1, waiting for transfers between devices, on_device(): mixed_coef = lax.all_to_all(everywhere, 'space', 0, 0, tiled=True)  9.91 us
    ppermute x16, waiting for transfers between devices, passed_along(): lax.ppermute(value, axis, [(i, (i + by) % count) for i in range(count)])  9.06 us
    unnamed x274, local copies, waits for them, and re-layouts  6.36 us
    sub x32, other arithmetic, colour_apply(): real_out = real_out + left_real * right_real - left_imag * right_imag  5.32 us
    all_to_all x1, starting transfers between devices, on_device(): mixed_coef = lax.all_to_all(everywhere, 'space', 0, 0, tiled=True)  4.62 us
    another operation x16, other arithmetic, colour_apply(): return jnp.stack([real_out, imag_out], axis=3)  4.31 us
  transfers between devices with their start and end apart: 17, of which 3 were waited for; matrix products, arithmetic and copies ran while one was open for 17% of the time, Pallas kernels for 0%

profile of v1, /device:TPU:1, one launch (start us, length us, event | category | flops | bytes accessed | tf_op | source)
XLA Modules:
  0.0 174.9 jit_solution(9603596270019357305)
XLA Ops:
  0.0 1.1 copy_convert_fusion
  2.3 9.9 %collective-permute-start = (bf16[2,1,2,2,3,16,128]{6,5,1,3,0,4,2:T(8,128)(2,1)}, bf16[2,1,2,2,3,16,128]{6,5,1,3,0,4,2:T(8,128)(2,1)}, u32[]{:S(2)}, u32[]{:S(2)}) collective-permute-start(bf16[2,1,2,2,3,16,128]{6,5,1,3,0,4,2:T(8,128)(2,1)} %slice.4887), channel_id=1, source_target_pairs={{0,504},{8,0},{16,8},{24,16},{32,24},{40,32},{48,40},{56,48},{64,5... | collective-permute-start | bytes 294920 | tf_op jit(solution)/shard_map/ppermute | solution.py:21
  13.3 1.9 %collective-permute-start.1 = (bf16[2,1,2,2,3,16,128]{6,5,1,3,0,4,2:T(8,128)(2,1)}, bf16[2,1,2,2,3,16,128]{6,5,1,3,0,4,2:T(8,128)(2,1)}, u32[]{:S(2)}, u32[]{:S(2)}) collective-permute-start(bf16[2,1,2,2,3,16,128]{6,5,1,3,0,4,2:T(8,128)(2,1)} %fusion.137), channel_id=1, source_target_pairs={{0,8},{8,16},{16,24},{24,32},{32,40},{40,48},{48,56},{56,64},{64,7... | collective-permute-start | bytes 294920 | tf_op jit(solution)/shard_map/ppermute | solution.py:21
  16.2 2.9 %collective-permute-start.2 = (bf16[1,2,2,2,3,16,128]{6,5,1,3,0,4,2:T(8,128)(2,1)}, bf16[1,2,2,2,3,16,128]{6,5,1,3,0,4,2:T(8,128)(2,1)}, u32[]{:S(2)}, u32[]{:S(2)}) collective-permute-start(bf16[1,2,2,2,3,16,128]{6,5,1,3,0,4,2:T(8,128)(2,1)} %slice.4886), channel_id=1, source_target_pairs={{0,7},{1,0},{2,1},{3,2},{4,3},{5,4},{6,5},{7,6},{8,15},{9,8},{10,9... | collective-permute-start | bytes 294920 | tf_op jit(solution)/shard_map/ppermute | solution.py:21
  20.0 5.7 %collective-permute-start.3 = (bf16[1,2,2,2,3,16,128]{6,5,1,3,0,4,2:T(8,128)(2,1)}, bf16[1,2,2,2,3,16,128]{6,5,1,3,0,4,2:T(8,128)(2,1)}, u32[]{:S(2)}, u32[]{:S(2)}) collective-permute-start(bf16[1,2,2,2,3,16,128]{6,5,1,3,0,4,2:T(8,128)(2,1)} %fusion.135), channel_id=1, source_target_pairs={{0,1},{1,2},{2,3},{3,4},{4,5},{5,6},{6,7},{7,0},{8,9},{9,10},{10,1... | collective-permute-start | bytes 294920 | tf_op jit(solution)/shard_map/ppermute | solution.py:21
  29.4 0.9 multiply_add_fusion.54
  31.4 0.9 multiply_add_fusion.53
  32.3 0.9 multiply_subtract_fusion.38
  35.3 0.9 fusion.37
  37.0 0.9 fusion.36
  41.4 1.1 copy-done.1
  42.8 0.9 convert_multiply_fusion.7
  44.0 0.9 convert_multiply_fusion.6
  45.1 0.9 convert_element_type.88
  46.4 0.9 convert_element_type.89
  52.5 7.9 %collective-permute-start.4 = (bf16[2,1,2,2,3,16,128]{6,5,1,3,0,4,2:T(8,128)(2,1)S(1)}, bf16[2,1,2,2,3,16,128]{6,5,1,3,0,4,2:T(8,128)(2,1)S(1)}, u32[]{:S(2)}, u32[]{:S(2)}) collective-permute-start(bf16[2,1,2,2,3,16,128]{6,5,1,3,0,4,2:T(8,128)(2,1)S(1)} %slice.4885), channel_id=1, source_target_pairs={{0,504},{8,0},{16,8},{24,16},{32,24},{40,32},{48,40},{56,48},{64,5... | collective-permute-start | bytes 294920 | tf_op jit(solution)/shard_map/ppermute | solution.py:21
  60.6 2.1 %collective-permute-start.5 = (bf16[2,1,2,2,3,16,128]{6,5,1,3,0,4,2:T(8,128)(2,1)S(1)}, bf16[2,1,2,2,3,16,128]{6,5,1,3,0,4,2:T(8,128)(2,1)S(1)}, u32[]{:S(2)}, u32[]{:S(2)}) collective-permute-start(bf16[2,1,2,2,3,16,128]{6,5,1,3,0,4,2:T(8,128)(2,1)S(1)} %fusion.133), channel_id=1, source_target_pairs={{0,8},{8,16},{16,24},{24,32},{32,40},{40,48},{48,56},{56,64},{64,7... | collective-permute-start | bytes 294920 | tf_op jit(solution)/shard_map/ppermute | solution.py:21
  63.8 5.4 %collective-permute-start.6 = (bf16[1,2,2,2,3,16,128]{6,5,1,3,0,4,2:T(8,128)(2,1)S(1)}, bf16[1,2,2,2,3,16,128]{6,5,1,3,0,4,2:T(8,128)(2,1)S(1)}, u32[]{:S(2)}, u32[]{:S(2)}) collective-permute-start(bf16[1,2,2,2,3,16,128]{6,5,1,3,0,4,2:T(8,128)(2,1)S(1)} %slice.4884), channel_id=1, source_target_pairs={{0,7},{1,0},{2,1},{3,2},{4,3},{5,4},{6,5},{7,6},{8,15},{9,8},{10,9... | collective-permute-start | bytes 294920 | tf_op jit(solution)/shard_map/ppermute | solution.py:21
  69.4 1.9 %collective-permute-start.7 = (bf16[1,2,2,2,3,16,128]{6,5,1,3,0,4,2:T(8,128)(2,1)S(1)}, bf16[1,2,2,2,3,16,128]{6,5,1,3,0,4,2:T(8,128)(2,1)S(1)}, u32[]{:S(2)}, u32[]{:S(2)}) collective-permute-start(bf16[1,2,2,2,3,16,128]{6,5,1,3,0,4,2:T(8,128)(2,1)S(1)} %fusion.131), channel_id=1, source_target_pairs={{0,1},{1,2},{2,3},{3,4},{4,5},{5,6},{6,7},{7,0},{8,9},{9,10},{10,1... | collective-permute-start | bytes 294920 | tf_op jit(solution)/shard_map/ppermute | solution.py:21
  73.4 2.3 %collective-permute-done.7 = bf16[1,2,2,2,3,16,128]{6,5,1,3,0,4,2:T(8,128)(2,1)S(1)} collective-permute-done((bf16[1,2,2,2,3,16,128]{6,5,1,3,0,4,2:T(8,128)(2,1)S(1)}, bf16[1,2,2,2,3,16,128]{6,5,1,3,0,4,2:T(8,128)(2,1)S(1)}, u32[]{:S(2)}, u32[]{:S(2)}) %collective-permute-start.7) | collective-permute-done | bytes 98336 | tf_op jit(solution)/shard_map/ppermute | solution.py:21
  77.9 18.7 %all_to_all.10 = f32[64,2,2,256]{3,1,2,0:T(2,128)S(1)} all-to-all(f32[64,2,2,256]{3,1,2,0:T(2,128)S(1)} %copy.582), channel_id=1, replica_groups=mesh['space'=64,'tm'=8] {'space'}, dimensions={0} | all-to-all | bytes 524288 | tf_op jit(solution)/shard_map/all_to_all | solution.py:202
  98.7 4.6 %all-to-all-start.1 = ((bf16[64,2,2,256]{3,1,2,0:T(2,128)(2,1)}), bf16[64,2,2,256]{3,1,2,0:T(2,128)(2,1)S(1)}, u32[]{:S(2)}, u32[]{:S(2)}) async-start(bf16[64,2,2,256]{3,1,2,0:T(2,128)(2,1)} %reshape.3588), calls=%async_computation.1 | async-start | bytes 262144 | tf_op jit(solution)/shard_map/all_to_all | solution.py:208
  103.4 9.9 %all-to-all-done.1 = bf16[64,2,2,256]{3,1,2,0:T(2,128)(2,1)S(1)} async-done(((bf16[64,2,2,256]{3,1,2,0:T(2,128)(2,1)}), bf16[64,2,2,256]{3,1,2,0:T(2,128)(2,1)S(1)}, u32[]{:S(2)}, u32[]{:S(2)}) %all-to-all-start.1) | async-done | bytes 131104 | tf_op jit(solution)/shard_map/all_to_all | solution.py:208
  117.5 3.4 %collective-permute-start.8 = (bf16[2,1,2,2,3,16,128]{6,5,1,3,0,4,2:T(8,128)(2,1)S(1)}, bf16[2,1,2,2,3,16,128]{6,5,1,3,0,4,2:T(8,128)(2,1)S(1)}, u32[]{:S(2)}, u32[]{:S(2)}) collective-permute-start(bf16[2,1,2,2,3,16,128]{6,5,1,3,0,4,2:T(8,128)(2,1)S(1)} %slice.4883), channel_id=1, source_target_pairs={{0,504},{8,0},{16,8},{24,16},{32,24},{40,32},{48,40},{56,48},{64,5... | collective-permute-start | bytes 294920 | tf_op jit(solution)/shard_map/ppermute | solution.py:21
  121.1 1.9 %collective-permute-start.9 = (bf16[2,1,2,2,3,16,128]{6,5,1,3,0,4,2:T(8,128)(2,1)S(1)}, bf16[2,1,2,2,3,16,128]{6,5,1,3,0,4,2:T(8,128)(2,1)S(1)}, u32[]{:S(2)}, u32[]{:S(2)}) collective-permute-start(bf16[2,1,2,2,3,16,128]{6,5,1,3,0,4,2:T(8,128)(2,1)S(1)} %fusion.129), channel_id=1, source_target_pairs={{0,8},{8,16},{16,24},{24,32},{32,40},{40,48},{48,56},{56,64},{64,7... | collective-permute-start | bytes 294920 | tf_op jit(solution)/shard_map/ppermute | solution.py:21
  124.3 11.4 %collective-permute-start.10 = (bf16[1,2,2,2,3,16,128]{6,5,1,3,0,4,2:T(8,128)(2,1)S(1)}, bf16[1,2,2,2,3,16,128]{6,5,1,3,0,4,2:T(8,128)(2,1)S(1)}, u32[]{:S(2)}, u32[]{:S(2)}) collective-permute-start(bf16[1,2,2,2,3,16,128]{6,5,1,3,0,4,2:T(8,128)(2,1)S(1)} %slice.4882), channel_id=1, source_target_pairs={{0,7},{1,0},{2,1},{3,2},{4,3},{5,4},{6,5},{7,6},{8,15},{9,8},{10,9... | collective-permute-start | bytes 294920 | tf_op jit(solution)/shard_map/ppermute | solution.py:21
  136.1 2.3 %collective-permute-start.11 = (bf16[1,2,2,2,3,16,128]{6,5,1,3,0,4,2:T(8,128)(2,1)S(1)}, bf16[1,2,2,2,3,16,128]{6,5,1,3,0,4,2:T(8,128)(2,1)S(1)}, u32[]{:S(2)}, u32[]{:S(2)}) collective-permute-start(bf16[1,2,2,2,3,16,128]{6,5,1,3,0,4,2:T(8,128)(2,1)S(1)} %fusion.127), channel_id=1, source_target_pairs={{0,1},{1,2},{2,3},{3,4},{4,5},{5,6},{6,7},{7,0},{8,9},{9,10},{10,1... | collective-permute-start | bytes 294920 | tf_op jit(solution)/shard_map/ppermute | solution.py:21
  145.5 7.6 %collective-permute-start.12 = (bf16[2,1,2,2,3,16,128]{6,5,1,3,0,4,2:T(8,128)(2,1)S(1)}, bf16[2,1,2,2,3,16,128]{6,5,1,3,0,4,2:T(8,128)(2,1)S(1)}, u32[]{:S(2)}, u32[]{:S(2)}) collective-permute-start(bf16[2,1,2,2,3,16,128]{6,5,1,3,0,4,2:T(8,128)(2,1)S(1)} %slice.4881), channel_id=1, source_target_pairs={{0,504},{8,0},{16,8},{24,16},{32,24},{40,32},{48,40},{56,48},{64,5... | collective-permute-start | bytes 294920 | tf_op jit(solution)/shard_map/ppermute | solution.py:21
  153.1 5.7 %collective-permute-start.14 = (bf16[1,2,2,2,3,16,128]{6,5,1,3,0,4,2:T(8,128)(2,1)S(1)}, bf16[1,2,2,2,3,16,128]{6,5,1,3,0,4,2:T(8,128)(2,1)S(1)}, u32[]{:S(2)}, u32[]{:S(2)}) collective-permute-start(bf16[1,2,2,2,3,16,128]{6,5,1,3,0,4,2:T(8,128)(2,1)S(1)} %slice.4880), channel_id=1, source_target_pairs={{0,7},{1,0},{2,1},{3,2},{4,3},{5,4},{6,5},{7,6},{8,15},{9,8},{10,9... | collective-permute-start | bytes 294920 | tf_op jit(solution)/shard_map/ppermute | solution.py:21
  159.0 1.9 %collective-permute-start.15 = (bf16[1,2,2,2,3,16,128]{6,5,1,3,0,4,2:T(8,128)(2,1)S(1)}, bf16[1,2,2,2,3,16,128]{6,5,1,3,0,4,2:T(8,128)(2,1)S(1)}, u32[]{:S(2)}, u32[]{:S(2)}) collective-permute-start(bf16[1,2,2,2,3,16,128]{6,5,1,3,0,4,2:T(8,128)(2,1)S(1)} %fusion.123), channel_id=1, source_target_pairs={{0,1},{1,2},{2,3},{3,4},{4,5},{5,6},{6,7},{7,0},{8,9},{9,10},{10,1... | collective-permute-start | bytes 294920 | tf_op jit(solution)/shard_map/ppermute | solution.py:21
  162.8 1.9 %collective-permute-start.13 = (bf16[2,1,2,2,3,16,128]{6,5,1,3,0,4,2:T(8,128)(2,1)S(1)}, bf16[2,1,2,2,3,16,128]{6,5,1,3,0,4,2:T(8,128)(2,1)S(1)}, u32[]{:S(2)}, u32[]{:S(2)}) collective-permute-start(bf16[2,1,2,2,3,16,128]{6,5,1,3,0,4,2:T(8,128)(2,1)S(1)} %fusion.125), channel_id=1, source_target_pairs={{0,8},{8,16},{16,24},{24,32},{32,40},{40,48},{48,56},{56,64},{64,7... | collective-permute-start | bytes 294920 | tf_op jit(solution)/shard_map/ppermute | solution.py:21
  166.0 6.7 %collective-permute-done.13 = bf16[2,1,2,2,3,16,128]{6,5,1,3,0,4,2:T(8,128)(2,1)S(1)} collective-permute-done((bf16[2,1,2,2,3,16,128]{6,5,1,3,0,4,2:T(8,128)(2,1)S(1)}, bf16[2,1,2,2,3,16,128]{6,5,1,3,0,4,2:T(8,128)(2,1)S(1)}, u32[]{:S(2)}, u32[]{:S(2)}) %collective-permute-start.13) | collective-permute-done | bytes 98336 | tf_op jit(solution)/shard_map/ppermute | solution.py:21
  (637 shorter events, 44.1 us)
Async XLA Ops:
  1.4 10.8 %copy-start.131 = (bf16[2,2,4,2,3,3,128]{6,3,5,4,2,1,0:T(2,128)(2,1)S(1)}, bf16[2,2,4,2,3,3,128]{6,3,5,4,2,1,0:T(2,128)(2,1)}, u32[]{:S(2)}) copy-start(bf16[2,2,4,2,3,3,128]{6,3,5,4,2,1,0:T(2,128)(2,1)} %param.6) | copy-start | bytes 221188
  2.3 42.9 %collective-permute-start = (bf16[2,1,2,2,3,16,128]{6,5,1,3,0,4,2:T(8,128)(2,1)}, bf16[2,1,2,2,3,16,128]{6,5,1,3,0,4,2:T(8,128)(2,1)}, u32[]{:S(2)}, u32[]{:S(2)}) collective-permute-start(bf16[2,1,2,2,3,16,128]{6,5,1,3,0,4,2:T(8,128)(2,1)} %slice.4887), channel_id=1, source_target_pairs={{0,504},{8,0},{16,8},{24,16},{32,24},{40,32},{48,40},{56,48},{64,5... | collective-permute-start | bytes 294920 | tf_op jit(solution)/shard_map/ppermute | solution.py:21
  13.3 33.1 %collective-permute-start.1 = (bf16[2,1,2,2,3,16,128]{6,5,1,3,0,4,2:T(8,128)(2,1)}, bf16[2,1,2,2,3,16,128]{6,5,1,3,0,4,2:T(8,128)(2,1)}, u32[]{:S(2)}, u32[]{:S(2)}) collective-permute-start(bf16[2,1,2,2,3,16,128]{6,5,1,3,0,4,2:T(8,128)(2,1)} %fusion.137), channel_id=1, source_target_pairs={{0,8},{8,16},{16,24},{24,32},{32,40},{40,48},{48,56},{56,64},{64,7... | collective-permute-start | bytes 294920 | tf_op jit(solution)/shard_map/ppermute | solution.py:21
  16.2 26.6 %collective-permute-start.2 = (bf16[1,2,2,2,3,16,128]{6,5,1,3,0,4,2:T(8,128)(2,1)}, bf16[1,2,2,2,3,16,128]{6,5,1,3,0,4,2:T(8,128)(2,1)}, u32[]{:S(2)}, u32[]{:S(2)}) collective-permute-start(bf16[1,2,2,2,3,16,128]{6,5,1,3,0,4,2:T(8,128)(2,1)} %slice.4886), channel_id=1, source_target_pairs={{0,7},{1,0},{2,1},{3,2},{4,3},{5,4},{6,5},{7,6},{8,15},{9,8},{10,9... | collective-permute-start | bytes 294920 | tf_op jit(solution)/shard_map/ppermute | solution.py:21
  20.0 24.0 %collective-permute-start.3 = (bf16[1,2,2,2,3,16,128]{6,5,1,3,0,4,2:T(8,128)(2,1)}, bf16[1,2,2,2,3,16,128]{6,5,1,3,0,4,2:T(8,128)(2,1)}, u32[]{:S(2)}, u32[]{:S(2)}) collective-permute-start(bf16[1,2,2,2,3,16,128]{6,5,1,3,0,4,2:T(8,128)(2,1)} %fusion.135), channel_id=1, source_target_pairs={{0,1},{1,2},{2,3},{3,4},{4,5},{5,6},{6,7},{7,0},{8,9},{9,10},{10,1... | collective-permute-start | bytes 294920 | tf_op jit(solution)/shard_map/ppermute | solution.py:21
  37.9 33.8 %copy-start.98 = (f32[2,2,3,128]{3,1,2,0:T(2,128)}, f32[2,2,3,128]{3,1,2,0:T(2,128)S(1)}, u32[]{:S(2)}) copy-start(f32[2,2,3,128]{3,1,2,0:T(2,128)S(1)} %get-tuple-element.678) | copy-start | bytes 18436
  37.9 33.8 %copy-start.100 = (f32[2,2,3,128]{3,1,2,0:T(2,128)}, f32[2,2,3,128]{3,1,2,0:T(2,128)S(1)}, u32[]{:S(2)}) copy-start(f32[2,2,3,128]{3,1,2,0:T(2,128)S(1)} %get-tuple-element.679) | copy-start | bytes 18436
  37.9 33.8 %copy-start.102 = (f32[2,2,3,128]{3,1,2,0:T(2,128)}, f32[2,2,3,128]{3,1,2,0:T(2,128)S(1)}, u32[]{:S(2)}) copy-start(f32[2,2,3,128]{3,1,2,0:T(2,128)S(1)} %get-tuple-element.680) | copy-start | bytes 18436
  38.0 33.8 %copy-start.104 = (f32[2,2,3,128]{3,1,2,0:T(2,128)}, f32[2,2,3,128]{3,1,2,0:T(2,128)S(1)}, u32[]{:S(2)}) copy-start(f32[2,2,3,128]{3,1,2,0:T(2,128)S(1)} %get-tuple-element.681) | copy-start | bytes 18436
  38.0 33.8 %copy-start.106 = (f32[2,2,3,128]{3,1,2,0:T(2,128)}, f32[2,2,3,128]{3,1,2,0:T(2,128)S(1)}, u32[]{:S(2)}) copy-start(f32[2,2,3,128]{3,1,2,0:T(2,128)S(1)} %get-tuple-element.682) | copy-start | bytes 18436
  38.0 33.8 %copy-start.108 = (f32[2,2,3,128]{3,1,2,0:T(2,128)}, f32[2,2,3,128]{3,1,2,0:T(2,128)S(1)}, u32[]{:S(2)}) copy-start(f32[2,2,3,128]{3,1,2,0:T(2,128)S(1)} %get-tuple-element.683) | copy-start | bytes 18436
  52.4 10.3 %copy-start.135 = (pred[128]{0:T(512)(128)(4,1)S(1)}, pred[128]{0:T(512)(128)(4,1)}, u32[]{:S(2)}) copy-start(pred[128]{0:T(512)(128)(4,1)} %broadcast_compare_fusion.1) | copy-start | bytes 388
  52.5 20.2 %collective-permute-start.4 = (bf16[2,1,2,2,3,16,128]{6,5,1,3,0,4,2:T(8,128)(2,1)S(1)}, bf16[2,1,2,2,3,16,128]{6,5,1,3,0,4,2:T(8,128)(2,1)S(1)}, u32[]{:S(2)}, u32[]{:S(2)}) collective-permute-start(bf16[2,1,2,2,3,16,128]{6,5,1,3,0,4,2:T(8,128)(2,1)S(1)} %slice.4885), channel_id=1, source_target_pairs={{0,504},{8,0},{16,8},{24,16},{32,24},{40,32},{48,40},{56,48},{64,5... | collective-permute-start | bytes 294920 | tf_op jit(solution)/shard_map/ppermute | solution.py:21
  60.6 12.3 %collective-permute-start.5 = (bf16[2,1,2,2,3,16,128]{6,5,1,3,0,4,2:T(8,128)(2,1)S(1)}, bf16[2,1,2,2,3,16,128]{6,5,1,3,0,4,2:T(8,128)(2,1)S(1)}, u32[]{:S(2)}, u32[]{:S(2)}) collective-permute-start(bf16[2,1,2,2,3,16,128]{6,5,1,3,0,4,2:T(8,128)(2,1)S(1)} %fusion.133), channel_id=1, source_target_pairs={{0,8},{8,16},{16,24},{24,32},{32,40},{40,48},{48,56},{56,64},{64,7... | collective-permute-start | bytes 294920 | tf_op jit(solution)/shard_map/ppermute | solution.py:21
  63.8 9.4 %collective-permute-start.6 = (bf16[1,2,2,2,3,16,128]{6,5,1,3,0,4,2:T(8,128)(2,1)S(1)}, bf16[1,2,2,2,3,16,128]{6,5,1,3,0,4,2:T(8,128)(2,1)S(1)}, u32[]{:S(2)}, u32[]{:S(2)}) collective-permute-start(bf16[1,2,2,2,3,16,128]{6,5,1,3,0,4,2:T(8,128)(2,1)S(1)} %slice.4884), channel_id=1, source_target_pairs={{0,7},{1,0},{2,1},{3,2},{4,3},{5,4},{6,5},{7,6},{8,15},{9,8},{10,9... | collective-permute-start | bytes 294920 | tf_op jit(solution)/shard_map/ppermute | solution.py:21
  69.4 6.3 %collective-permute-start.7 = (bf16[1,2,2,2,3,16,128]{6,5,1,3,0,4,2:T(8,128)(2,1)S(1)}, bf16[1,2,2,2,3,16,128]{6,5,1,3,0,4,2:T(8,128)(2,1)S(1)}, u32[]{:S(2)}, u32[]{:S(2)}) collective-permute-start(bf16[1,2,2,2,3,16,128]{6,5,1,3,0,4,2:T(8,128)(2,1)S(1)} %fusion.131), channel_id=1, source_target_pairs={{0,1},{1,2},{2,3},{3,4},{4,5},{5,6},{6,7},{7,0},{8,9},{9,10},{10,1... | collective-permute-start | bytes 294920 | tf_op jit(solution)/shard_map/ppermute | solution.py:21
  77.5 19.2 %copy-start = (bf16[2,2,256,256]{3,2,1,0:T(8,128)(2,1)S(1)}, bf16[2,2,256,256]{3,2,1,0:T(8,128)(2,1)}, u32[]{:S(2)}) copy-start(bf16[2,2,256,256]{3,2,1,0:T(8,128)(2,1)} %param.9) | copy-start | bytes 1572868
  98.7 14.6 %all-to-all-start.1 = ((bf16[64,2,2,256]{3,1,2,0:T(2,128)(2,1)}), bf16[64,2,2,256]{3,1,2,0:T(2,128)(2,1)S(1)}, u32[]{:S(2)}, u32[]{:S(2)}) async-start(bf16[64,2,2,256]{3,1,2,0:T(2,128)(2,1)} %reshape.3588), calls=%async_computation.1 | async-start | bytes 262144 | tf_op jit(solution)/shard_map/all_to_all | solution.py:208
  117.5 22.5 %collective-permute-start.8 = (bf16[2,1,2,2,3,16,128]{6,5,1,3,0,4,2:T(8,128)(2,1)S(1)}, bf16[2,1,2,2,3,16,128]{6,5,1,3,0,4,2:T(8,128)(2,1)S(1)}, u32[]{:S(2)}, u32[]{:S(2)}) collective-permute-start(bf16[2,1,2,2,3,16,128]{6,5,1,3,0,4,2:T(8,128)(2,1)S(1)} %slice.4883), channel_id=1, source_target_pairs={{0,504},{8,0},{16,8},{24,16},{32,24},{40,32},{48,40},{56,48},{64,5... | collective-permute-start | bytes 294920 | tf_op jit(solution)/shard_map/ppermute | solution.py:21
  121.1 19.5 %collective-permute-start.9 = (bf16[2,1,2,2,3,16,128]{6,5,1,3,0,4,2:T(8,128)(2,1)S(1)}, bf16[2,1,2,2,3,16,128]{6,5,1,3,0,4,2:T(8,128)(2,1)S(1)}, u32[]{:S(2)}, u32[]{:S(2)}) collective-permute-start(bf16[2,1,2,2,3,16,128]{6,5,1,3,0,4,2:T(8,128)(2,1)S(1)} %fusion.129), channel_id=1, source_target_pairs={{0,8},{8,16},{16,24},{24,32},{32,40},{40,48},{48,56},{56,64},{64,7... | collective-permute-start | bytes 294920 | tf_op jit(solution)/shard_map/ppermute | solution.py:21
  124.0 11.7 %copy-start.82 = (f32[2,2,3,128]{3,1,2,0:T(2,128)S(1)}, f32[2,2,3,128]{3,1,2,0:T(2,128)}, u32[]{:S(2)}) copy-start(f32[2,2,3,128]{3,1,2,0:T(2,128)} %copy-done.80) | copy-start | bytes 18436
  124.0 11.7 %copy-start.85 = (f32[2,2,3,128]{3,1,2,0:T(2,128)S(1)}, f32[2,2,3,128]{3,1,2,0:T(2,128)}, u32[]{:S(2)}) copy-start(f32[2,2,3,128]{3,1,2,0:T(2,128)} %copy-done.83) | copy-start | bytes 18436
  124.1 11.7 %copy-start.88 = (f32[2,2,3,128]{3,1,2,0:T(2,128)S(1)}, f32[2,2,3,128]{3,1,2,0:T(2,128)}, u32[]{:S(2)}) copy-start(f32[2,2,3,128]{3,1,2,0:T(2,128)} %copy-done.86) | copy-start | bytes 18436
  124.1 11.7 %copy-start.91 = (f32[2,2,3,128]{3,1,2,0:T(2,128)S(1)}, f32[2,2,3,128]{3,1,2,0:T(2,128)}, u32[]{:S(2)}) copy-start(f32[2,2,3,128]{3,1,2,0:T(2,128)} %copy-done.89) | copy-start | bytes 18436
  124.1 11.7 %copy-start.94 = (f32[2,2,3,128]{3,1,2,0:T(2,128)S(1)}, f32[2,2,3,128]{3,1,2,0:T(2,128)}, u32[]{:S(2)}) copy-start(f32[2,2,3,128]{3,1,2,0:T(2,128)} %copy-done.92) | copy-start | bytes 18436
  124.1 11.7 %copy-start.97 = (f32[2,2,3,128]{3,1,2,0:T(2,128)S(1)}, f32[2,2,3,128]{3,1,2,0:T(2,128)}, u32[]{:S(2)}) copy-start(f32[2,2,3,128]{3,1,2,0:T(2,128)} %copy-done.95) | copy-start | bytes 18436
  124.3 16.6 %collective-permute-start.10 = (bf16[1,2,2,2,3,16,128]{6,5,1,3,0,4,2:T(8,128)(2,1)S(1)}, bf16[1,2,2,2,3,16,128]{6,5,1,3,0,4,2:T(8,128)(2,1)S(1)}, u32[]{:S(2)}, u32[]{:S(2)}) collective-permute-start(bf16[1,2,2,2,3,16,128]{6,5,1,3,0,4,2:T(8,128)(2,1)S(1)} %slice.4882), channel_id=1, source_target_pairs={{0,7},{1,0},{2,1},{3,2},{4,3},{5,4},{6,5},{7,6},{8,15},{9,8},{10,9... | collective-permute-start | bytes 294920 | tf_op jit(solution)/shard_map/ppermute | solution.py:21
  136.1 5.7 %collective-permute-start.11 = (bf16[1,2,2,2,3,16,128]{6,5,1,3,0,4,2:T(8,128)(2,1)S(1)}, bf16[1,2,2,2,3,16,128]{6,5,1,3,0,4,2:T(8,128)(2,1)S(1)}, u32[]{:S(2)}, u32[]{:S(2)}) collective-permute-start(bf16[1,2,2,2,3,16,128]{6,5,1,3,0,4,2:T(8,128)(2,1)S(1)} %fusion.127), channel_id=1, source_target_pairs={{0,1},{1,2},{2,3},{3,4},{4,5},{5,6},{6,7},{7,0},{8,9},{9,10},{10,1... | collective-permute-start | bytes 294920 | tf_op jit(solution)/shard_map/ppermute | solution.py:21
  145.5 20.3 %collective-permute-start.12 = (bf16[2,1,2,2,3,16,128]{6,5,1,3,0,4,2:T(8,128)(2,1)S(1)}, bf16[2,1,2,2,3,16,128]{6,5,1,3,0,4,2:T(8,128)(2,1)S(1)}, u32[]{:S(2)}, u32[]{:S(2)}) collective-permute-start(bf16[2,1,2,2,3,16,128]{6,5,1,3,0,4,2:T(8,128)(2,1)S(1)} %slice.4881), channel_id=1, source_target_pairs={{0,504},{8,0},{16,8},{24,16},{32,24},{40,32},{48,40},{56,48},{64,5... | collective-permute-start | bytes 294920 | tf_op jit(solution)/shard_map/ppermute | solution.py:21
  153.1 19.8 %collective-permute-start.14 = (bf16[1,2,2,2,3,16,128]{6,5,1,3,0,4,2:T(8,128)(2,1)S(1)}, bf16[1,2,2,2,3,16,128]{6,5,1,3,0,4,2:T(8,128)(2,1)S(1)}, u32[]{:S(2)}, u32[]{:S(2)}) collective-permute-start(bf16[1,2,2,2,3,16,128]{6,5,1,3,0,4,2:T(8,128)(2,1)S(1)} %slice.4880), channel_id=1, source_target_pairs={{0,7},{1,0},{2,1},{3,2},{4,3},{5,4},{6,5},{7,6},{8,15},{9,8},{10,9... | collective-permute-start | bytes 294920 | tf_op jit(solution)/shard_map/ppermute | solution.py:21
  159.0 14.2 %collective-permute-start.15 = (bf16[1,2,2,2,3,16,128]{6,5,1,3,0,4,2:T(8,128)(2,1)S(1)}, bf16[1,2,2,2,3,16,128]{6,5,1,3,0,4,2:T(8,128)(2,1)S(1)}, u32[]{:S(2)}, u32[]{:S(2)}) collective-permute-start(bf16[1,2,2,2,3,16,128]{6,5,1,3,0,4,2:T(8,128)(2,1)S(1)} %fusion.123), channel_id=1, source_target_pairs={{0,1},{1,2},{2,3},{3,4},{4,5},{5,6},{6,7},{7,0},{8,9},{9,10},{10,1... | collective-permute-start | bytes 294920 | tf_op jit(solution)/shard_map/ppermute | solution.py:21
  162.8 10.0 %collective-permute-start.13 = (bf16[2,1,2,2,3,16,128]{6,5,1,3,0,4,2:T(8,128)(2,1)S(1)}, bf16[2,1,2,2,3,16,128]{6,5,1,3,0,4,2:T(8,128)(2,1)S(1)}, u32[]{:S(2)}, u32[]{:S(2)}) collective-permute-start(bf16[2,1,2,2,3,16,128]{6,5,1,3,0,4,2:T(8,128)(2,1)S(1)} %fusion.125), channel_id=1, source_target_pairs={{0,8},{8,16},{16,24},{24,32},{32,40},{40,48},{48,56},{56,64},{64,7... | collective-permute-start | bytes 294920 | tf_op jit(solution)/shard_map/ppermute | solution.py:21
  (122 other events, 309.6 us)

commit v2 on v1

v2 whole, which is shorter than its diff:
```python
import functools

import jax
import jax.numpy as jnp
from jax import lax
from jax.experimental import pallas as pl
from jax.experimental.pallas import tpu as pltpu
from jax.sharding import PartitionSpec as P

X = 16
Y = 8

HOPPING = 0.125
HALF_MAP = (
    ((1, 0.0, -1.0), (0, 0.0, -1.0)),
    ((1, -1.0, 0.0), (0, 1.0, 0.0)),
    ((0, 0.0, -1.0), (1, 0.0, 1.0)),
    ((0, 1.0, 0.0), (1, 1.0, 0.0)),
)
ROWS = 8
LIMIT = 16 << 20
F32 = jnp.float32
BF16 = jnp.bfloat16


def dagger_map(forward_map):
    result = [None, None]
    for row_number in range(2):
        column, real_coef, imag_coef = forward_map[row_number]
        result[column] = (row_number, real_coef, -imag_coef)
    return tuple(result)


def plus(left, right, sign):
    return left + right if sign > 0 else left - right


def project(spinor, direction, sign):
    half = []
    for row, (column, a, b) in enumerate(HALF_MAP[direction]):
        real, imag = [], []
        for colour in range(3):
            if a != 0.0:
                real.append(plus(spinor(row, 0, colour), spinor(2 + column, 0, colour), sign * a))
                imag.append(plus(spinor(row, 1, colour), spinor(2 + column, 1, colour), sign * a))
            else:
                real.append(plus(spinor(row, 0, colour), spinor(2 + column, 1, colour), -sign * b))
                imag.append(plus(spinor(row, 1, colour), spinor(2 + column, 0, colour), sign * b))
        half.append([real, imag])
    return half


def link_times(link, half, adjoint):
    result = [[[None] * 3, [None] * 3] for _ in range(2)]
    for a in range(3):
        for b in range(3):
            if adjoint:
                real, imag = link(0, b, a), link(1, b, a)
            else:
                real, imag = link(0, a, b), link(1, a, b)
            for spin in range(2):
                hr, hi = half[spin][0][b], half[spin][1][b]
                if adjoint:
                    new_real = real * hr + imag * hi
                    new_imag = real * hi - imag * hr
                else:
                    new_real = real * hr - imag * hi
                    new_imag = real * hi + imag * hr
                out = result[spin]
                out[0][a] = new_real if out[0][a] is None else out[0][a] + new_real
                out[1][a] = new_imag if out[1][a] is None else out[1][a] + new_imag
    return result


def lower_terms(half, direction):
    terms = []
    for row, (column, a, b) in enumerate(dagger_map(HALF_MAP[direction])):
        for colour in range(3):
            if a != 0.0:
                terms.append((2 + row, 0, colour, a, half[column][0][colour]))
                terms.append((2 + row, 1, colour, a, half[column][1][colour]))
            else:
                terms.append((2 + row, 0, colour, -b, half[column][1][colour]))
                terms.append((2 + row, 1, colour, b, half[column][0][colour]))
    return terms


def spread(total, half, direction, lower_sign):
    for spin in range(2):
        for ri in range(2):
            for colour in range(3):
                key = (spin, ri, colour)
                total[key] = total[key] + half[spin][ri][colour]
    for spin, ri, colour, sign, value in lower_terms(half, direction):
        key = (spin, ri, colour)
        total[key] = plus(total[key], value, sign * lower_sign)


def mapped(half, function):
    return [[[function(v) for v in part] for part in spin] for spin in half]


def reader(ref, t, z, rows):
    return lambda spin, ri, colour: ref[t, z, spin, ri, colour, rows, :].astype(F32)


def link_reader(links, t, z, mu):
    return lambda ri, a, b: links[t, z, pl.ds(((mu * 3 + a) * 3 + b) * 2 + ri, 1), :]


KEYS = [(s, r, c) for s in range(4) for r in range(2) for c in range(3)]


def local_part(psi, links, clover, out):
    layers = psi.shape[1]
    slices = psi.shape[0]
    halves = psi.shape[5] // ROWS
    lane = lax.broadcasted_iota(jnp.int32, (ROWS, X * Y), 1) % X
    at_last = lane == X - 1
    at_first = lane == 0

    def ahead(direction, value):
        if direction == 1:
            return pltpu.roll(value, X * Y - X, 1)
        return jnp.where(at_last, pltpu.roll(value, X - 1, 1), pltpu.roll(value, X * Y - 1, 1))

    def behind(direction, value):
        if direction == 1:
            return pltpu.roll(value, X, 1)
        return jnp.where(at_first, pltpu.roll(value, X * Y - X + 1, 1), pltpu.roll(value, 1, 1))

    def plane(i, carry):
        t = i // (layers * halves)
        z = (i // halves) % layers
        rows = pl.ds(pl.multiple_of((i % halves) * ROWS, ROWS), ROWS)
        read = reader(psi, t, z, rows)
        total = {}
        for chiral in range(2):
            for row in range(6):
                spin, colour = 2 * chiral + row // 3, row % 3
                real = read(spin, 0, colour)
                imag = read(spin, 1, colour)
                for column in range(6):
                    at = ((chiral * 6 + row) * 6 + column) * 2
                    cr = clover[t, z, pl.ds(at, 1), :]
                    ci = clover[t, z, pl.ds(at + 1, 1), :]
                    xr = read(2 * chiral + column // 3, 0, column % 3)
                    xi = read(2 * chiral + column // 3, 1, column % 3)
                    real = real + (cr * xr - ci * xi)
                    imag = imag + (cr * xi + ci * xr)
                total[(spin, 0, colour)] = real
                total[(spin, 1, colour)] = imag
        for direction in range(2):
            link = link_reader(links, t, z, direction)
            half = mapped(project(read, direction, -1), functools.partial(ahead, direction))
            spread(total, link_times(link, half, False), direction, -1)
            half = link_times(link, project(read, direction, 1), True)
            spread(total, mapped(half, functools.partial(behind, direction)), direction, 1)
        for key in KEYS:
            out[t, z, key[0], key[1], key[2], rows, :] = total[key]
        return carry

    lax.fori_loop(0, slices * layers * halves, plane, 0)

    def bonds(direction, count, low_cell, high_cell):
        def bond(i, carry):
            other = i // halves
            rows = pl.ds(pl.multiple_of((i % halves) * ROWS, ROWS), ROWS)
            low, high = low_cell(other), high_cell(other)
            link = link_reader(links, *low, direction)
            for source, target, adjoint in ((high, low, False), (low, high, True)):
                sign = 1 if adjoint else -1
                half = link_times(link, project(reader(psi, *source, rows), direction, sign), adjoint)
                read = reader(out, *target, rows)
                total = {key: read(*key) for key in KEYS}
                spread(total, half, direction, sign)
                for key in KEYS:
                    out[target[0], target[1], key[0], key[1], key[2], rows, :] = total[key]
            return carry

        lax.fori_loop(0, count * halves, bond, 0)

    for z in range(layers - 1):
        bonds(2, slices, lambda t, z=z: (t, z), lambda t, z=z: (t, z + 1))
    for t in range(slices - 1):
        bonds(3, layers, lambda z, t=t: (t, z), lambda z, t=t: (t + 1, z))


def half_value(ref, index):
    return [
        [[ref[index, s, r, c].astype(F32) for c in range(3)] for r in range(2)] for s in range(2)
    ]


def put_half(ref, index, half):
    for s in range(2):
        for r in range(2):
            for c in range(3):
                ref[index, s, r, c] = half[s][r][c].astype(BF16)


def by_parity(place, function, pair):
    odd = place % 2 == 1
    pl.when(odd)(lambda: function(pair[0], pair[1]))
    pl.when(jnp.logical_not(odd))(lambda: function(pair[1], pair[0]))


def faces_part(psi, links, where, z_inner, z_outer, t_inner, t_outer):
    by_parity(where[0], functools.partial(z_faces, psi, links), (z_inner, z_outer))
    by_parity(where[1], functools.partial(t_faces, psi, links), (t_inner, t_outer))


def z_faces(psi, links, z_low, z_high):
    slices, layers = psi.shape[0], psi.shape[1]
    rows = slice(None)

    def of_z(t, carry):
        put_half(z_low, t, project(reader(psi, t, 0, rows), 2, -1))
        half = project(reader(psi, t, layers - 1, rows), 2, 1)
        put_half(z_high, t, link_times(link_reader(links, t, layers - 1, 2), half, True))
        return carry

    lax.fori_loop(0, slices, of_z, 0)


def t_faces(psi, links, t_low, t_high):
    slices, layers = psi.shape[0], psi.shape[1]
    rows = slice(None)

    def of_t(z, carry):
        put_half(t_low, z, project(reader(psi, 0, z, rows), 3, -1))
        half = project(reader(psi, slices - 1, z, rows), 3, 1)
        put_half(t_high, z, link_times(link_reader(links, slices - 1, z, 3), half, True))
        return carry

    lax.fori_loop(0, layers, of_t, 0)


def put(source, out, target, half, direction, sign):
    t, z = target
    read = reader(source, t, z, slice(None))
    total = {key: read(*key) for key in KEYS}
    spread(total, half, direction, sign)
    for key in KEYS:
        out[t, z, key[0], key[1], key[2]] = total[key]


def halo_part(acc, links, where, z_inner, z_outer, t_inner, t_outer, out):
    by_parity(where[0], functools.partial(z_halo, acc, links, out), (z_inner, z_outer))
    by_parity(where[1], functools.partial(t_halo, links, where, out), (t_inner, t_outer))


def z_halo(acc, links, out, z_before, z_after):
    slices, layers = acc.shape[0], acc.shape[1]

    def of_z(t, carry):
        for z in range(1, layers - 1):
            for key in KEYS:
                out[t, z, key[0], key[1], key[2]] = acc[t, z, key[0], key[1], key[2]]
        put(acc, out, (t, 0), half_value(z_before, t), 2, 1)
        half = link_times(link_reader(links, t, layers - 1, 2), half_value(z_after, t), False)
        put(acc, out, (t, layers - 1), half, 2, -1)
        return carry

    lax.fori_loop(0, slices, of_z, 0)


def t_halo(links, where, out, t_before, t_after):
    slices, layers = out.shape[0], out.shape[1]
    first = jnp.where(where[1] == 0, -1.0, 1.0).astype(F32)
    last = jnp.where(where[1] == where[2] - 1, -1.0, 1.0).astype(F32)

    def of_t(z, carry):
        put(out, out, (0, z), mapped(half_value(t_before, z), lambda v: v * first), 3, 1)
        half = mapped(half_value(t_after, z), lambda v: v * last)
        half = link_times(link_reader(links, slices - 1, z, 3), half, False)
        put(out, out, (slices - 1, z), half, 3, -1)
        return carry

    lax.fori_loop(0, layers, of_t, 0)


def position():
    return lax.axis_index("space"), lax.axis_index("tm"), lax.axis_size("tm")


VMEM = pl.BlockSpec(memory_space=pltpu.VMEM)
SMEM = pl.BlockSpec(memory_space=pltpu.SMEM)


def call(kernel, in_count, out_shapes, scratch=(), smem=(), flops=1 << 22, name=None):
    specs = [SMEM if i in smem else VMEM for i in range(in_count)]
    return pl.pallas_call(
        kernel,
        out_shape=out_shapes,
        in_specs=specs,
        out_specs=jax.tree.map(lambda _: VMEM, out_shapes),
        scratch_shapes=list(scratch),
        cost_estimate=pl.CostEstimate(flops=flops, bytes_accessed=1 << 21, transcendentals=0),
        compiler_params=pltpu.CompilerParams(vmem_limit_bytes=LIMIT),
        name=name,
    )


def entry_kernel(source, gauge, psi, links, *sent):
    psi[...] = source[...].astype(F32)
    slices, layers = source.shape[0], source.shape[1]
    for t in range(slices):
        for z in range(layers):
            for mu in range(4):
                for a in range(3):
                    for b in range(3):
                        row = ((mu * 3 + a) * 3 + b) * 2
                        value = gauge[t, z, mu, a, b].astype(F32)
                        links[t, z, pl.ds(row, 2), :] = value * (-HOPPING)
    faces_part(psi, links, position(), *sent)


def clover_kernel(clover, rows):
    slices, layers = clover.shape[0], clover.shape[1]
    for t in range(slices):
        for z in range(layers):
            for chiral in range(2):
                for i in range(6):
                    for j in range(6):
                        row = ((chiral * 6 + i) * 6 + j) * 2
                        rows[t, z, pl.ds(row, 2), :] = clover[t, z, chiral, i, j].astype(F32)


def local_kernel(psi, links, clover, out):
    local_part(psi, links, clover, out)


def middle_kernel(acc, links, *refs):
    received, (psi, *sent) = refs[:4], refs[4:]
    halo_part(acc, links, position(), *received, psi)
    faces_part(psi, links, position(), *sent)


def last_kernel(acc, links, *refs):
    received, (result, psi) = refs[:4], refs[4:]
    halo_part(acc, links, position(), *received, psi)
    result[...] = psi[...].astype(BF16)


def coefficient_kernel(scale, acc, links, *refs):
    received, (vectors, result, psi, rounded) = refs[:4], refs[4:]
    halo_part(acc, links, position(), *received, psi)
    slices, layers = acc.shape[0], acc.shape[1]
    columns = acc.shape[5]
    half_count = vectors.shape[4] // 128
    for t in range(slices):
        for z in range(layers):
            for colour in range(3):
                for spin in range(4):
                    for ri in range(2):
                        row = (ri * 4 + spin) * columns
                        rounded[t, z, colour, pl.ds(row, columns), :] = psi[
                            t, z, spin, ri, colour
                        ].astype(BF16)
    side = 4 * columns
    for t in range(slices):
        sums = []
        for part in range(2):
            total = None
            for z in range(layers):
                for colour in range(3):
                    product = lax.dot_general(
                        rounded[t, z, colour],
                        vectors[t, z, part, colour],
                        (((1,), (1,)), ((), ())),
                        preferred_element_type=F32,
                    )
                    total = product if total is None else total + product
            sums.append(total)
        real = (sums[0][:side] + sums[1][side:]) * scale
        imag = (sums[0][side:] - sums[1][:side]) * scale
        for ri, value in enumerate((real, imag)):
            for k in range(half_count):
                row = (t * 2 + ri) * half_count + k
                result[:, row, :] = value[:, k * 128 : (k + 1) * 128]


def mix_kernel(shares, elemental, result):
    slices = elemental.shape[0]
    eigen_count = elemental.shape[2]
    half_count = eigen_count // 128
    total = jnp.sum(shares[...], axis=0)

    def pieces(value):
        first = value.astype(BF16)
        rest = value - first.astype(F32)
        second = rest.astype(BF16)
        third = (rest - second.astype(F32)).astype(BF16)
        return [first, second, third]

    def row_of(t, ri):
        start = (t * 2 + ri) * half_count
        return jnp.concatenate([total[start + k : start + k + 1] for k in range(half_count)], axis=1)

    for t in range(slices):
        parts = jnp.concatenate([row_of(t, 0), row_of(t, 1)], axis=0)
        terms = []
        for component in range(2):
            weights = elemental[t, component]
            whole = None
            for piece in pieces(parts):
                product = lax.dot_general(
                    piece, weights, (((1,), (1,)), ((), ())), preferred_element_type=F32
                )
                whole = product if whole is None else whole + product
            terms.append(whole)
        real = terms[0][0:1] - terms[1][1:2]
        imag = terms[0][1:2] + terms[1][0:1]
        for ri, value in enumerate((real, imag)):
            for k in range(half_count):
                row = (t * 2 + ri) * half_count + k
                piece = value[:, k * 128 : (k + 1) * 128].astype(BF16)
                result[:, row : row + 1, :] = jnp.broadcast_to(
                    piece[None], (result.shape[0], 1, 128)
                )


def expand_kernel(mixed, vectors, links, psi, *refs):
    sent, (turned, left) = refs[:4], refs[4:]
    slices, layers = psi.shape[0], psi.shape[1]
    columns = psi.shape[5]
    eigen_count = vectors.shape[4]
    half_count = eigen_count // 128
    side = 4 * columns
    scale = eigen_count ** (-0.5)
    turned[...] = mixed[...].astype(F32)
    for t in range(slices):
        for ri in range(2):
            for k in range(half_count):
                row = (t * 2 + ri) * half_count + k
                value = turned[:, row, :]
                lanes = slice(k * 128, (k + 1) * 128)
                own = value.astype(BF16)
                if ri == 0:
                    left[0, :side, lanes] = own
                    left[1, side:, lanes] = own
                else:
                    left[0, side:, lanes] = own
                    left[1, :side, lanes] = (-value).astype(BF16)
        for z in range(layers):
            for colour in range(3):
                value = jnp.dot(left[0], vectors[t, z, 0, colour], preferred_element_type=F32)
                value += jnp.dot(left[1], vectors[t, z, 1, colour], preferred_element_type=F32)
                value = value * scale
                for ri in range(2):
                    for spin in range(4):
                        row = (ri * 4 + spin) * columns
                        psi[t, z, spin, ri, colour] = value[row : row + columns]
    faces_part(psi, links, position(), *sent)


def on_device(source, gauge_links, clover, eigenvectors, elemental):
    slices, layers = source.shape[0], source.shape[1]
    columns, sites = source.shape[5], source.shape[6]
    eigen_count = eigenvectors.shape[4]
    space_count = lax.axis_size("space")
    spinor_type = jax.ShapeDtypeStruct(source.shape, F32)
    z_face = jax.ShapeDtypeStruct((slices, 2, 2, 3, columns, sites), BF16)
    t_face = jax.ShapeDtypeStruct((layers, 2, 2, 3, columns, sites), BF16)
    faces = (z_face, z_face, t_face, t_face)
    link_rows = jax.ShapeDtypeStruct((slices, layers, 72, sites), F32)
    clover_rows = jax.ShapeDtypeStruct((slices, layers, 144, sites), F32)
    row_count = slices * 2 * eigen_count // 128

    def swapped(value, axis, offset):
        count = lax.axis_size(axis)
        pairs = [(i % count, (i + 1) % count) for i in range(offset, count + offset, 2)]
        return lax.ppermute(value, axis, pairs + [(b, a) for a, b in pairs])

    def exchanged(z_inner, z_outer, t_inner, t_outer):
        z_far = swapped(z_outer, "space", 1)
        t_far = swapped(t_outer, "tm", 1)
        return swapped(z_inner, "space", 0), z_far, swapped(t_inner, "tm", 0), t_far

    psi, links, *sent = call(
        entry_kernel, 2, (spinor_type, link_rows) + faces, name="entry"
    )(source, jnp.transpose(gauge_links, (0, 1, 2, 4, 5, 3, 6)))
    got = exchanged(*sent)
    clover_f32 = call(clover_kernel, 1, clover_rows, name="clover_rows")(
        jnp.transpose(clover, (0, 1, 2, 4, 5, 3, 6))
    )

    def local(spinor):
        return call(local_kernel, 3, spinor_type, flops=1 << 26, name="local")(
            spinor, links, clover_f32
        )

    def middle(acc, received):
        return call(middle_kernel, 6, (spinor_type,) + faces, name="middle")(
            acc, links, *received
        )

    acc = local(psi)
    psi, *sent = middle(acc, got)
    got = exchanged(*sent)
    acc = local(psi)
    normaliser = (3.0 * X * Y * layers * space_count) ** (-0.5)
    scratch_psi = pltpu.VMEM(source.shape, F32)
    partial_sums = call(
        functools.partial(coefficient_kernel, normaliser),
        7,
        jax.ShapeDtypeStruct((4 * columns, row_count, 128), F32),
        scratch=(scratch_psi, pltpu.VMEM((slices, layers, 3, 8 * columns, sites), BF16)),
        name="coefficients",
    )(acc, links, *got, eigenvectors)
    shares = lax.all_to_all(partial_sums, "space", 0, 0, tiled=True)
    mixed = call(
        mix_kernel,
        2,
        jax.ShapeDtypeStruct((space_count, row_count, 128), BF16),
        name="mix",
    )(shares, elemental)
    mixed = lax.all_to_all(mixed, "space", 0, 0, tiled=True)
    psi, *sent = call(
        expand_kernel,
        3,
        (spinor_type,) + faces,
        scratch=(
            pltpu.VMEM((4 * columns, row_count, 128), F32),
            pltpu.VMEM((2, 8 * columns, eigen_count), BF16),
        ),
        name="expand",
    )(mixed, eigenvectors, links)
    got = exchanged(*sent)
    acc = local(psi)
    psi, *sent = middle(acc, got)
    got = exchanged(*sent)
    acc = local(psi)
    return call(
        last_kernel,
        6,
        jax.ShapeDtypeStruct(source.shape, BF16),
        scratch=(scratch_psi,),
        name="last",
    )(acc, links, *got)


def solution(mesh):
    placed = (
        P("tm", "space", None, None, None, None, None),
        P("tm", "space", None, None, None, None, None),
        P("tm", "space", None, None, None, None, None),
        P("tm", "space", None, None, None, None),
        P("tm", None, None, None),
    )
    return jax.shard_map(
        on_device,
        mesh=mesh,
        in_specs=placed,
        out_specs=P("tm", "space", None, None, None, None, None),
        check_vma=False,
    )
```

time: 176 us -> 124 us (0.70)
  other arithmetic: 35.2 us -> 0 us
  starting transfers between devices: 78.4 us -> 63.8 us
  Pallas kernels: 0 us -> 14.3 us
  local copies, waits for them, and re-layouts: 16.4 us -> 2.8 us
  blocking collectives: 18.7 us -> 31.8 us
  waiting for transfers between devices: 19 us -> 10.2 us
  between operations: 4.25 us -> 0.34 us
  matrix products: 2.89 us -> 0 us
    pallas_call x0 -> x12, Pallas kernels: none -> 14.3 us  [the longest x4 8.93 us: local(): call(local_kernel, 3, spinor_type, flops=1 << 26, name='local')]
    all_to_all x1 -> x2, blocking collectives: 18.7 us -> 31.8 us  [the longest x1 16 us: on_device(): shares = lax.all_to_all(partial_sums, 'space', 0, 0, tiled=True)]
    sub x87 -> x0, other arithmetic: 10.9 us -> none  [the longest x32 5.32 us: colour_apply(): real_out = real_out + left_real * right_real - left_imag * right_imag]
    ppermute x16, starting transfers between devices: 73.8 us -> 63.8 us  [swapped(): return lax.ppermute(value, axis, pairs + [(b, a) for a, b in pairs])]
    all_to_all x1 -> x0, waiting for transfers between devices: 9.91 us -> none  [on_device(): mixed_coef = lax.all_to_all(everywhere, 'space', 0, 0, tiled=True)]
    add x32 -> x0, other arithmetic: 7.35 us -> none  [the longest x8 3.2 us: clover_apply(): imag_out = imag_out + left_real * right_imag + left_imag * right_real]
    another operation x83 -> x0, other arithmetic: 7.33 us -> none  [the longest x16 4.31 us: colour_apply(): return jnp.stack([real_out, imag_out], axis=3)]
    slice x34 -> x0, local copies, waits for them, and re-layouts: 5.27 us -> none  [the longest x8 1.48 us: dirac(): lax.slice_in_dim(ahead_own, 1, size, axis=dim)]
  transfers between devices with their start and end apart: 17 -> 16, of which waited for: 3 -> 3; matrix products, arithmetic and copies ran while one was open for 17% -> 0% of each run, Pallas kernels for 0% -> 7%
where the time goes in v2:
time: 124 us; the launch traced here: 123 us
  starting transfers between devices  63.8 us (51%)
  blocking collectives  31.8 us (26%)
  Pallas kernels  14.3 us (12%)
  waiting for transfers between devices  10.2 us (8%)
  local copies, waits for them, and re-layouts  2.8 us (2%)
    ppermute x16, starting transfers between devices, swapped(): return lax.ppermute(value, axis, pairs + [(b, a) for a, b in pairs])  63.8 us
    all_to_all x1, blocking collectives, on_device(): shares = lax.all_to_all(partial_sums, 'space', 0, 0, tiled=True)  16 us
    all_to_all x1, blocking collectives, on_device(): mixed = lax.all_to_all(mixed, 'space', 0, 0, tiled=True)  15.8 us
    ppermute x16, waiting for transfers between devices, swapped(): return lax.ppermute(value, axis, pairs + [(b, a) for a, b in pairs])  10.2 us
    pallas_call x4, Pallas kernels, local(): call(local_kernel, 3, spinor_type, flops=1 << 26, name='local')  8.93 us
    unnamed x10, local copies, waits for them, and re-layouts  2.8 us
  transfers between devices with their start and end apart: 16, of which 3 were waited for; matrix products, arithmetic and copies ran while one was open for 0% of the time, Pallas kernels for 7%

profile of v2, /device:TPU:1, one launch (start us, length us, event | category | flops | bytes accessed | tf_op | source)
XLA Modules:
  0.0 123.2 jit_solution(18112027276662824129)
XLA Ops:
  0.0 1.0 copy-done.2
  1.0 0.9 copy-done.4
  2.2 4.0 %collective-permute-start = (bf16[2,2,2,3,16,128]{5,4,3,2,1,0:T(8,128)(2,1)S(1)}, bf16[2,2,2,3,16,128]{5,4,3,2,1,0:T(8,128)(2,1)S(1)}, u32[]{:S(2)}, u32[]{:S(2)}) collective-permute-start(bf16[2,2,2,3,16,128]{5,4,3,2,1,0:T(8,128)(2,1)S(1)} %get-tuple-element.28), channel_id=1, source_target_pairs={{0,8},{16,24},{32,40},{48,56},{64,72},{80,88},{96,104},{112,120},{... | collective-permute-start | bytes 294920 | tf_op jit(solution)/shard_map/ppermute | solution.py:474
  6.3 8.9 %collective-permute-start.1 = (bf16[2,2,2,3,16,128]{5,4,3,2,1,0:T(8,128)(2,1)S(1)}, bf16[2,2,2,3,16,128]{5,4,3,2,1,0:T(8,128)(2,1)S(1)}, u32[]{:S(2)}, u32[]{:S(2)}) collective-permute-start(bf16[2,2,2,3,16,128]{5,4,3,2,1,0:T(8,128)(2,1)S(1)} %get-tuple-element.29), channel_id=1, source_target_pairs={{8,16},{24,32},{40,48},{56,64},{72,80},{88,96},{104,112},{120,128}... | collective-permute-start | bytes 294920 | tf_op jit(solution)/shard_map/ppermute | solution.py:474
  15.1 3.1 %collective-permute-start.2 = (bf16[2,2,2,3,16,128]{5,4,3,2,1,0:T(8,128)(2,1)S(1)}, bf16[2,2,2,3,16,128]{5,4,3,2,1,0:T(8,128)(2,1)S(1)}, u32[]{:S(2)}, u32[]{:S(2)}) collective-permute-start(bf16[2,2,2,3,16,128]{5,4,3,2,1,0:T(8,128)(2,1)S(1)} %get-tuple-element.30), channel_id=1, source_target_pairs={{0,1},{2,3},{4,5},{6,7},{1,0},{3,2},{5,4},{7,6},{8,9},{10,11},{12,... | collective-permute-start | bytes 294920 | tf_op jit(solution)/shard_map/ppermute | solution.py:474
  18.3 5.7 %collective-permute-start.3 = (bf16[2,2,2,3,16,128]{5,4,3,2,1,0:T(8,128)(2,1)S(1)}, bf16[2,2,2,3,16,128]{5,4,3,2,1,0:T(8,128)(2,1)S(1)}, u32[]{:S(2)}, u32[]{:S(2)}) collective-permute-start(bf16[2,2,2,3,16,128]{5,4,3,2,1,0:T(8,128)(2,1)S(1)} %get-tuple-element.31), channel_id=1, source_target_pairs={{1,2},{3,4},{5,6},{7,0},{2,1},{4,3},{6,5},{0,7},{9,10},{11,12},{13... | collective-permute-start | bytes 294920 | tf_op jit(solution)/shard_map/ppermute | solution.py:474
  24.0 0.9 copy-done.3
  25.0 2.2 %local.4.acc = f32[2,2,4,2,3,16,128]{6,5,4,3,2,1,0:T(8,128)S(1)} custom-call(f32[2,2,4,2,3,16,128]{6,5,4,3,2,1,0:T(8,128)S(1)} %get-tuple-element.26.psi, f32[2,2,72,128]{3,2,1,0:T(8,128)S(1)} %get-tuple-element.27.links, f32[2,2,144,128]{3,2,1,0:T(8,128)S(1)} %clover_rows.1.clover), custom_call_target="tpu_custom_call" | custom-call | flops 67108864 | bytes 2097152 | tf_op jit(solution)/shard_map/local/pallas_call | solution.py:490
  27.9 1.9 %collective-permute-start.4 = (bf16[2,2,2,3,16,128]{5,4,3,2,1,0:T(8,128)(2,1)S(1)}, bf16[2,2,2,3,16,128]{5,4,3,2,1,0:T(8,128)(2,1)S(1)}, u32[]{:S(2)}, u32[]{:S(2)}) collective-permute-start(bf16[2,2,2,3,16,128]{5,4,3,2,1,0:T(8,128)(2,1)S(1)} %get-tuple-element.33), channel_id=1, source_target_pairs={{0,8},{16,24},{32,40},{48,56},{64,72},{80,88},{96,104},{112,120},{... | collective-permute-start | bytes 294920 | tf_op jit(solution)/shard_map/ppermute | solution.py:474
  29.8 4.0 %collective-permute-start.5 = (bf16[2,2,2,3,16,128]{5,4,3,2,1,0:T(8,128)(2,1)S(1)}, bf16[2,2,2,3,16,128]{5,4,3,2,1,0:T(8,128)(2,1)S(1)}, u32[]{:S(2)}, u32[]{:S(2)}) collective-permute-start(bf16[2,2,2,3,16,128]{5,4,3,2,1,0:T(8,128)(2,1)S(1)} %get-tuple-element.34), channel_id=1, source_target_pairs={{8,16},{24,32},{40,48},{56,64},{72,80},{88,96},{104,112},{120,128}... | collective-permute-start | bytes 294920 | tf_op jit(solution)/shard_map/ppermute | solution.py:474
  33.8 6.9 %collective-permute-start.6 = (bf16[2,2,2,3,16,128]{5,4,3,2,1,0:T(8,128)(2,1)S(1)}, bf16[2,2,2,3,16,128]{5,4,3,2,1,0:T(8,128)(2,1)S(1)}, u32[]{:S(2)}, u32[]{:S(2)}) collective-permute-start(bf16[2,2,2,3,16,128]{5,4,3,2,1,0:T(8,128)(2,1)S(1)} %get-tuple-element.35), channel_id=1, source_target_pairs={{0,1},{2,3},{4,5},{6,7},{1,0},{3,2},{5,4},{7,6},{8,9},{10,11},{12,... | collective-permute-start | bytes 294920 | tf_op jit(solution)/shard_map/ppermute | solution.py:474
  40.8 1.9 %collective-permute-start.7 = (bf16[2,2,2,3,16,128]{5,4,3,2,1,0:T(8,128)(2,1)S(1)}, bf16[2,2,2,3,16,128]{5,4,3,2,1,0:T(8,128)(2,1)S(1)}, u32[]{:S(2)}, u32[]{:S(2)}) collective-permute-start(bf16[2,2,2,3,16,128]{5,4,3,2,1,0:T(8,128)(2,1)S(1)} %get-tuple-element.36), channel_id=1, source_target_pairs={{1,2},{3,4},{5,6},{7,0},{2,1},{4,3},{6,5},{0,7},{9,10},{11,12},{13... | collective-permute-start | bytes 294920 | tf_op jit(solution)/shard_map/ppermute | solution.py:474
  42.7 2.2 %local.5.acc = f32[2,2,4,2,3,16,128]{6,5,4,3,2,1,0:T(8,128)S(1)} custom-call(f32[2,2,4,2,3,16,128]{6,5,4,3,2,1,0:T(8,128)S(1)} %get-tuple-element.32.psi, f32[2,2,72,128]{3,2,1,0:T(8,128)S(1)} %get-tuple-element.27.links, f32[2,2,144,128]{3,2,1,0:T(8,128)S(1)} %clover_rows.1.clover), custom_call_target="tpu_custom_call" | custom-call | flops 67108864 | bytes 2097152 | tf_op jit(solution)/shard_map/local/pallas_call | solution.py:490
  45.0 3.8 %collective-permute-done.7.refs_3_ = bf16[2,2,2,3,16,128]{5,4,3,2,1,0:T(8,128)(2,1)S(1)} collective-permute-done((bf16[2,2,2,3,16,128]{5,4,3,2,1,0:T(8,128)(2,1)S(1)}, bf16[2,2,2,3,16,128]{5,4,3,2,1,0:T(8,128)(2,1)S(1)}, u32[]{:S(2)}, u32[]{:S(2)}) %collective-permute-start.7) | collective-permute-done | bytes 98336 | tf_op jit(solution)/shard_map/ppermute | solution.py:474
  48.8 1.0 coefficients.1
  49.8 16.0 %all_to_all.10.shares = f32[64,8,128]{2,1,0:T(8,128)S(1)} all-to-all(f32[64,8,128]{2,1,0:T(8,128)S(1)} %coefficients.1), channel_id=1, replica_groups=mesh['space'=64,'tm'=8] {'space'}, dimensions={0} | all-to-all | bytes 524288 | tf_op jit(solution)/shard_map/all_to_all | solution.py:512
  65.8 0.7 mix.1
  66.5 15.8 %all_to_all.11.mixed = bf16[64,8,128]{2,1,0:T(8,128)(2,1)S(1)} all-to-all(bf16[64,8,128]{2,1,0:T(8,128)(2,1)S(1)} %mix.1), channel_id=1, replica_groups=mesh['space'=64,'tm'=8] {'space'}, dimensions={0} | all-to-all | bytes 262144 | tf_op jit(solution)/shard_map/all_to_all | solution.py:519
  82.3 1.2 expand.1
  83.4 2.7 %collective-permute-start.8 = (bf16[2,2,2,3,16,128]{5,4,3,2,1,0:T(8,128)(2,1)S(1)}, bf16[2,2,2,3,16,128]{5,4,3,2,1,0:T(8,128)(2,1)S(1)}, u32[]{:S(2)}, u32[]{:S(2)}) collective-permute-start(bf16[2,2,2,3,16,128]{5,4,3,2,1,0:T(8,128)(2,1)S(1)} %get-tuple-element.38), channel_id=1, source_target_pairs={{0,8},{16,24},{32,40},{48,56},{64,72},{80,88},{96,104},{112,120},{... | collective-permute-start | bytes 294920 | tf_op jit(solution)/shard_map/ppermute | solution.py:474
  86.1 3.0 %collective-permute-start.9 = (bf16[2,2,2,3,16,128]{5,4,3,2,1,0:T(8,128)(2,1)S(1)}, bf16[2,2,2,3,16,128]{5,4,3,2,1,0:T(8,128)(2,1)S(1)}, u32[]{:S(2)}, u32[]{:S(2)}) collective-permute-start(bf16[2,2,2,3,16,128]{5,4,3,2,1,0:T(8,128)(2,1)S(1)} %get-tuple-element.39), channel_id=1, source_target_pairs={{8,16},{24,32},{40,48},{56,64},{72,80},{88,96},{104,112},{120,128}... | collective-permute-start | bytes 294920 | tf_op jit(solution)/shard_map/ppermute | solution.py:474
  89.2 5.5 %collective-permute-start.10 = (bf16[2,2,2,3,16,128]{5,4,3,2,1,0:T(8,128)(2,1)S(1)}, bf16[2,2,2,3,16,128]{5,4,3,2,1,0:T(8,128)(2,1)S(1)}, u32[]{:S(2)}, u32[]{:S(2)}) collective-permute-start(bf16[2,2,2,3,16,128]{5,4,3,2,1,0:T(8,128)(2,1)S(1)} %get-tuple-element.40), channel_id=1, source_target_pairs={{0,1},{2,3},{4,5},{6,7},{1,0},{3,2},{5,4},{7,6},{8,9},{10,11},{12,... | collective-permute-start | bytes 294920 | tf_op jit(solution)/shard_map/ppermute | solution.py:474
  94.6 2.1 %collective-permute-start.11 = (bf16[2,2,2,3,16,128]{5,4,3,2,1,0:T(8,128)(2,1)S(1)}, bf16[2,2,2,3,16,128]{5,4,3,2,1,0:T(8,128)(2,1)S(1)}, u32[]{:S(2)}, u32[]{:S(2)}) collective-permute-start(bf16[2,2,2,3,16,128]{5,4,3,2,1,0:T(8,128)(2,1)S(1)} %get-tuple-element.41), channel_id=1, source_target_pairs={{1,2},{3,4},{5,6},{7,0},{2,1},{4,3},{6,5},{0,7},{9,10},{11,12},{13... | collective-permute-start | bytes 294920 | tf_op jit(solution)/shard_map/ppermute | solution.py:474
  96.7 2.2 %local.6.acc = f32[2,2,4,2,3,16,128]{6,5,4,3,2,1,0:T(8,128)S(1)} custom-call(f32[2,2,4,2,3,16,128]{6,5,4,3,2,1,0:T(8,128)S(1)} %get-tuple-element.37.psi, f32[2,2,72,128]{3,2,1,0:T(8,128)S(1)} %get-tuple-element.27.links, f32[2,2,144,128]{3,2,1,0:T(8,128)S(1)} %clover_rows.1.clover), custom_call_target="tpu_custom_call" | custom-call | flops 67108864 | bytes 2097152 | tf_op jit(solution)/shard_map/local/pallas_call | solution.py:490
  99.0 3.4 %collective-permute-done.11.refs_3_ = bf16[2,2,2,3,16,128]{5,4,3,2,1,0:T(8,128)(2,1)S(1)} collective-permute-done((bf16[2,2,2,3,16,128]{5,4,3,2,1,0:T(8,128)(2,1)S(1)}, bf16[2,2,2,3,16,128]{5,4,3,2,1,0:T(8,128)(2,1)S(1)}, u32[]{:S(2)}, u32[]{:S(2)}) %collective-permute-start.11) | collective-permute-done | bytes 98336 | tf_op jit(solution)/shard_map/ppermute | solution.py:474
  102.9 1.9 %collective-permute-start.12 = (bf16[2,2,2,3,16,128]{5,4,3,2,1,0:T(8,128)(2,1)S(1)}, bf16[2,2,2,3,16,128]{5,4,3,2,1,0:T(8,128)(2,1)S(1)}, u32[]{:S(2)}, u32[]{:S(2)}) collective-permute-start(bf16[2,2,2,3,16,128]{5,4,3,2,1,0:T(8,128)(2,1)S(1)} %get-tuple-element.43), channel_id=1, source_target_pairs={{0,8},{16,24},{32,40},{48,56},{64,72},{80,88},{96,104},{112,120},{... | collective-permute-start | bytes 294920 | tf_op jit(solution)/shard_map/ppermute | solution.py:474
  104.9 6.5 %collective-permute-start.13 = (bf16[2,2,2,3,16,128]{5,4,3,2,1,0:T(8,128)(2,1)S(1)}, bf16[2,2,2,3,16,128]{5,4,3,2,1,0:T(8,128)(2,1)S(1)}, u32[]{:S(2)}, u32[]{:S(2)}) collective-permute-start(bf16[2,2,2,3,16,128]{5,4,3,2,1,0:T(8,128)(2,1)S(1)} %get-tuple-element.44), channel_id=1, source_target_pairs={{8,16},{24,32},{40,48},{56,64},{72,80},{88,96},{104,112},{120,128}... | collective-permute-start | bytes 294920 | tf_op jit(solution)/shard_map/ppermute | solution.py:474
  111.4 3.6 %collective-permute-start.14 = (bf16[2,2,2,3,16,128]{5,4,3,2,1,0:T(8,128)(2,1)S(1)}, bf16[2,2,2,3,16,128]{5,4,3,2,1,0:T(8,128)(2,1)S(1)}, u32[]{:S(2)}, u32[]{:S(2)}) collective-permute-start(bf16[2,2,2,3,16,128]{5,4,3,2,1,0:T(8,128)(2,1)S(1)} %get-tuple-element.45), channel_id=1, source_target_pairs={{0,1},{2,3},{4,5},{6,7},{1,0},{3,2},{5,4},{7,6},{8,9},{10,11},{12,... | collective-permute-start | bytes 294920 | tf_op jit(solution)/shard_map/ppermute | solution.py:474
  115.0 1.9 %collective-permute-start.15 = (bf16[2,2,2,3,16,128]{5,4,3,2,1,0:T(8,128)(2,1)S(1)}, bf16[2,2,2,3,16,128]{5,4,3,2,1,0:T(8,128)(2,1)S(1)}, u32[]{:S(2)}, u32[]{:S(2)}) collective-permute-start(bf16[2,2,2,3,16,128]{5,4,3,2,1,0:T(8,128)(2,1)S(1)} %get-tuple-element.46), channel_id=1, source_target_pairs={{1,2},{3,4},{5,6},{7,0},{2,1},{4,3},{6,5},{0,7},{9,10},{11,12},{13... | collective-permute-start | bytes 294920 | tf_op jit(solution)/shard_map/ppermute | solution.py:474
  116.9 2.2 %local.7.acc = f32[2,2,4,2,3,16,128]{6,5,4,3,2,1,0:T(8,128)S(1)} custom-call(f32[2,2,4,2,3,16,128]{6,5,4,3,2,1,0:T(8,128)S(1)} %get-tuple-element.42.psi, f32[2,2,72,128]{3,2,1,0:T(8,128)S(1)} %get-tuple-element.27.links, f32[2,2,144,128]{3,2,1,0:T(8,128)S(1)} %clover_rows.1.clover), custom_call_target="tpu_custom_call" | custom-call | flops 67108864 | bytes 2097152 | tf_op jit(solution)/shard_map/local/pallas_call | solution.py:490
  119.2 3.0 %collective-permute-done.15.refs_3_ = bf16[2,2,2,3,16,128]{5,4,3,2,1,0:T(8,128)(2,1)S(1)} collective-permute-done((bf16[2,2,2,3,16,128]{5,4,3,2,1,0:T(8,128)(2,1)S(1)}, bf16[2,2,2,3,16,128]{5,4,3,2,1,0:T(8,128)(2,1)S(1)}, u32[]{:S(2)}, u32[]{:S(2)}) %collective-permute-start.15) | collective-permute-done | bytes 98336 | tf_op jit(solution)/shard_map/ppermute | solution.py:474
  122.2 1.1 last.1
  (24 shorter events, 1.5 us)
Async XLA Ops:
  0.0 1.0 copy-start.2
  1.0 0.9 copy-start.4
  2.2 25.1 %collective-permute-start = (bf16[2,2,2,3,16,128]{5,4,3,2,1,0:T(8,128)(2,1)S(1)}, bf16[2,2,2,3,16,128]{5,4,3,2,1,0:T(8,128)(2,1)S(1)}, u32[]{:S(2)}, u32[]{:S(2)}) collective-permute-start(bf16[2,2,2,3,16,128]{5,4,3,2,1,0:T(8,128)(2,1)S(1)} %get-tuple-element.28), channel_id=1, source_target_pairs={{0,8},{16,24},{32,40},{48,56},{64,72},{80,88},{96,104},{112,120},{... | collective-permute-start | bytes 294920 | tf_op jit(solution)/shard_map/ppermute | solution.py:474
  6.3 21.0 %collective-permute-start.1 = (bf16[2,2,2,3,16,128]{5,4,3,2,1,0:T(8,128)(2,1)S(1)}, bf16[2,2,2,3,16,128]{5,4,3,2,1,0:T(8,128)(2,1)S(1)}, u32[]{:S(2)}, u32[]{:S(2)}) collective-permute-start(bf16[2,2,2,3,16,128]{5,4,3,2,1,0:T(8,128)(2,1)S(1)} %get-tuple-element.29), channel_id=1, source_target_pairs={{8,16},{24,32},{40,48},{56,64},{72,80},{88,96},{104,112},{120,128}... | collective-permute-start | bytes 294920 | tf_op jit(solution)/shard_map/ppermute | solution.py:474
  15.1 12.2 %collective-permute-start.2 = (bf16[2,2,2,3,16,128]{5,4,3,2,1,0:T(8,128)(2,1)S(1)}, bf16[2,2,2,3,16,128]{5,4,3,2,1,0:T(8,128)(2,1)S(1)}, u32[]{:S(2)}, u32[]{:S(2)}) collective-permute-start(bf16[2,2,2,3,16,128]{5,4,3,2,1,0:T(8,128)(2,1)S(1)} %get-tuple-element.30), channel_id=1, source_target_pairs={{0,1},{2,3},{4,5},{6,7},{1,0},{3,2},{5,4},{7,6},{8,9},{10,11},{12,... | collective-permute-start | bytes 294920 | tf_op jit(solution)/shard_map/ppermute | solution.py:474
  18.3 9.0 %collective-permute-start.3 = (bf16[2,2,2,3,16,128]{5,4,3,2,1,0:T(8,128)(2,1)S(1)}, bf16[2,2,2,3,16,128]{5,4,3,2,1,0:T(8,128)(2,1)S(1)}, u32[]{:S(2)}, u32[]{:S(2)}) collective-permute-start(bf16[2,2,2,3,16,128]{5,4,3,2,1,0:T(8,128)(2,1)S(1)} %get-tuple-element.31), channel_id=1, source_target_pairs={{1,2},{3,4},{5,6},{7,0},{2,1},{4,3},{6,5},{0,7},{9,10},{11,12},{13... | collective-permute-start | bytes 294920 | tf_op jit(solution)/shard_map/ppermute | solution.py:474
  24.0 0.9 copy-start.3
  27.3 21.5 %copy-start = (bf16[2,2,2,3,256,128]{5,4,3,2,1,0:T(8,128)(2,1)S(1)}, bf16[2,2,2,3,256,128]{5,4,3,2,1,0:T(8,128)(2,1)}, u32[]{:S(2)}) copy-start(bf16[2,2,2,3,256,128]{5,4,3,2,1,0:T(8,128)(2,1)} %vectors.1) | copy-start | bytes 4718596
  27.9 17.1 %collective-permute-start.4 = (bf16[2,2,2,3,16,128]{5,4,3,2,1,0:T(8,128)(2,1)S(1)}, bf16[2,2,2,3,16,128]{5,4,3,2,1,0:T(8,128)(2,1)S(1)}, u32[]{:S(2)}, u32[]{:S(2)}) collective-permute-start(bf16[2,2,2,3,16,128]{5,4,3,2,1,0:T(8,128)(2,1)S(1)} %get-tuple-element.33), channel_id=1, source_target_pairs={{0,8},{16,24},{32,40},{48,56},{64,72},{80,88},{96,104},{112,120},{... | collective-permute-start | bytes 294920 | tf_op jit(solution)/shard_map/ppermute | solution.py:474
  29.8 15.2 %collective-permute-start.5 = (bf16[2,2,2,3,16,128]{5,4,3,2,1,0:T(8,128)(2,1)S(1)}, bf16[2,2,2,3,16,128]{5,4,3,2,1,0:T(8,128)(2,1)S(1)}, u32[]{:S(2)}, u32[]{:S(2)}) collective-permute-start(bf16[2,2,2,3,16,128]{5,4,3,2,1,0:T(8,128)(2,1)S(1)} %get-tuple-element.34), channel_id=1, source_target_pairs={{8,16},{24,32},{40,48},{56,64},{72,80},{88,96},{104,112},{120,128}... | collective-permute-start | bytes 294920 | tf_op jit(solution)/shard_map/ppermute | solution.py:474
  33.8 11.1 %collective-permute-start.6 = (bf16[2,2,2,3,16,128]{5,4,3,2,1,0:T(8,128)(2,1)S(1)}, bf16[2,2,2,3,16,128]{5,4,3,2,1,0:T(8,128)(2,1)S(1)}, u32[]{:S(2)}, u32[]{:S(2)}) collective-permute-start(bf16[2,2,2,3,16,128]{5,4,3,2,1,0:T(8,128)(2,1)S(1)} %get-tuple-element.35), channel_id=1, source_target_pairs={{0,1},{2,3},{4,5},{6,7},{1,0},{3,2},{5,4},{7,6},{8,9},{10,11},{12,... | collective-permute-start | bytes 294920 | tf_op jit(solution)/shard_map/ppermute | solution.py:474
  40.8 8.0 %collective-permute-start.7 = (bf16[2,2,2,3,16,128]{5,4,3,2,1,0:T(8,128)(2,1)S(1)}, bf16[2,2,2,3,16,128]{5,4,3,2,1,0:T(8,128)(2,1)S(1)}, u32[]{:S(2)}, u32[]{:S(2)}) collective-permute-start(bf16[2,2,2,3,16,128]{5,4,3,2,1,0:T(8,128)(2,1)S(1)} %get-tuple-element.36), channel_id=1, source_target_pairs={{1,2},{3,4},{5,6},{7,0},{2,1},{4,3},{6,5},{0,7},{9,10},{11,12},{13... | collective-permute-start | bytes 294920 | tf_op jit(solution)/shard_map/ppermute | solution.py:474
  44.9 20.9 %copy-start.1 = (bf16[2,2,256,256]{3,2,1,0:T(8,128)(2,1)S(1)}, bf16[2,2,256,256]{3,2,1,0:T(8,128)(2,1)}, u32[]{:S(2)}) copy-start(bf16[2,2,256,256]{3,2,1,0:T(8,128)(2,1)} %elemental.1) | copy-start | bytes 1572868
  83.4 15.6 %collective-permute-start.8 = (bf16[2,2,2,3,16,128]{5,4,3,2,1,0:T(8,128)(2,1)S(1)}, bf16[2,2,2,3,16,128]{5,4,3,2,1,0:T(8,128)(2,1)S(1)}, u32[]{:S(2)}, u32[]{:S(2)}) collective-permute-start(bf16[2,2,2,3,16,128]{5,4,3,2,1,0:T(8,128)(2,1)S(1)} %get-tuple-element.38), channel_id=1, source_target_pairs={{0,8},{16,24},{32,40},{48,56},{64,72},{80,88},{96,104},{112,120},{... | collective-permute-start | bytes 294920 | tf_op jit(solution)/shard_map/ppermute | solution.py:474
  86.1 12.8 %collective-permute-start.9 = (bf16[2,2,2,3,16,128]{5,4,3,2,1,0:T(8,128)(2,1)S(1)}, bf16[2,2,2,3,16,128]{5,4,3,2,1,0:T(8,128)(2,1)S(1)}, u32[]{:S(2)}, u32[]{:S(2)}) collective-permute-start(bf16[2,2,2,3,16,128]{5,4,3,2,1,0:T(8,128)(2,1)S(1)} %get-tuple-element.39), channel_id=1, source_target_pairs={{8,16},{24,32},{40,48},{56,64},{72,80},{88,96},{104,112},{120,128}... | collective-permute-start | bytes 294920 | tf_op jit(solution)/shard_map/ppermute | solution.py:474
  89.2 9.8 %collective-permute-start.10 = (bf16[2,2,2,3,16,128]{5,4,3,2,1,0:T(8,128)(2,1)S(1)}, bf16[2,2,2,3,16,128]{5,4,3,2,1,0:T(8,128)(2,1)S(1)}, u32[]{:S(2)}, u32[]{:S(2)}) collective-permute-start(bf16[2,2,2,3,16,128]{5,4,3,2,1,0:T(8,128)(2,1)S(1)} %get-tuple-element.40), channel_id=1, source_target_pairs={{0,1},{2,3},{4,5},{6,7},{1,0},{3,2},{5,4},{7,6},{8,9},{10,11},{12,... | collective-permute-start | bytes 294920 | tf_op jit(solution)/shard_map/ppermute | solution.py:474
  94.6 7.8 %collective-permute-start.11 = (bf16[2,2,2,3,16,128]{5,4,3,2,1,0:T(8,128)(2,1)S(1)}, bf16[2,2,2,3,16,128]{5,4,3,2,1,0:T(8,128)(2,1)S(1)}, u32[]{:S(2)}, u32[]{:S(2)}) collective-permute-start(bf16[2,2,2,3,16,128]{5,4,3,2,1,0:T(8,128)(2,1)S(1)} %get-tuple-element.41), channel_id=1, source_target_pairs={{1,2},{3,4},{5,6},{7,0},{2,1},{4,3},{6,5},{0,7},{9,10},{11,12},{13... | collective-permute-start | bytes 294920 | tf_op jit(solution)/shard_map/ppermute | solution.py:474
  102.9 16.2 %collective-permute-start.12 = (bf16[2,2,2,3,16,128]{5,4,3,2,1,0:T(8,128)(2,1)S(1)}, bf16[2,2,2,3,16,128]{5,4,3,2,1,0:T(8,128)(2,1)S(1)}, u32[]{:S(2)}, u32[]{:S(2)}) collective-permute-start(bf16[2,2,2,3,16,128]{5,4,3,2,1,0:T(8,128)(2,1)S(1)} %get-tuple-element.43), channel_id=1, source_target_pairs={{0,8},{16,24},{32,40},{48,56},{64,72},{80,88},{96,104},{112,120},{... | collective-permute-start | bytes 294920 | tf_op jit(solution)/shard_map/ppermute | solution.py:474
  104.9 14.3 %collective-permute-start.13 = (bf16[2,2,2,3,16,128]{5,4,3,2,1,0:T(8,128)(2,1)S(1)}, bf16[2,2,2,3,16,128]{5,4,3,2,1,0:T(8,128)(2,1)S(1)}, u32[]{:S(2)}, u32[]{:S(2)}) collective-permute-start(bf16[2,2,2,3,16,128]{5,4,3,2,1,0:T(8,128)(2,1)S(1)} %get-tuple-element.44), channel_id=1, source_target_pairs={{8,16},{24,32},{40,48},{56,64},{72,80},{88,96},{104,112},{120,128}... | collective-permute-start | bytes 294920 | tf_op jit(solution)/shard_map/ppermute | solution.py:474
  111.4 7.8 %collective-permute-start.14 = (bf16[2,2,2,3,16,128]{5,4,3,2,1,0:T(8,128)(2,1)S(1)}, bf16[2,2,2,3,16,128]{5,4,3,2,1,0:T(8,128)(2,1)S(1)}, u32[]{:S(2)}, u32[]{:S(2)}) collective-permute-start(bf16[2,2,2,3,16,128]{5,4,3,2,1,0:T(8,128)(2,1)S(1)} %get-tuple-element.45), channel_id=1, source_target_pairs={{0,1},{2,3},{4,5},{6,7},{1,0},{3,2},{5,4},{7,6},{8,9},{10,11},{12,... | collective-permute-start | bytes 294920 | tf_op jit(solution)/shard_map/ppermute | solution.py:474
  115.0 7.2 %collective-permute-start.15 = (bf16[2,2,2,3,16,128]{5,4,3,2,1,0:T(8,128)(2,1)S(1)}, bf16[2,2,2,3,16,128]{5,4,3,2,1,0:T(8,128)(2,1)S(1)}, u32[]{:S(2)}, u32[]{:S(2)}) collective-permute-start(bf16[2,2,2,3,16,128]{5,4,3,2,1,0:T(8,128)(2,1)S(1)} %get-tuple-element.46), channel_id=1, source_target_pairs={{1,2},{3,4},{5,6},{7,0},{2,1},{4,3},{6,5},{0,7},{9,10},{11,12},{13... | collective-permute-start | bytes 294920 | tf_op jit(solution)/shard_map/ppermute | solution.py:474

commit v3 on v2

--- a/solution.py
+++ b/solution.py
@@ -50,25 +50,32 @@
     return half
 
 
+def products(rows, vector, sums, conjugate):
+    real, less, more = rows
+    vr, vi, both = vector
+    terms = (real * both, more * vr, less * vi) if conjugate else (real * both, less * vr, more * vi)
+    return list(terms) if sums is None else [old + new for old, new in zip(sums, terms)]
+
+
+def total_of(sums, conjugate):
+    if conjugate:
+        return sums[0] + sums[2], sums[0] - sums[1]
+    return sums[0] - sums[2], sums[0] + sums[1]
+
+
 def link_times(link, half, adjoint):
     result = [[[None] * 3, [None] * 3] for _ in range(2)]
+    vectors = [
+        [(h[0][b], h[1][b], h[0][b] + h[1][b]) for b in range(3)] for h in half
+    ]
     for a in range(3):
+        sums = [None, None]
         for b in range(3):
-            if adjoint:
-                real, imag = link(0, b, a), link(1, b, a)
-            else:
-                real, imag = link(0, a, b), link(1, a, b)
+            rows = link(b, a) if adjoint else link(a, b)
             for spin in range(2):
-                hr, hi = half[spin][0][b], half[spin][1][b]
-                if adjoint:
-                    new_real = real * hr + imag * hi
-                    new_imag = real * hi - imag * hr
-                else:
-                    new_real = real * hr - imag * hi
-                    new_imag = real * hi + imag * hr
-                out = result[spin]
-                out[0][a] = new_real if out[0][a] is None else out[0][a] + new_real
-                out[1][a] = new_imag if out[1][a] is None else out[1][a] + new_imag
+                sums[spin] = products(rows, vectors[spin][b], sums[spin], adjoint)
+        for spin in range(2):
+            result[spin][0][a], result[spin][1][a] = total_of(sums[spin], adjoint)
     return result
 
 
@@ -104,8 +111,18 @@
     return lambda spin, ri, colour: ref[t, z, spin, ri, colour, rows, :].astype(F32)
 
 
+def three_rows(ref, t, z, entry):
+    return [ref[t, z, pl.ds(entry * 3 + i, 1), :] for i in range(3)]
+
+
+def put_three_rows(ref, t, z, entry, value):
+    real, imag = value[0:1], value[1:2]
+    for i, row in enumerate((real, imag - real, imag + real)):
+        ref[t, z, pl.ds(entry * 3 + i, 1), :] = row
+
+
 def link_reader(links, t, z, mu):
-    return lambda ri, a, b: links[t, z, pl.ds(((mu * 3 + a) * 3 + b) * 2 + ri, 1), :]
+    return lambda a, b: three_rows(links, t, z, (mu * 3 + a) * 3 + b)
 
 
 KEYS = [(s, r, c) for s in range(4) for r in range(2) for c in range(3)]
@@ -136,20 +153,20 @@
         read = reader(psi, t, z, rows)
         total = {}
         for chiral in range(2):
+            vectors = []
+            for column in range(6):
+                real = read(2 * chiral + column // 3, 0, column % 3)
+                imag = read(2 * chiral + column // 3, 1, column % 3)
+                vectors.append((real, imag, real + imag))
             for row in range(6):
                 spin, colour = 2 * chiral + row // 3, row % 3
-                real = read(spin, 0, colour)
-                imag = read(spin, 1, colour)
+                sums = None
                 for column in range(6):
-                    at = ((chiral * 6 + row) * 6 + column) * 2
-                    cr = clover[t, z, pl.ds(at, 1), :]
-                    ci = clover[t, z, pl.ds(at + 1, 1), :]
-                    xr = read(2 * chiral + column // 3, 0, column % 3)
-                    xi = read(2 * chiral + column // 3, 1, column % 3)
-                    real = real + (cr * xr - ci * xi)
-                    imag = imag + (cr * xi + ci * xr)
-                total[(spin, 0, colour)] = real
-                total[(spin, 1, colour)] = imag
+                    entry = three_rows(clover, t, z, (chiral * 6 + row) * 6 + column)
+                    sums = products(entry, vectors[column], sums, False)
+                real, imag = total_of(sums, False)
+                total[(spin, 0, colour)] = vectors[row][0] + real
+                total[(spin, 1, colour)] = vectors[row][1] + imag
         for direction in range(2):
             link = link_reader(links, t, z, direction)
             half = mapped(project(read, direction, -1), functools.partial(ahead, direction))
@@ -205,7 +222,7 @@
     pl.when(jnp.logical_not(odd))(lambda: function(pair[1], pair[0]))
 
 
-def faces_part(psi, links, where, z_inner, z_outer, t_inner, t_outer):
+def faces_part(psi, links, where, z_outer, z_inner, t_outer, t_inner):
     by_parity(where[0], functools.partial(z_faces, psi, links), (z_inner, z_outer))
     by_parity(where[1], functools.partial(t_faces, psi, links), (t_inner, t_outer))
 
@@ -245,7 +262,7 @@
         out[t, z, key[0], key[1], key[2]] = total[key]
 
 
-def halo_part(acc, links, where, z_inner, z_outer, t_inner, t_outer, out):
+def halo_part(acc, links, where, z_outer, z_inner, t_outer, t_inner, out):
     by_parity(where[0], functools.partial(z_halo, acc, links, out), (z_inner, z_outer))
     by_parity(where[1], functools.partial(t_halo, links, where, out), (t_inner, t_outer))
 
@@ -285,11 +302,15 @@
 
 
 VMEM = pl.BlockSpec(memory_space=pltpu.VMEM)
-SMEM = pl.BlockSpec(memory_space=pltpu.SMEM)
-
-
-def call(kernel, in_count, out_shapes, scratch=(), smem=(), flops=1 << 22, name=None):
-    specs = [SMEM if i in smem else VMEM for i in range(in_count)]
+FAR = pl.BlockSpec(memory_space=pltpu.HBM)
+
+
+def in_far(value):
+    return pltpu.with_memory_space_constraint(value, pltpu.HBM)
+
+
+def call(kernel, in_count, out_shapes, scratch=(), far=(), flops=1 << 22, name=None):
+    specs = [FAR if i in far else VMEM for i in range(in_count)]
     return pl.pallas_call(
         kernel,
         out_shape=out_shapes,
@@ -302,17 +323,23 @@
     )
 
 
-def entry_kernel(source, gauge, psi, links, *sent):
-    psi[...] = source[...].astype(F32)
+def entry_kernel(source_far, gauge_far, psi, links, *refs):
+    sent, (source, gauge, arrived) = refs[:4], refs[4:]
+    gauge_copy = pltpu.make_async_copy(gauge_far, gauge, arrived.at[0])
+    source_copy = pltpu.make_async_copy(source_far, source, arrived.at[1])
+    gauge_copy.start()
+    source_copy.start()
+    gauge_copy.wait()
     slices, layers = source.shape[0], source.shape[1]
     for t in range(slices):
         for z in range(layers):
             for mu in range(4):
                 for a in range(3):
                     for b in range(3):
-                        row = ((mu * 3 + a) * 3 + b) * 2
-                        value = gauge[t, z, mu, a, b].astype(F32)
-                        links[t, z, pl.ds(row, 2), :] = value * (-HOPPING)
+                        value = gauge[t, z, mu, a, b].astype(F32) * (-HOPPING)
+                        put_three_rows(links, t, z, (mu * 3 + a) * 3 + b, value)
+    source_copy.wait()
+    psi[...] = source[...].astype(F32)
     faces_part(psi, links, position(), *sent)
 
 
@@ -323,8 +350,8 @@
             for chiral in range(2):
                 for i in range(6):
                     for j in range(6):
-                        row = ((chiral * 6 + i) * 6 + j) * 2
-                        rows[t, z, pl.ds(row, 2), :] = clover[t, z, chiral, i, j].astype(F32)
+                        value = clover[t, z, chiral, i, j].astype(F32)
+                        put_three_rows(rows, t, z, (chiral * 6 + i) * 6 + j, value)
 
 
 def local_kernel(psi, links, clover, out):
@@ -464,8 +491,8 @@
     z_face = jax.ShapeDtypeStruct((slices, 2, 2, 3, columns, sites), BF16)
     t_face = jax.ShapeDtypeStruct((layers, 2, 2, 3, columns, sites), BF16)
     faces = (z_face, z_face, t_face, t_face)
-    link_rows = jax.ShapeDtypeStruct((slices, layers, 72, sites), F32)
-    clover_rows = jax.ShapeDtypeStruct((slices, layers, 144, sites), F32)
+    link_rows = jax.ShapeDtypeStruct((slices, layers, 108, sites), F32)
+    clover_rows = jax.ShapeDtypeStruct((slices, layers, 216, sites), F32)
     row_count = slices * 2 * eigen_count // 128
 
     def swapped(value, axis, offset):
@@ -473,14 +500,27 @@
         pairs = [(i % count, (i + 1) % count) for i in range(offset, count + offset, 2)]
         return lax.ppermute(value, axis, pairs + [(b, a) for a, b in pairs])
 
-    def exchanged(z_inner, z_outer, t_inner, t_outer):
-        z_far = swapped(z_outer, "space", 1)
-        t_far = swapped(t_outer, "tm", 1)
-        return swapped(z_inner, "space", 0), z_far, swapped(t_inner, "tm", 0), t_far
-
+    def exchanged(z_outer, z_inner, t_outer, t_inner):
+        return (
+            swapped(z_outer, "space", 1),
+            swapped(z_inner, "space", 0),
+            swapped(t_outer, "tm", 1),
+            swapped(t_inner, "tm", 0),
+        )
+
+    gauge = jnp.transpose(gauge_links, (0, 1, 2, 4, 5, 3, 6))
     psi, links, *sent = call(
-        entry_kernel, 2, (spinor_type, link_rows) + faces, name="entry"
-    )(source, jnp.transpose(gauge_links, (0, 1, 2, 4, 5, 3, 6)))
+        entry_kernel,
+        2,
+        (spinor_type, link_rows) + faces,
+        scratch=(
+            pltpu.VMEM(source.shape, BF16),
+            pltpu.VMEM(gauge.shape, BF16),
+            pltpu.SemaphoreType.DMA((2,)),
+        ),
+        far=(0, 1),
+        name="entry",
+    )(in_far(source), in_far(gauge))
     got = exchanged(*sent)
     clover_f32 = call(clover_kernel, 1, clover_rows, name="clover_rows")(
         jnp.transpose(clover, (0, 1, 2, 4, 5, 3, 6))

time: 124 us -> 115 us (0.927)
  waiting for transfers between devices: 10.2 us -> 0.58 us
  blocking collectives: 31.8 us -> 33.8 us
  local copies, waits for them, and re-layouts: 2.8 us -> 0.92 us
    ppermute x16, waiting for transfers between devices: 10.2 us -> 0.58 us  [swapped(): return lax.ppermute(value, axis, pairs + [(b, a) for a, b in pairs])]
    all_to_all x1, blocking collectives: 16 us -> 18 us  [on_device(): shares = lax.all_to_all(partial_sums, 'space', 0, 0, tiled=True)]
    unnamed x10 -> x6, local copies, waits for them, and re-layouts: 2.8 us -> 0.92 us
    pallas_call x4, Pallas kernels: 8.93 us -> 7.62 us  [local(): call(local_kernel, 3, spinor_type, flops=1 << 26, name='local')]
  transfers between devices with their start and end apart: 16 -> 16, of which waited for: 3 -> 1; matrix products, arithmetic and copies ran while one was open for 0% -> 0% of each run, Pallas kernels for 7% -> 7%
where the time goes in v3:
time: 115 us; the launch traced here: 113 us
  starting transfers between devices  63.8 us (55%)
  blocking collectives  33.8 us (29%)
  Pallas kernels  14 us (12%)
    ppermute x16, starting transfers between devices, swapped(): return lax.ppermute(value, axis, pairs + [(b, a) for a, b in pairs])  63.8 us
    all_to_all x1, blocking collectives, on_device(): shares = lax.all_to_all(partial_sums, 'space', 0, 0, tiled=True)  18 us
    all_to_all x1, blocking collectives, on_device(): mixed = lax.all_to_all(mixed, 'space', 0, 0, tiled=True)  15.8 us
    pallas_call x4, Pallas kernels, local(): call(local_kernel, 3, spinor_type, flops=1 << 26, name='local')  7.62 us
  transfers between devices with their start and end apart: 16, of which 1 were waited for; matrix products, arithmetic and copies ran while one was open for 0% of the time, Pallas kernels for 7%

profile of v3, /device:TPU:1, one launch (start us, length us, event | category | flops | bytes accessed | tf_op | source)
XLA Modules:
  0.0 113.4 jit_solution(15891339266760033925)
XLA Ops:
  0.0 1.3 %entry.1 = (f32[2,2,4,2,3,16,128]{6,5,4,3,2,1,0:T(8,128)S(1)}, f32[2,2,108,128]{3,2,1,0:T(8,128)S(1)}, bf16[2,2,2,3,16,128]{5,4,3,2,1,0:T(8,128)(2,1)S(1)}, bf16...) custom-call(bf16[2,2,4,2,3,16,128]{6,5,4,3,2,1,0:T(8,128)(2,1)} %sou, ...), custom_call_target="tpu_custom_call" | custom-call | flops 4194304 | bytes 2097152 | tf_op jit(solution)/shard_map/entry/pallas_call | solution.py:512
  1.3 9.9 %collective-permute-start = (bf16[2,2,2,3,16,128]{5,4,3,2,1,0:T(8,128)(2,1)S(1)}, bf16[2,2,2,3,16,128]{5,4,3,2,1,0:T(8,128)(2,1)S(1)}, u32[]{:S(2)}, u32[]{:S(2)}) collective-permute-start(bf16[2,2,2,3,16,128]{5,4,3,2,1,0:T(8,128)(2,1)S(1)} %get-tuple-element.28), channel_id=1, source_target_pairs={{8,16},{24,32},{40,48},{56,64},{72,80},{88,96},{104,112},{120,128}... | collective-permute-start | bytes 294920 | tf_op jit(solution)/shard_map/ppermute | solution.py:501
  11.3 1.9 %collective-permute-start.1 = (bf16[2,2,2,3,16,128]{5,4,3,2,1,0:T(8,128)(2,1)S(1)}, bf16[2,2,2,3,16,128]{5,4,3,2,1,0:T(8,128)(2,1)S(1)}, u32[]{:S(2)}, u32[]{:S(2)}) collective-permute-start(bf16[2,2,2,3,16,128]{5,4,3,2,1,0:T(8,128)(2,1)S(1)} %get-tuple-element.29), channel_id=1, source_target_pairs={{0,8},{16,24},{32,40},{48,56},{64,72},{80,88},{96,104},{112,120},{... | collective-permute-start | bytes 294920 | tf_op jit(solution)/shard_map/ppermute | solution.py:501
  13.2 6.6 %collective-permute-start.2 = (bf16[2,2,2,3,16,128]{5,4,3,2,1,0:T(8,128)(2,1)S(1)}, bf16[2,2,2,3,16,128]{5,4,3,2,1,0:T(8,128)(2,1)S(1)}, u32[]{:S(2)}, u32[]{:S(2)}) collective-permute-start(bf16[2,2,2,3,16,128]{5,4,3,2,1,0:T(8,128)(2,1)S(1)} %get-tuple-element.30), channel_id=1, source_target_pairs={{1,2},{3,4},{5,6},{7,0},{2,1},{4,3},{6,5},{0,7},{9,10},{11,12},{13... | collective-permute-start | bytes 294920 | tf_op jit(solution)/shard_map/ppermute | solution.py:501
  19.8 5.4 %collective-permute-start.3 = (bf16[2,2,2,3,16,128]{5,4,3,2,1,0:T(8,128)(2,1)S(1)}, bf16[2,2,2,3,16,128]{5,4,3,2,1,0:T(8,128)(2,1)S(1)}, u32[]{:S(2)}, u32[]{:S(2)}) collective-permute-start(bf16[2,2,2,3,16,128]{5,4,3,2,1,0:T(8,128)(2,1)S(1)} %get-tuple-element.31), channel_id=1, source_target_pairs={{0,1},{2,3},{4,5},{6,7},{1,0},{3,2},{5,4},{7,6},{8,9},{10,11},{12,... | collective-permute-start | bytes 294920 | tf_op jit(solution)/shard_map/ppermute | solution.py:501
  25.3 0.9 copy-done.2
  26.2 0.2 clover_rows.1.clover
  26.4 1.9 %local.4.acc = f32[2,2,4,2,3,16,128]{6,5,4,3,2,1,0:T(8,128)S(1)} custom-call(f32[2,2,4,2,3,16,128]{6,5,4,3,2,1,0:T(8,128)S(1)} %get-tuple-element.26.psi, f32[2,2,108,128]{3,2,1,0:T(8,128)S(1)} %get-tuple-element.27.links, f32[2,2,216,128]{3,2,1,0:T(8,128)S(1)} %clover_rows.1.clover), custom_call_target="tpu_custom_call" | custom-call | flops 67108864 | bytes 2097152 | tf_op jit(solution)/shard_map/local/pallas_call | solution.py:530
  28.4 0.5 middle.2
  28.9 4.0 %collective-permute-start.4 = (bf16[2,2,2,3,16,128]{5,4,3,2,1,0:T(8,128)(2,1)S(1)}, bf16[2,2,2,3,16,128]{5,4,3,2,1,0:T(8,128)(2,1)S(1)}, u32[]{:S(2)}, u32[]{:S(2)}) collective-permute-start(bf16[2,2,2,3,16,128]{5,4,3,2,1,0:T(8,128)(2,1)S(1)} %get-tuple-element.33), channel_id=1, source_target_pairs={{8,16},{24,32},{40,48},{56,64},{72,80},{88,96},{104,112},{120,128}... | collective-permute-start | bytes 294920 | tf_op jit(solution)/shard_map/ppermute | solution.py:501
  32.9 1.9 %collective-permute-start.5 = (bf16[2,2,2,3,16,128]{5,4,3,2,1,0:T(8,128)(2,1)S(1)}, bf16[2,2,2,3,16,128]{5,4,3,2,1,0:T(8,128)(2,1)S(1)}, u32[]{:S(2)}, u32[]{:S(2)}) collective-permute-start(bf16[2,2,2,3,16,128]{5,4,3,2,1,0:T(8,128)(2,1)S(1)} %get-tuple-element.34), channel_id=1, source_target_pairs={{0,8},{16,24},{32,40},{48,56},{64,72},{80,88},{96,104},{112,120},{... | collective-permute-start | bytes 294920 | tf_op jit(solution)/shard_map/ppermute | solution.py:501
  34.8 3.6 %collective-permute-start.6 = (bf16[2,2,2,3,16,128]{5,4,3,2,1,0:T(8,128)(2,1)S(1)}, bf16[2,2,2,3,16,128]{5,4,3,2,1,0:T(8,128)(2,1)S(1)}, u32[]{:S(2)}, u32[]{:S(2)}) collective-permute-start(bf16[2,2,2,3,16,128]{5,4,3,2,1,0:T(8,128)(2,1)S(1)} %get-tuple-element.35), channel_id=1, source_target_pairs={{1,2},{3,4},{5,6},{7,0},{2,1},{4,3},{6,5},{0,7},{9,10},{11,12},{13... | collective-permute-start | bytes 294920 | tf_op jit(solution)/shard_map/ppermute | solution.py:501
  38.4 1.9 %collective-permute-start.7 = (bf16[2,2,2,3,16,128]{5,4,3,2,1,0:T(8,128)(2,1)S(1)}, bf16[2,2,2,3,16,128]{5,4,3,2,1,0:T(8,128)(2,1)S(1)}, u32[]{:S(2)}, u32[]{:S(2)}) collective-permute-start(bf16[2,2,2,3,16,128]{5,4,3,2,1,0:T(8,128)(2,1)S(1)} %get-tuple-element.36), channel_id=1, source_target_pairs={{0,1},{2,3},{4,5},{6,7},{1,0},{3,2},{5,4},{7,6},{8,9},{10,11},{12,... | collective-permute-start | bytes 294920 | tf_op jit(solution)/shard_map/ppermute | solution.py:501
  40.3 1.9 %local.5.acc = f32[2,2,4,2,3,16,128]{6,5,4,3,2,1,0:T(8,128)S(1)} custom-call(f32[2,2,4,2,3,16,128]{6,5,4,3,2,1,0:T(8,128)S(1)} %get-tuple-element.32.psi, f32[2,2,108,128]{3,2,1,0:T(8,128)S(1)} %get-tuple-element.27.links, f32[2,2,216,128]{3,2,1,0:T(8,128)S(1)} %clover_rows.1.clover), custom_call_target="tpu_custom_call" | custom-call | flops 67108864 | bytes 2097152 | tf_op jit(solution)/shard_map/local/pallas_call | solution.py:530
  42.3 0.5 collective-permute-done.6.refs_2_
  42.8 1.0 coefficients.1
  43.8 18.0 %all_to_all.10.shares = f32[64,8,128]{2,1,0:T(8,128)S(1)} all-to-all(f32[64,8,128]{2,1,0:T(8,128)S(1)} %coefficients.1), channel_id=1, replica_groups=mesh['space'=64,'tm'=8] {'space'}, dimensions={0} | all-to-all | bytes 524288 | tf_op jit(solution)/shard_map/all_to_all | solution.py:552
  61.8 0.7 mix.1
  62.5 15.8 %all_to_all.11.mixed = bf16[64,8,128]{2,1,0:T(8,128)(2,1)S(1)} all-to-all(bf16[64,8,128]{2,1,0:T(8,128)(2,1)S(1)} %mix.1), channel_id=1, replica_groups=mesh['space'=64,'tm'=8] {'space'}, dimensions={0} | all-to-all | bytes 262144 | tf_op jit(solution)/shard_map/all_to_all | solution.py:559
  78.3 1.1 expand.1
  79.4 3.6 %collective-permute-start.8 = (bf16[2,2,2,3,16,128]{5,4,3,2,1,0:T(8,128)(2,1)S(1)}, bf16[2,2,2,3,16,128]{5,4,3,2,1,0:T(8,128)(2,1)S(1)}, u32[]{:S(2)}, u32[]{:S(2)}) collective-permute-start(bf16[2,2,2,3,16,128]{5,4,3,2,1,0:T(8,128)(2,1)S(1)} %get-tuple-element.38), channel_id=1, source_target_pairs={{8,16},{24,32},{40,48},{56,64},{72,80},{88,96},{104,112},{120,128}... | collective-permute-start | bytes 294920 | tf_op jit(solution)/shard_map/ppermute | solution.py:501
  83.0 1.9 %collective-permute-start.9 = (bf16[2,2,2,3,16,128]{5,4,3,2,1,0:T(8,128)(2,1)S(1)}, bf16[2,2,2,3,16,128]{5,4,3,2,1,0:T(8,128)(2,1)S(1)}, u32[]{:S(2)}, u32[]{:S(2)}) collective-permute-start(bf16[2,2,2,3,16,128]{5,4,3,2,1,0:T(8,128)(2,1)S(1)} %get-tuple-element.39), channel_id=1, source_target_pairs={{0,8},{16,24},{32,40},{48,56},{64,72},{80,88},{96,104},{112,120},{... | collective-permute-start | bytes 294920 | tf_op jit(solution)/shard_map/ppermute | solution.py:501
  85.0 6.5 %collective-permute-start.10 = (bf16[2,2,2,3,16,128]{5,4,3,2,1,0:T(8,128)(2,1)S(1)}, bf16[2,2,2,3,16,128]{5,4,3,2,1,0:T(8,128)(2,1)S(1)}, u32[]{:S(2)}, u32[]{:S(2)}) collective-permute-start(bf16[2,2,2,3,16,128]{5,4,3,2,1,0:T(8,128)(2,1)S(1)} %get-tuple-element.40), channel_id=1, source_target_pairs={{1,2},{3,4},{5,6},{7,0},{2,1},{4,3},{6,5},{0,7},{9,10},{11,12},{13... | collective-permute-start | bytes 294920 | tf_op jit(solution)/shard_map/ppermute | solution.py:501
  91.5 1.9 %collective-permute-start.11 = (bf16[2,2,2,3,16,128]{5,4,3,2,1,0:T(8,128)(2,1)S(1)}, bf16[2,2,2,3,16,128]{5,4,3,2,1,0:T(8,128)(2,1)S(1)}, u32[]{:S(2)}, u32[]{:S(2)}) collective-permute-start(bf16[2,2,2,3,16,128]{5,4,3,2,1,0:T(8,128)(2,1)S(1)} %get-tuple-element.41), channel_id=1, source_target_pairs={{0,1},{2,3},{4,5},{6,7},{1,0},{3,2},{5,4},{7,6},{8,9},{10,11},{12,... | collective-permute-start | bytes 294920 | tf_op jit(solution)/shard_map/ppermute | solution.py:501
  93.4 1.9 %local.6.acc = f32[2,2,4,2,3,16,128]{6,5,4,3,2,1,0:T(8,128)S(1)} custom-call(f32[2,2,4,2,3,16,128]{6,5,4,3,2,1,0:T(8,128)S(1)} %get-tuple-element.37.psi, f32[2,2,108,128]{3,2,1,0:T(8,128)S(1)} %get-tuple-element.27.links, f32[2,2,216,128]{3,2,1,0:T(8,128)S(1)} %clover_rows.1.clover), custom_call_target="tpu_custom_call" | custom-call | flops 67108864 | bytes 2097152 | tf_op jit(solution)/shard_map/local/pallas_call | solution.py:530
  95.4 0.5 middle.3
  95.9 6.2 %collective-permute-start.12 = (bf16[2,2,2,3,16,128]{5,4,3,2,1,0:T(8,128)(2,1)S(1)}, bf16[2,2,2,3,16,128]{5,4,3,2,1,0:T(8,128)(2,1)S(1)}, u32[]{:S(2)}, u32[]{:S(2)}) collective-permute-start(bf16[2,2,2,3,16,128]{5,4,3,2,1,0:T(8,128)(2,1)S(1)} %get-tuple-element.43), channel_id=1, source_target_pairs={{8,16},{24,32},{40,48},{56,64},{72,80},{88,96},{104,112},{120,128}... | collective-permute-start | bytes 294920 | tf_op jit(solution)/shard_map/ppermute | solution.py:501
  102.1 1.9 %collective-permute-start.13 = (bf16[2,2,2,3,16,128]{5,4,3,2,1,0:T(8,128)(2,1)S(1)}, bf16[2,2,2,3,16,128]{5,4,3,2,1,0:T(8,128)(2,1)S(1)}, u32[]{:S(2)}, u32[]{:S(2)}) collective-permute-start(bf16[2,2,2,3,16,128]{5,4,3,2,1,0:T(8,128)(2,1)S(1)} %get-tuple-element.44), channel_id=1, source_target_pairs={{0,8},{16,24},{32,40},{48,56},{64,72},{80,88},{96,104},{112,120},{... | collective-permute-start | bytes 294920 | tf_op jit(solution)/shard_map/ppermute | solution.py:501
  104.0 4.3 %collective-permute-start.14 = (bf16[2,2,2,3,16,128]{5,4,3,2,1,0:T(8,128)(2,1)S(1)}, bf16[2,2,2,3,16,128]{5,4,3,2,1,0:T(8,128)(2,1)S(1)}, u32[]{:S(2)}, u32[]{:S(2)}) collective-permute-start(bf16[2,2,2,3,16,128]{5,4,3,2,1,0:T(8,128)(2,1)S(1)} %get-tuple-element.45), channel_id=1, source_target_pairs={{1,2},{3,4},{5,6},{7,0},{2,1},{4,3},{6,5},{0,7},{9,10},{11,12},{13... | collective-permute-start | bytes 294920 | tf_op jit(solution)/shard_map/ppermute | solution.py:501
  108.3 2.1 %collective-permute-start.15 = (bf16[2,2,2,3,16,128]{5,4,3,2,1,0:T(8,128)(2,1)S(1)}, bf16[2,2,2,3,16,128]{5,4,3,2,1,0:T(8,128)(2,1)S(1)}, u32[]{:S(2)}, u32[]{:S(2)}) collective-permute-start(bf16[2,2,2,3,16,128]{5,4,3,2,1,0:T(8,128)(2,1)S(1)} %get-tuple-element.46), channel_id=1, source_target_pairs={{0,1},{2,3},{4,5},{6,7},{1,0},{3,2},{5,4},{7,6},{8,9},{10,11},{12,... | collective-permute-start | bytes 294920 | tf_op jit(solution)/shard_map/ppermute | solution.py:501
  110.3 1.9 %local.7.acc = f32[2,2,4,2,3,16,128]{6,5,4,3,2,1,0:T(8,128)S(1)} custom-call(f32[2,2,4,2,3,16,128]{6,5,4,3,2,1,0:T(8,128)S(1)} %get-tuple-element.42.psi, f32[2,2,108,128]{3,2,1,0:T(8,128)S(1)} %get-tuple-element.27.links, f32[2,2,216,128]{3,2,1,0:T(8,128)S(1)} %clover_rows.1.clover), custom_call_target="tpu_custom_call" | custom-call | flops 67108864 | bytes 2097152 | tf_op jit(solution)/shard_map/local/pallas_call | solution.py:530
  112.3 1.1 last.1
  (20 shorter events, 0.1 us)
Async XLA Ops:
  1.3 27.0 %collective-permute-start = (bf16[2,2,2,3,16,128]{5,4,3,2,1,0:T(8,128)(2,1)S(1)}, bf16[2,2,2,3,16,128]{5,4,3,2,1,0:T(8,128)(2,1)S(1)}, u32[]{:S(2)}, u32[]{:S(2)}) collective-permute-start(bf16[2,2,2,3,16,128]{5,4,3,2,1,0:T(8,128)(2,1)S(1)} %get-tuple-element.28), channel_id=1, source_target_pairs={{8,16},{24,32},{40,48},{56,64},{72,80},{88,96},{104,112},{120,128}... | collective-permute-start | bytes 294920 | tf_op jit(solution)/shard_map/ppermute | solution.py:501
  11.3 17.1 %collective-permute-start.1 = (bf16[2,2,2,3,16,128]{5,4,3,2,1,0:T(8,128)(2,1)S(1)}, bf16[2,2,2,3,16,128]{5,4,3,2,1,0:T(8,128)(2,1)S(1)}, u32[]{:S(2)}, u32[]{:S(2)}) collective-permute-start(bf16[2,2,2,3,16,128]{5,4,3,2,1,0:T(8,128)(2,1)S(1)} %get-tuple-element.29), channel_id=1, source_target_pairs={{0,8},{16,24},{32,40},{48,56},{64,72},{80,88},{96,104},{112,120},{... | collective-permute-start | bytes 294920 | tf_op jit(solution)/shard_map/ppermute | solution.py:501
  13.2 15.2 %collective-permute-start.2 = (bf16[2,2,2,3,16,128]{5,4,3,2,1,0:T(8,128)(2,1)S(1)}, bf16[2,2,2,3,16,128]{5,4,3,2,1,0:T(8,128)(2,1)S(1)}, u32[]{:S(2)}, u32[]{:S(2)}) collective-permute-start(bf16[2,2,2,3,16,128]{5,4,3,2,1,0:T(8,128)(2,1)S(1)} %get-tuple-element.30), channel_id=1, source_target_pairs={{1,2},{3,4},{5,6},{7,0},{2,1},{4,3},{6,5},{0,7},{9,10},{11,12},{13... | collective-permute-start | bytes 294920 | tf_op jit(solution)/shard_map/ppermute | solution.py:501
  19.8 8.5 %collective-permute-start.3 = (bf16[2,2,2,3,16,128]{5,4,3,2,1,0:T(8,128)(2,1)S(1)}, bf16[2,2,2,3,16,128]{5,4,3,2,1,0:T(8,128)(2,1)S(1)}, u32[]{:S(2)}, u32[]{:S(2)}) collective-permute-start(bf16[2,2,2,3,16,128]{5,4,3,2,1,0:T(8,128)(2,1)S(1)} %get-tuple-element.31), channel_id=1, source_target_pairs={{0,1},{2,3},{4,5},{6,7},{1,0},{3,2},{5,4},{7,6},{8,9},{10,11},{12,... | collective-permute-start | bytes 294920 | tf_op jit(solution)/shard_map/ppermute | solution.py:501
  25.3 0.9 copy-start.2
  28.3 14.5 %copy-start = (bf16[2,2,2,3,256,128]{5,4,3,2,1,0:T(8,128)(2,1)S(1)}, bf16[2,2,2,3,256,128]{5,4,3,2,1,0:T(8,128)(2,1)}, u32[]{:S(2)}) copy-start(bf16[2,2,2,3,256,128]{5,4,3,2,1,0:T(8,128)(2,1)} %vectors.1) | copy-start | bytes 4718596
  28.9 13.4 %collective-permute-start.4 = (bf16[2,2,2,3,16,128]{5,4,3,2,1,0:T(8,128)(2,1)S(1)}, bf16[2,2,2,3,16,128]{5,4,3,2,1,0:T(8,128)(2,1)S(1)}, u32[]{:S(2)}, u32[]{:S(2)}) collective-permute-start(bf16[2,2,2,3,16,128]{5,4,3,2,1,0:T(8,128)(2,1)S(1)} %get-tuple-element.33), channel_id=1, source_target_pairs={{8,16},{24,32},{40,48},{56,64},{72,80},{88,96},{104,112},{120,128}... | collective-permute-start | bytes 294920 | tf_op jit(solution)/shard_map/ppermute | solution.py:501
  32.9 9.4 %collective-permute-start.5 = (bf16[2,2,2,3,16,128]{5,4,3,2,1,0:T(8,128)(2,1)S(1)}, bf16[2,2,2,3,16,128]{5,4,3,2,1,0:T(8,128)(2,1)S(1)}, u32[]{:S(2)}, u32[]{:S(2)}) collective-permute-start(bf16[2,2,2,3,16,128]{5,4,3,2,1,0:T(8,128)(2,1)S(1)} %get-tuple-element.34), channel_id=1, source_target_pairs={{0,8},{16,24},{32,40},{48,56},{64,72},{80,88},{96,104},{112,120},{... | collective-permute-start | bytes 294920 | tf_op jit(solution)/shard_map/ppermute | solution.py:501
  34.8 8.0 %collective-permute-start.6 = (bf16[2,2,2,3,16,128]{5,4,3,2,1,0:T(8,128)(2,1)S(1)}, bf16[2,2,2,3,16,128]{5,4,3,2,1,0:T(8,128)(2,1)S(1)}, u32[]{:S(2)}, u32[]{:S(2)}) collective-permute-start(bf16[2,2,2,3,16,128]{5,4,3,2,1,0:T(8,128)(2,1)S(1)} %get-tuple-element.35), channel_id=1, source_target_pairs={{1,2},{3,4},{5,6},{7,0},{2,1},{4,3},{6,5},{0,7},{9,10},{11,12},{13... | collective-permute-start | bytes 294920 | tf_op jit(solution)/shard_map/ppermute | solution.py:501
  38.4 4.4 %collective-permute-start.7 = (bf16[2,2,2,3,16,128]{5,4,3,2,1,0:T(8,128)(2,1)S(1)}, bf16[2,2,2,3,16,128]{5,4,3,2,1,0:T(8,128)(2,1)S(1)}, u32[]{:S(2)}, u32[]{:S(2)}) collective-permute-start(bf16[2,2,2,3,16,128]{5,4,3,2,1,0:T(8,128)(2,1)S(1)} %get-tuple-element.36), channel_id=1, source_target_pairs={{0,1},{2,3},{4,5},{6,7},{1,0},{3,2},{5,4},{7,6},{8,9},{10,11},{12,... | collective-permute-start | bytes 294920 | tf_op jit(solution)/shard_map/ppermute | solution.py:501
  42.2 19.6 %copy-start.1 = (bf16[2,2,256,256]{3,2,1,0:T(8,128)(2,1)S(1)}, bf16[2,2,256,256]{3,2,1,0:T(8,128)(2,1)}, u32[]{:S(2)}) copy-start(bf16[2,2,256,256]{3,2,1,0:T(8,128)(2,1)} %elemental.1) | copy-start | bytes 1572868
  79.4 15.9 %collective-permute-start.8 = (bf16[2,2,2,3,16,128]{5,4,3,2,1,0:T(8,128)(2,1)S(1)}, bf16[2,2,2,3,16,128]{5,4,3,2,1,0:T(8,128)(2,1)S(1)}, u32[]{:S(2)}, u32[]{:S(2)}) collective-permute-start(bf16[2,2,2,3,16,128]{5,4,3,2,1,0:T(8,128)(2,1)S(1)} %get-tuple-element.38), channel_id=1, source_target_pairs={{8,16},{24,32},{40,48},{56,64},{72,80},{88,96},{104,112},{120,128}... | collective-permute-start | bytes 294920 | tf_op jit(solution)/shard_map/ppermute | solution.py:501
  83.0 12.3 %collective-permute-start.9 = (bf16[2,2,2,3,16,128]{5,4,3,2,1,0:T(8,128)(2,1)S(1)}, bf16[2,2,2,3,16,128]{5,4,3,2,1,0:T(8,128)(2,1)S(1)}, u32[]{:S(2)}, u32[]{:S(2)}) collective-permute-start(bf16[2,2,2,3,16,128]{5,4,3,2,1,0:T(8,128)(2,1)S(1)} %get-tuple-element.39), channel_id=1, source_target_pairs={{0,8},{16,24},{32,40},{48,56},{64,72},{80,88},{96,104},{112,120},{... | collective-permute-start | bytes 294920 | tf_op jit(solution)/shard_map/ppermute | solution.py:501
  85.0 10.4 %collective-permute-start.10 = (bf16[2,2,2,3,16,128]{5,4,3,2,1,0:T(8,128)(2,1)S(1)}, bf16[2,2,2,3,16,128]{5,4,3,2,1,0:T(8,128)(2,1)S(1)}, u32[]{:S(2)}, u32[]{:S(2)}) collective-permute-start(bf16[2,2,2,3,16,128]{5,4,3,2,1,0:T(8,128)(2,1)S(1)} %get-tuple-element.40), channel_id=1, source_target_pairs={{1,2},{3,4},{5,6},{7,0},{2,1},{4,3},{6,5},{0,7},{9,10},{11,12},{13... | collective-permute-start | bytes 294920 | tf_op jit(solution)/shard_map/ppermute | solution.py:501
  91.5 3.9 %collective-permute-start.11 = (bf16[2,2,2,3,16,128]{5,4,3,2,1,0:T(8,128)(2,1)S(1)}, bf16[2,2,2,3,16,128]{5,4,3,2,1,0:T(8,128)(2,1)S(1)}, u32[]{:S(2)}, u32[]{:S(2)}) collective-permute-start(bf16[2,2,2,3,16,128]{5,4,3,2,1,0:T(8,128)(2,1)S(1)} %get-tuple-element.41), channel_id=1, source_target_pairs={{0,1},{2,3},{4,5},{6,7},{1,0},{3,2},{5,4},{7,6},{8,9},{10,11},{12,... | collective-permute-start | bytes 294920 | tf_op jit(solution)/shard_map/ppermute | solution.py:501
  95.9 16.4 %collective-permute-start.12 = (bf16[2,2,2,3,16,128]{5,4,3,2,1,0:T(8,128)(2,1)S(1)}, bf16[2,2,2,3,16,128]{5,4,3,2,1,0:T(8,128)(2,1)S(1)}, u32[]{:S(2)}, u32[]{:S(2)}) collective-permute-start(bf16[2,2,2,3,16,128]{5,4,3,2,1,0:T(8,128)(2,1)S(1)} %get-tuple-element.43), channel_id=1, source_target_pairs={{8,16},{24,32},{40,48},{56,64},{72,80},{88,96},{104,112},{120,128}... | collective-permute-start | bytes 294920 | tf_op jit(solution)/shard_map/ppermute | solution.py:501
  102.1 10.2 %collective-permute-start.13 = (bf16[2,2,2,3,16,128]{5,4,3,2,1,0:T(8,128)(2,1)S(1)}, bf16[2,2,2,3,16,128]{5,4,3,2,1,0:T(8,128)(2,1)S(1)}, u32[]{:S(2)}, u32[]{:S(2)}) collective-permute-start(bf16[2,2,2,3,16,128]{5,4,3,2,1,0:T(8,128)(2,1)S(1)} %get-tuple-element.44), channel_id=1, source_target_pairs={{0,8},{16,24},{32,40},{48,56},{64,72},{80,88},{96,104},{112,120},{... | collective-permute-start | bytes 294920 | tf_op jit(solution)/shard_map/ppermute | solution.py:501
  104.0 8.3 %collective-permute-start.14 = (bf16[2,2,2,3,16,128]{5,4,3,2,1,0:T(8,128)(2,1)S(1)}, bf16[2,2,2,3,16,128]{5,4,3,2,1,0:T(8,128)(2,1)S(1)}, u32[]{:S(2)}, u32[]{:S(2)}) collective-permute-start(bf16[2,2,2,3,16,128]{5,4,3,2,1,0:T(8,128)(2,1)S(1)} %get-tuple-element.45), channel_id=1, source_target_pairs={{1,2},{3,4},{5,6},{7,0},{2,1},{4,3},{6,5},{0,7},{9,10},{11,12},{13... | collective-permute-start | bytes 294920 | tf_op jit(solution)/shard_map/ppermute | solution.py:501
  108.3 4.0 %collective-permute-start.15 = (bf16[2,2,2,3,16,128]{5,4,3,2,1,0:T(8,128)(2,1)S(1)}, bf16[2,2,2,3,16,128]{5,4,3,2,1,0:T(8,128)(2,1)S(1)}, u32[]{:S(2)}, u32[]{:S(2)}) collective-permute-start(bf16[2,2,2,3,16,128]{5,4,3,2,1,0:T(8,128)(2,1)S(1)} %get-tuple-element.46), channel_id=1, source_target_pairs={{0,1},{2,3},{4,5},{6,7},{1,0},{3,2},{5,4},{7,6},{8,9},{10,11},{12,... | collective-permute-start | bytes 294920 | tf_op jit(solution)/shard_map/ppermute | solution.py:501

commit v4 on v3

--- a/solution.py
+++ b/solution.py
@@ -222,7 +222,7 @@
     pl.when(jnp.logical_not(odd))(lambda: function(pair[1], pair[0]))
 
 
-def faces_part(psi, links, where, z_outer, z_inner, t_outer, t_inner):
+def faces_part(psi, links, where, t_outer, t_inner, z_outer, z_inner):
     by_parity(where[0], functools.partial(z_faces, psi, links), (z_inner, z_outer))
     by_parity(where[1], functools.partial(t_faces, psi, links), (t_inner, t_outer))
 
@@ -262,7 +262,7 @@
         out[t, z, key[0], key[1], key[2]] = total[key]
 
 
-def halo_part(acc, links, where, z_outer, z_inner, t_outer, t_inner, out):
+def halo_part(acc, links, where, t_outer, t_inner, z_outer, z_inner, out):
     by_parity(where[0], functools.partial(z_halo, acc, links, out), (z_inner, z_outer))
     by_parity(where[1], functools.partial(t_halo, links, where, out), (t_inner, t_outer))
 
@@ -323,12 +323,14 @@
     )
 
 
-def entry_kernel(source_far, gauge_far, psi, links, *refs):
-    sent, (source, gauge, arrived) = refs[:4], refs[4:]
+def entry_kernel(source_far, gauge_far, clover_far, psi, links, *refs):
+    sent, (clover, source, gauge, arrived) = refs[:4], refs[4:]
     gauge_copy = pltpu.make_async_copy(gauge_far, gauge, arrived.at[0])
     source_copy = pltpu.make_async_copy(source_far, source, arrived.at[1])
+    clover_copy = pltpu.make_async_copy(clover_far, clover, arrived.at[2])
     gauge_copy.start()
     source_copy.start()
+    clover_copy.start()
     gauge_copy.wait()
     slices, layers = source.shape[0], source.shape[1]
     for t in range(slices):
@@ -341,6 +343,7 @@
     source_copy.wait()
     psi[...] = source[...].astype(F32)
     faces_part(psi, links, position(), *sent)
+    clover_copy.wait()
 
 
 def clover_kernel(clover, rows):
@@ -490,7 +493,7 @@
     spinor_type = jax.ShapeDtypeStruct(source.shape, F32)
     z_face = jax.ShapeDtypeStruct((slices, 2, 2, 3, columns, sites), BF16)
     t_face = jax.ShapeDtypeStruct((layers, 2, 2, 3, columns, sites), BF16)
-    faces = (z_face, z_face, t_face, t_face)
+    faces = (t_face, t_face, z_face, z_face)
     link_rows = jax.ShapeDtypeStruct((slices, layers, 108, sites), F32)
     clover_rows = jax.ShapeDtypeStruct((slices, layers, 216, sites), F32)
     row_count = slices * 2 * eigen_count // 128
@@ -500,31 +503,31 @@
         pairs = [(i % count, (i + 1) % count) for i in range(offset, count + offset, 2)]
         return lax.ppermute(value, axis, pairs + [(b, a) for a, b in pairs])
 
-    def exchanged(z_outer, z_inner, t_outer, t_inner):
+    def exchanged(t_outer, t_inner, z_outer, z_inner):
         return (
+            swapped(t_outer, "tm", 1),
+            swapped(t_inner, "tm", 0),
             swapped(z_outer, "space", 1),
             swapped(z_inner, "space", 0),
-            swapped(t_outer, "tm", 1),
-            swapped(t_inner, "tm", 0),
         )
 
     gauge = jnp.transpose(gauge_links, (0, 1, 2, 4, 5, 3, 6))
-    psi, links, *sent = call(
+    clover = jnp.transpose(clover, (0, 1, 2, 4, 5, 3, 6))
+    clover_near = jax.ShapeDtypeStruct(clover.shape, BF16)
+    psi, links, *sent, clover = call(
         entry_kernel,
-        2,
-        (spinor_type, link_rows) + faces,
+        3,
+        (spinor_type, link_rows) + faces + (clover_near,),
         scratch=(
             pltpu.VMEM(source.shape, BF16),
             pltpu.VMEM(gauge.shape, BF16),
-            pltpu.SemaphoreType.DMA((2,)),
+            pltpu.SemaphoreType.DMA((3,)),
         ),
-        far=(0, 1),
+        far=(0, 1, 2),
         name="entry",
-    )(in_far(source), in_far(gauge))
+    )(in_far(source), in_far(gauge), in_far(clover))
     got = exchanged(*sent)
-    clover_f32 = call(clover_kernel, 1, clover_rows, name="clover_rows")(
-        jnp.transpose(clover, (0, 1, 2, 4, 5, 3, 6))
-    )
+    clover_f32 = call(clover_kernel, 1, clover_rows, name="clover_rows")(clover)
 
     def local(spinor):
         return call(local_kernel, 3, spinor_type, flops=1 << 26, name="local")(

time: 115 us -> 118 us (1.026)
  waiting for transfers between devices: 0.58 us -> 8.45 us
  blocking collectives: 33.8 us -> 30.8 us
    ppermute x16, waiting for transfers between devices: 0.58 us -> 8.45 us  [swapped(): return lax.ppermute(value, axis, pairs + [(b, a) for a, b in pairs])]
    all_to_all x1, blocking collectives: 18 us -> 16.2 us  [on_device(): shares = lax.all_to_all(partial_sums, 'space', 0, 0, tiled=True)]
  transfers between devices with their start and end apart: 16 -> 16, of which waited for: 1 -> 5; matrix products, arithmetic and copies ran while one was open for 0% -> 0% of each run, Pallas kernels for 7% -> 7%
where the time goes in v4:
time: 118 us; the launch traced here: 117 us
  starting transfers between devices  63.7 us (54%)
  blocking collectives  30.8 us (26%)
  Pallas kernels  13.9 us (12%)
  waiting for transfers between devices  8.45 us (7%)
    ppermute x16, starting transfers between devices, swapped(): return lax.ppermute(value, axis, pairs + [(b, a) for a, b in pairs])  63.7 us
    all_to_all x1, blocking collectives, on_device(): shares = lax.all_to_all(partial_sums, 'space', 0, 0, tiled=True)  16.2 us
    all_to_all x1, blocking collectives, on_device(): mixed = lax.all_to_all(mixed, 'space', 0, 0, tiled=True)  14.7 us
    ppermute x16, waiting for transfers between devices, swapped(): return lax.ppermute(value, axis, pairs + [(b, a) for a, b in pairs])  8.45 us
    pallas_call x4, Pallas kernels, local(): call(local_kernel, 3, spinor_type, flops=1 << 26, name='local')  7.62 us
  transfers between devices with their start and end apart: 16, of which 5 were waited for; matrix products, arithmetic and copies ran while one was open for 0% of the time, Pallas kernels for 7%

profile of v4, /device:TPU:1, one launch (start us, length us, event | category | flops | bytes accessed | tf_op | source)
XLA Modules:
  0.0 117.2 jit_solution(16272935395948056823)
XLA Ops:
  0.0 1.3 %entry.1 = (f32[2,2,4,2,3,16,128]{6,5,4,3,2,1,0:T(8,128)S(1)}, f32[2,2,108,128]{3,2,1,0:T(8,128)S(1)}, bf16[2,2,2,3,16,128]{5,4,3,2,1,0:T(8,128)(2,1)S(1)}, bf16...) custom-call(bf16[2,2,4,2,3,16,128]{6,5,4,3,2,1,0:T(8,128)(2,1)} %sou, ...), custom_call_target="tpu_custom_call" | custom-call | flops 4194304 | bytes 2097152 | tf_op jit(solution)/shard_map/entry/pallas_call | solution.py:517
  1.3 7.2 %collective-permute-start = (bf16[2,2,2,3,16,128]{5,4,3,2,1,0:T(8,128)(2,1)S(1)}, bf16[2,2,2,3,16,128]{5,4,3,2,1,0:T(8,128)(2,1)S(1)}, u32[]{:S(2)}, u32[]{:S(2)}) collective-permute-start(bf16[2,2,2,3,16,128]{5,4,3,2,1,0:T(8,128)(2,1)S(1)} %get-tuple-element.30), channel_id=1, source_target_pairs={{1,2},{3,4},{5,6},{7,0},{2,1},{4,3},{6,5},{0,7},{9,10},{11,12},{13... | collective-permute-start | bytes 294920 | tf_op jit(solution)/shard_map/ppermute | solution.py:504
  8.5 6.6 %collective-permute-start.1 = (bf16[2,2,2,3,16,128]{5,4,3,2,1,0:T(8,128)(2,1)S(1)}, bf16[2,2,2,3,16,128]{5,4,3,2,1,0:T(8,128)(2,1)S(1)}, u32[]{:S(2)}, u32[]{:S(2)}) collective-permute-start(bf16[2,2,2,3,16,128]{5,4,3,2,1,0:T(8,128)(2,1)S(1)} %get-tuple-element.31), channel_id=1, source_target_pairs={{0,1},{2,3},{4,5},{6,7},{1,0},{3,2},{5,4},{7,6},{8,9},{10,11},{12,... | collective-permute-start | bytes 294920 | tf_op jit(solution)/shard_map/ppermute | solution.py:504
  15.1 8.2 %collective-permute-start.2 = (bf16[2,2,2,3,16,128]{5,4,3,2,1,0:T(8,128)(2,1)S(1)}, bf16[2,2,2,3,16,128]{5,4,3,2,1,0:T(8,128)(2,1)S(1)}, u32[]{:S(2)}, u32[]{:S(2)}) collective-permute-start(bf16[2,2,2,3,16,128]{5,4,3,2,1,0:T(8,128)(2,1)S(1)} %get-tuple-element.32), channel_id=1, source_target_pairs={{8,16},{24,32},{40,48},{56,64},{72,80},{88,96},{104,112},{120,128}... | collective-permute-start | bytes 294920 | tf_op jit(solution)/shard_map/ppermute | solution.py:504
  23.3 1.9 %collective-permute-start.3 = (bf16[2,2,2,3,16,128]{5,4,3,2,1,0:T(8,128)(2,1)S(1)}, bf16[2,2,2,3,16,128]{5,4,3,2,1,0:T(8,128)(2,1)S(1)}, u32[]{:S(2)}, u32[]{:S(2)}) collective-permute-start(bf16[2,2,2,3,16,128]{5,4,3,2,1,0:T(8,128)(2,1)S(1)} %get-tuple-element.33), channel_id=1, source_target_pairs={{0,8},{16,24},{32,40},{48,56},{64,72},{80,88},{96,104},{112,120},{... | collective-permute-start | bytes 294920 | tf_op jit(solution)/shard_map/ppermute | solution.py:504
  25.5 1.9 %local.4.acc = f32[2,2,4,2,3,16,128]{6,5,4,3,2,1,0:T(8,128)S(1)} custom-call(f32[2,2,4,2,3,16,128]{6,5,4,3,2,1,0:T(8,128)S(1)} %get-tuple-element.27.psi, f32[2,2,108,128]{3,2,1,0:T(8,128)S(1)} %get-tuple-element.28.links, f32[2,2,216,128]{3,2,1,0:T(8,128)S(1)} %clover_rows.1.clover), custom_call_target="tpu_custom_call" | custom-call | flops 67108864 | bytes 2097152 | tf_op jit(solution)/shard_map/local/pallas_call | solution.py:533
  27.5 1.8 %collective-permute-done.3.refs_3_ = bf16[2,2,2,3,16,128]{5,4,3,2,1,0:T(8,128)(2,1)S(1)} collective-permute-done((bf16[2,2,2,3,16,128]{5,4,3,2,1,0:T(8,128)(2,1)S(1)}, bf16[2,2,2,3,16,128]{5,4,3,2,1,0:T(8,128)(2,1)S(1)}, u32[]{:S(2)}, u32[]{:S(2)}) %collective-permute-start.3) | collective-permute-done | bytes 98336 | tf_op jit(solution)/shard_map/ppermute | solution.py:504
  29.8 3.6 %collective-permute-start.4 = (bf16[2,2,2,3,16,128]{5,4,3,2,1,0:T(8,128)(2,1)S(1)}, bf16[2,2,2,3,16,128]{5,4,3,2,1,0:T(8,128)(2,1)S(1)}, u32[]{:S(2)}, u32[]{:S(2)}) collective-permute-start(bf16[2,2,2,3,16,128]{5,4,3,2,1,0:T(8,128)(2,1)S(1)} %get-tuple-element.35), channel_id=1, source_target_pairs={{1,2},{3,4},{5,6},{7,0},{2,1},{4,3},{6,5},{0,7},{9,10},{11,12},{13... | collective-permute-start | bytes 294920 | tf_op jit(solution)/shard_map/ppermute | solution.py:504
  33.3 1.9 %collective-permute-start.5 = (bf16[2,2,2,3,16,128]{5,4,3,2,1,0:T(8,128)(2,1)S(1)}, bf16[2,2,2,3,16,128]{5,4,3,2,1,0:T(8,128)(2,1)S(1)}, u32[]{:S(2)}, u32[]{:S(2)}) collective-permute-start(bf16[2,2,2,3,16,128]{5,4,3,2,1,0:T(8,128)(2,1)S(1)} %get-tuple-element.36), channel_id=1, source_target_pairs={{0,1},{2,3},{4,5},{6,7},{1,0},{3,2},{5,4},{7,6},{8,9},{10,11},{12,... | collective-permute-start | bytes 294920 | tf_op jit(solution)/shard_map/ppermute | solution.py:504
  35.3 4.0 %collective-permute-start.6 = (bf16[2,2,2,3,16,128]{5,4,3,2,1,0:T(8,128)(2,1)S(1)}, bf16[2,2,2,3,16,128]{5,4,3,2,1,0:T(8,128)(2,1)S(1)}, u32[]{:S(2)}, u32[]{:S(2)}) collective-permute-start(bf16[2,2,2,3,16,128]{5,4,3,2,1,0:T(8,128)(2,1)S(1)} %get-tuple-element.37), channel_id=1, source_target_pairs={{8,16},{24,32},{40,48},{56,64},{72,80},{88,96},{104,112},{120,128}... | collective-permute-start | bytes 294920 | tf_op jit(solution)/shard_map/ppermute | solution.py:504
  39.3 1.9 %collective-permute-start.7 = (bf16[2,2,2,3,16,128]{5,4,3,2,1,0:T(8,128)(2,1)S(1)}, bf16[2,2,2,3,16,128]{5,4,3,2,1,0:T(8,128)(2,1)S(1)}, u32[]{:S(2)}, u32[]{:S(2)}) collective-permute-start(bf16[2,2,2,3,16,128]{5,4,3,2,1,0:T(8,128)(2,1)S(1)} %get-tuple-element.38), channel_id=1, source_target_pairs={{0,8},{16,24},{32,40},{48,56},{64,72},{80,88},{96,104},{112,120},{... | collective-permute-start | bytes 294920 | tf_op jit(solution)/shard_map/ppermute | solution.py:504
  41.2 1.9 %local.5.acc = f32[2,2,4,2,3,16,128]{6,5,4,3,2,1,0:T(8,128)S(1)} custom-call(f32[2,2,4,2,3,16,128]{6,5,4,3,2,1,0:T(8,128)S(1)} %get-tuple-element.34.psi, f32[2,2,108,128]{3,2,1,0:T(8,128)S(1)} %get-tuple-element.28.links, f32[2,2,216,128]{3,2,1,0:T(8,128)S(1)} %clover_rows.1.clover), custom_call_target="tpu_custom_call" | custom-call | flops 67108864 | bytes 2097152 | tf_op jit(solution)/shard_map/local/pallas_call | solution.py:533
  43.2 2.1 %collective-permute-done.6.refs_2_ = bf16[2,2,2,3,16,128]{5,4,3,2,1,0:T(8,128)(2,1)S(1)} collective-permute-done((bf16[2,2,2,3,16,128]{5,4,3,2,1,0:T(8,128)(2,1)S(1)}, bf16[2,2,2,3,16,128]{5,4,3,2,1,0:T(8,128)(2,1)S(1)}, u32[]{:S(2)}, u32[]{:S(2)}) %collective-permute-start.6) | collective-permute-done | bytes 98336 | tf_op jit(solution)/shard_map/ppermute | solution.py:504
  45.2 1.0 coefficients.1
  46.2 16.2 %all_to_all.10.shares = f32[64,8,128]{2,1,0:T(8,128)S(1)} all-to-all(f32[64,8,128]{2,1,0:T(8,128)S(1)} %coefficients.1), channel_id=1, replica_groups=mesh['space'=64,'tm'=8] {'space'}, dimensions={0} | all-to-all | bytes 524288 | tf_op jit(solution)/shard_map/all_to_all | solution.py:555
  62.4 0.7 mix.1
  63.1 14.7 %all_to_all.11.mixed = bf16[64,8,128]{2,1,0:T(8,128)(2,1)S(1)} all-to-all(bf16[64,8,128]{2,1,0:T(8,128)(2,1)S(1)} %mix.1), channel_id=1, replica_groups=mesh['space'=64,'tm'=8] {'space'}, dimensions={0} | all-to-all | bytes 262144 | tf_op jit(solution)/shard_map/all_to_all | solution.py:562
  77.8 1.1 expand.1
  78.9 8.3 %collective-permute-start.8 = (bf16[2,2,2,3,16,128]{5,4,3,2,1,0:T(8,128)(2,1)S(1)}, bf16[2,2,2,3,16,128]{5,4,3,2,1,0:T(8,128)(2,1)S(1)}, u32[]{:S(2)}, u32[]{:S(2)}) collective-permute-start(bf16[2,2,2,3,16,128]{5,4,3,2,1,0:T(8,128)(2,1)S(1)} %get-tuple-element.40), channel_id=1, source_target_pairs={{1,2},{3,4},{5,6},{7,0},{2,1},{4,3},{6,5},{0,7},{9,10},{11,12},{13... | collective-permute-start | bytes 294920 | tf_op jit(solution)/shard_map/ppermute | solution.py:504
  87.2 1.9 %collective-permute-start.9 = (bf16[2,2,2,3,16,128]{5,4,3,2,1,0:T(8,128)(2,1)S(1)}, bf16[2,2,2,3,16,128]{5,4,3,2,1,0:T(8,128)(2,1)S(1)}, u32[]{:S(2)}, u32[]{:S(2)}) collective-permute-start(bf16[2,2,2,3,16,128]{5,4,3,2,1,0:T(8,128)(2,1)S(1)} %get-tuple-element.41), channel_id=1, source_target_pairs={{0,1},{2,3},{4,5},{6,7},{1,0},{3,2},{5,4},{7,6},{8,9},{10,11},{12,... | collective-permute-start | bytes 294920 | tf_op jit(solution)/shard_map/ppermute | solution.py:504
  89.1 3.4 %collective-permute-start.10 = (bf16[2,2,2,3,16,128]{5,4,3,2,1,0:T(8,128)(2,1)S(1)}, bf16[2,2,2,3,16,128]{5,4,3,2,1,0:T(8,128)(2,1)S(1)}, u32[]{:S(2)}, u32[]{:S(2)}) collective-permute-start(bf16[2,2,2,3,16,128]{5,4,3,2,1,0:T(8,128)(2,1)S(1)} %get-tuple-element.42), channel_id=1, source_target_pairs={{8,16},{24,32},{40,48},{56,64},{72,80},{88,96},{104,112},{120,128}... | collective-permute-start | bytes 294920 | tf_op jit(solution)/shard_map/ppermute | solution.py:504
  92.5 1.9 %collective-permute-start.11 = (bf16[2,2,2,3,16,128]{5,4,3,2,1,0:T(8,128)(2,1)S(1)}, bf16[2,2,2,3,16,128]{5,4,3,2,1,0:T(8,128)(2,1)S(1)}, u32[]{:S(2)}, u32[]{:S(2)}) collective-permute-start(bf16[2,2,2,3,16,128]{5,4,3,2,1,0:T(8,128)(2,1)S(1)} %get-tuple-element.43), channel_id=1, source_target_pairs={{0,8},{16,24},{32,40},{48,56},{64,72},{80,88},{96,104},{112,120},{... | collective-permute-start | bytes 294920 | tf_op jit(solution)/shard_map/ppermute | solution.py:504
  94.4 1.9 %local.6.acc = f32[2,2,4,2,3,16,128]{6,5,4,3,2,1,0:T(8,128)S(1)} custom-call(f32[2,2,4,2,3,16,128]{6,5,4,3,2,1,0:T(8,128)S(1)} %get-tuple-element.39.psi, f32[2,2,108,128]{3,2,1,0:T(8,128)S(1)} %get-tuple-element.28.links, f32[2,2,216,128]{3,2,1,0:T(8,128)S(1)} %clover_rows.1.clover), custom_call_target="tpu_custom_call" | custom-call | flops 67108864 | bytes 2097152 | tf_op jit(solution)/shard_map/local/pallas_call | solution.py:533
  96.3 2.7 %collective-permute-done.10.refs_2_ = bf16[2,2,2,3,16,128]{5,4,3,2,1,0:T(8,128)(2,1)S(1)} collective-permute-done((bf16[2,2,2,3,16,128]{5,4,3,2,1,0:T(8,128)(2,1)S(1)}, bf16[2,2,2,3,16,128]{5,4,3,2,1,0:T(8,128)(2,1)S(1)}, u32[]{:S(2)}, u32[]{:S(2)}) %collective-permute-start.10) | collective-permute-done | bytes 98336 | tf_op jit(solution)/shard_map/ppermute | solution.py:504
  99.5 3.5 %collective-permute-start.12 = (bf16[2,2,2,3,16,128]{5,4,3,2,1,0:T(8,128)(2,1)S(1)}, bf16[2,2,2,3,16,128]{5,4,3,2,1,0:T(8,128)(2,1)S(1)}, u32[]{:S(2)}, u32[]{:S(2)}) collective-permute-start(bf16[2,2,2,3,16,128]{5,4,3,2,1,0:T(8,128)(2,1)S(1)} %get-tuple-element.45), channel_id=1, source_target_pairs={{1,2},{3,4},{5,6},{7,0},{2,1},{4,3},{6,5},{0,7},{9,10},{11,12},{13... | collective-permute-start | bytes 294920 | tf_op jit(solution)/shard_map/ppermute | solution.py:504
  103.1 2.2 %collective-permute-start.13 = (bf16[2,2,2,3,16,128]{5,4,3,2,1,0:T(8,128)(2,1)S(1)}, bf16[2,2,2,3,16,128]{5,4,3,2,1,0:T(8,128)(2,1)S(1)}, u32[]{:S(2)}, u32[]{:S(2)}) collective-permute-start(bf16[2,2,2,3,16,128]{5,4,3,2,1,0:T(8,128)(2,1)S(1)} %get-tuple-element.46), channel_id=1, source_target_pairs={{0,1},{2,3},{4,5},{6,7},{1,0},{3,2},{5,4},{7,6},{8,9},{10,11},{12,... | collective-permute-start | bytes 294920 | tf_op jit(solution)/shard_map/ppermute | solution.py:504
  105.2 5.2 %collective-permute-start.14 = (bf16[2,2,2,3,16,128]{5,4,3,2,1,0:T(8,128)(2,1)S(1)}, bf16[2,2,2,3,16,128]{5,4,3,2,1,0:T(8,128)(2,1)S(1)}, u32[]{:S(2)}, u32[]{:S(2)}) collective-permute-start(bf16[2,2,2,3,16,128]{5,4,3,2,1,0:T(8,128)(2,1)S(1)} %get-tuple-element.47), channel_id=1, source_target_pairs={{8,16},{24,32},{40,48},{56,64},{72,80},{88,96},{104,112},{120,128}... | collective-permute-start | bytes 294920 | tf_op jit(solution)/shard_map/ppermute | solution.py:504
  110.5 1.9 %collective-permute-start.15 = (bf16[2,2,2,3,16,128]{5,4,3,2,1,0:T(8,128)(2,1)S(1)}, bf16[2,2,2,3,16,128]{5,4,3,2,1,0:T(8,128)(2,1)S(1)}, u32[]{:S(2)}, u32[]{:S(2)}) collective-permute-start(bf16[2,2,2,3,16,128]{5,4,3,2,1,0:T(8,128)(2,1)S(1)} %get-tuple-element.48), channel_id=1, source_target_pairs={{0,8},{16,24},{32,40},{48,56},{64,72},{80,88},{96,104},{112,120},{... | collective-permute-start | bytes 294920 | tf_op jit(solution)/shard_map/ppermute | solution.py:504
  112.4 1.9 %local.7.acc = f32[2,2,4,2,3,16,128]{6,5,4,3,2,1,0:T(8,128)S(1)} custom-call(f32[2,2,4,2,3,16,128]{6,5,4,3,2,1,0:T(8,128)S(1)} %get-tuple-element.44.psi, f32[2,2,108,128]{3,2,1,0:T(8,128)S(1)} %get-tuple-element.28.links, f32[2,2,216,128]{3,2,1,0:T(8,128)S(1)} %clover_rows.1.clover), custom_call_target="tpu_custom_call" | custom-call | flops 67108864 | bytes 2097152 | tf_op jit(solution)/shard_map/local/pallas_call | solution.py:533
  114.3 1.1 collective-permute-done.14.refs_2_
  115.5 0.7 collective-permute-done.15.refs_3_
  116.1 1.0 last.1
  (18 shorter events, 1.2 us)
Async XLA Ops:
  1.3 26.1 %collective-permute-start = (bf16[2,2,2,3,16,128]{5,4,3,2,1,0:T(8,128)(2,1)S(1)}, bf16[2,2,2,3,16,128]{5,4,3,2,1,0:T(8,128)(2,1)S(1)}, u32[]{:S(2)}, u32[]{:S(2)}) collective-permute-start(bf16[2,2,2,3,16,128]{5,4,3,2,1,0:T(8,128)(2,1)S(1)} %get-tuple-element.30), channel_id=1, source_target_pairs={{1,2},{3,4},{5,6},{7,0},{2,1},{4,3},{6,5},{0,7},{9,10},{11,12},{13... | collective-permute-start | bytes 294920 | tf_op jit(solution)/shard_map/ppermute | solution.py:504
  8.5 18.9 %collective-permute-start.1 = (bf16[2,2,2,3,16,128]{5,4,3,2,1,0:T(8,128)(2,1)S(1)}, bf16[2,2,2,3,16,128]{5,4,3,2,1,0:T(8,128)(2,1)S(1)}, u32[]{:S(2)}, u32[]{:S(2)}) collective-permute-start(bf16[2,2,2,3,16,128]{5,4,3,2,1,0:T(8,128)(2,1)S(1)} %get-tuple-element.31), channel_id=1, source_target_pairs={{0,1},{2,3},{4,5},{6,7},{1,0},{3,2},{5,4},{7,6},{8,9},{10,11},{12,... | collective-permute-start | bytes 294920 | tf_op jit(solution)/shard_map/ppermute | solution.py:504
  15.1 12.3 %collective-permute-start.2 = (bf16[2,2,2,3,16,128]{5,4,3,2,1,0:T(8,128)(2,1)S(1)}, bf16[2,2,2,3,16,128]{5,4,3,2,1,0:T(8,128)(2,1)S(1)}, u32[]{:S(2)}, u32[]{:S(2)}) collective-permute-start(bf16[2,2,2,3,16,128]{5,4,3,2,1,0:T(8,128)(2,1)S(1)} %get-tuple-element.32), channel_id=1, source_target_pairs={{8,16},{24,32},{40,48},{56,64},{72,80},{88,96},{104,112},{120,128}... | collective-permute-start | bytes 294920 | tf_op jit(solution)/shard_map/ppermute | solution.py:504
  23.3 6.0 %collective-permute-start.3 = (bf16[2,2,2,3,16,128]{5,4,3,2,1,0:T(8,128)(2,1)S(1)}, bf16[2,2,2,3,16,128]{5,4,3,2,1,0:T(8,128)(2,1)S(1)}, u32[]{:S(2)}, u32[]{:S(2)}) collective-permute-start(bf16[2,2,2,3,16,128]{5,4,3,2,1,0:T(8,128)(2,1)S(1)} %get-tuple-element.33), channel_id=1, source_target_pairs={{0,8},{16,24},{32,40},{48,56},{64,72},{80,88},{96,104},{112,120},{... | collective-permute-start | bytes 294920 | tf_op jit(solution)/shard_map/ppermute | solution.py:504
  27.4 17.8 %copy-start = (bf16[2,2,2,3,256,128]{5,4,3,2,1,0:T(8,128)(2,1)S(1)}, bf16[2,2,2,3,256,128]{5,4,3,2,1,0:T(8,128)(2,1)}, u32[]{:S(2)}) copy-start(bf16[2,2,2,3,256,128]{5,4,3,2,1,0:T(8,128)(2,1)} %vectors.1) | copy-start | bytes 4718596
  29.8 13.4 %collective-permute-start.4 = (bf16[2,2,2,3,16,128]{5,4,3,2,1,0:T(8,128)(2,1)S(1)}, bf16[2,2,2,3,16,128]{5,4,3,2,1,0:T(8,128)(2,1)S(1)}, u32[]{:S(2)}, u32[]{:S(2)}) collective-permute-start(bf16[2,2,2,3,16,128]{5,4,3,2,1,0:T(8,128)(2,1)S(1)} %get-tuple-element.35), channel_id=1, source_target_pairs={{1,2},{3,4},{5,6},{7,0},{2,1},{4,3},{6,5},{0,7},{9,10},{11,12},{13... | collective-permute-start | bytes 294920 | tf_op jit(solution)/shard_map/ppermute | solution.py:504
  33.3 9.8 %collective-permute-start.5 = (bf16[2,2,2,3,16,128]{5,4,3,2,1,0:T(8,128)(2,1)S(1)}, bf16[2,2,2,3,16,128]{5,4,3,2,1,0:T(8,128)(2,1)S(1)}, u32[]{:S(2)}, u32[]{:S(2)}) collective-permute-start(bf16[2,2,2,3,16,128]{5,4,3,2,1,0:T(8,128)(2,1)S(1)} %get-tuple-element.36), channel_id=1, source_target_pairs={{0,1},{2,3},{4,5},{6,7},{1,0},{3,2},{5,4},{7,6},{8,9},{10,11},{12,... | collective-permute-start | bytes 294920 | tf_op jit(solution)/shard_map/ppermute | solution.py:504
  35.3 10.0 %collective-permute-start.6 = (bf16[2,2,2,3,16,128]{5,4,3,2,1,0:T(8,128)(2,1)S(1)}, bf16[2,2,2,3,16,128]{5,4,3,2,1,0:T(8,128)(2,1)S(1)}, u32[]{:S(2)}, u32[]{:S(2)}) collective-permute-start(bf16[2,2,2,3,16,128]{5,4,3,2,1,0:T(8,128)(2,1)S(1)} %get-tuple-element.37), channel_id=1, source_target_pairs={{8,16},{24,32},{40,48},{56,64},{72,80},{88,96},{104,112},{120,128}... | collective-permute-start | bytes 294920 | tf_op jit(solution)/shard_map/ppermute | solution.py:504
  39.3 5.9 %collective-permute-start.7 = (bf16[2,2,2,3,16,128]{5,4,3,2,1,0:T(8,128)(2,1)S(1)}, bf16[2,2,2,3,16,128]{5,4,3,2,1,0:T(8,128)(2,1)S(1)}, u32[]{:S(2)}, u32[]{:S(2)}) collective-permute-start(bf16[2,2,2,3,16,128]{5,4,3,2,1,0:T(8,128)(2,1)S(1)} %get-tuple-element.38), channel_id=1, source_target_pairs={{0,8},{16,24},{32,40},{48,56},{64,72},{80,88},{96,104},{112,120},{... | collective-permute-start | bytes 294920 | tf_op jit(solution)/shard_map/ppermute | solution.py:504
  43.1 19.3 %copy-start.1 = (bf16[2,2,256,256]{3,2,1,0:T(8,128)(2,1)S(1)}, bf16[2,2,256,256]{3,2,1,0:T(8,128)(2,1)}, u32[]{:S(2)}) copy-start(bf16[2,2,256,256]{3,2,1,0:T(8,128)(2,1)} %elemental.1) | copy-start | bytes 1572868
  78.9 17.4 %collective-permute-start.8 = (bf16[2,2,2,3,16,128]{5,4,3,2,1,0:T(8,128)(2,1)S(1)}, bf16[2,2,2,3,16,128]{5,4,3,2,1,0:T(8,128)(2,1)S(1)}, u32[]{:S(2)}, u32[]{:S(2)}) collective-permute-start(bf16[2,2,2,3,16,128]{5,4,3,2,1,0:T(8,128)(2,1)S(1)} %get-tuple-element.40), channel_id=1, source_target_pairs={{1,2},{3,4},{5,6},{7,0},{2,1},{4,3},{6,5},{0,7},{9,10},{11,12},{13... | collective-permute-start | bytes 294920 | tf_op jit(solution)/shard_map/ppermute | solution.py:504
  87.2 9.1 %collective-permute-start.9 = (bf16[2,2,2,3,16,128]{5,4,3,2,1,0:T(8,128)(2,1)S(1)}, bf16[2,2,2,3,16,128]{5,4,3,2,1,0:T(8,128)(2,1)S(1)}, u32[]{:S(2)}, u32[]{:S(2)}) collective-permute-start(bf16[2,2,2,3,16,128]{5,4,3,2,1,0:T(8,128)(2,1)S(1)} %get-tuple-element.41), channel_id=1, source_target_pairs={{0,1},{2,3},{4,5},{6,7},{1,0},{3,2},{5,4},{7,6},{8,9},{10,11},{12,... | collective-permute-start | bytes 294920 | tf_op jit(solution)/shard_map/ppermute | solution.py:504
  89.1 10.0 %collective-permute-start.10 = (bf16[2,2,2,3,16,128]{5,4,3,2,1,0:T(8,128)(2,1)S(1)}, bf16[2,2,2,3,16,128]{5,4,3,2,1,0:T(8,128)(2,1)S(1)}, u32[]{:S(2)}, u32[]{:S(2)}) collective-permute-start(bf16[2,2,2,3,16,128]{5,4,3,2,1,0:T(8,128)(2,1)S(1)} %get-tuple-element.42), channel_id=1, source_target_pairs={{8,16},{24,32},{40,48},{56,64},{72,80},{88,96},{104,112},{120,128}... | collective-permute-start | bytes 294920 | tf_op jit(solution)/shard_map/ppermute | solution.py:504
  92.5 6.6 %collective-permute-start.11 = (bf16[2,2,2,3,16,128]{5,4,3,2,1,0:T(8,128)(2,1)S(1)}, bf16[2,2,2,3,16,128]{5,4,3,2,1,0:T(8,128)(2,1)S(1)}, u32[]{:S(2)}, u32[]{:S(2)}) collective-permute-start(bf16[2,2,2,3,16,128]{5,4,3,2,1,0:T(8,128)(2,1)S(1)} %get-tuple-element.43), channel_id=1, source_target_pairs={{0,8},{16,24},{32,40},{48,56},{64,72},{80,88},{96,104},{112,120},{... | collective-permute-start | bytes 294920 | tf_op jit(solution)/shard_map/ppermute | solution.py:504
  99.5 14.8 %collective-permute-start.12 = (bf16[2,2,2,3,16,128]{5,4,3,2,1,0:T(8,128)(2,1)S(1)}, bf16[2,2,2,3,16,128]{5,4,3,2,1,0:T(8,128)(2,1)S(1)}, u32[]{:S(2)}, u32[]{:S(2)}) collective-permute-start(bf16[2,2,2,3,16,128]{5,4,3,2,1,0:T(8,128)(2,1)S(1)} %get-tuple-element.45), channel_id=1, source_target_pairs={{1,2},{3,4},{5,6},{7,0},{2,1},{4,3},{6,5},{0,7},{9,10},{11,12},{13... | collective-permute-start | bytes 294920 | tf_op jit(solution)/shard_map/ppermute | solution.py:504
  103.1 11.3 %collective-permute-start.13 = (bf16[2,2,2,3,16,128]{5,4,3,2,1,0:T(8,128)(2,1)S(1)}, bf16[2,2,2,3,16,128]{5,4,3,2,1,0:T(8,128)(2,1)S(1)}, u32[]{:S(2)}, u32[]{:S(2)}) collective-permute-start(bf16[2,2,2,3,16,128]{5,4,3,2,1,0:T(8,128)(2,1)S(1)} %get-tuple-element.46), channel_id=1, source_target_pairs={{0,1},{2,3},{4,5},{6,7},{1,0},{3,2},{5,4},{7,6},{8,9},{10,11},{12,... | collective-permute-start | bytes 294920 | tf_op jit(solution)/shard_map/ppermute | solution.py:504
  105.2 10.2 %collective-permute-start.14 = (bf16[2,2,2,3,16,128]{5,4,3,2,1,0:T(8,128)(2,1)S(1)}, bf16[2,2,2,3,16,128]{5,4,3,2,1,0:T(8,128)(2,1)S(1)}, u32[]{:S(2)}, u32[]{:S(2)}) collective-permute-start(bf16[2,2,2,3,16,128]{5,4,3,2,1,0:T(8,128)(2,1)S(1)} %get-tuple-element.47), channel_id=1, source_target_pairs={{8,16},{24,32},{40,48},{56,64},{72,80},{88,96},{104,112},{120,128}... | collective-permute-start | bytes 294920 | tf_op jit(solution)/shard_map/ppermute | solution.py:504
  110.5 5.7 %collective-permute-start.15 = (bf16[2,2,2,3,16,128]{5,4,3,2,1,0:T(8,128)(2,1)S(1)}, bf16[2,2,2,3,16,128]{5,4,3,2,1,0:T(8,128)(2,1)S(1)}, u32[]{:S(2)}, u32[]{:S(2)}) collective-permute-start(bf16[2,2,2,3,16,128]{5,4,3,2,1,0:T(8,128)(2,1)S(1)} %get-tuple-element.48), channel_id=1, source_target_pairs={{0,8},{16,24},{32,40},{48,56},{64,72},{80,88},{96,104},{112,120},{... | collective-permute-start | bytes 294920 | tf_op jit(solution)/shard_map/ppermute | solution.py:504

commit v5 on v4

--- a/solution.py
+++ b/solution.py
@@ -17,7 +17,7 @@
     ((0, 0.0, -1.0), (1, 0.0, 1.0)),
     ((0, 1.0, 0.0), (1, 1.0, 0.0)),
 )
-ROWS = 8
+ROWS = 16
 LIMIT = 16 << 20
 F32 = jnp.float32
 BF16 = jnp.bfloat16
@@ -222,7 +222,7 @@
     pl.when(jnp.logical_not(odd))(lambda: function(pair[1], pair[0]))
 
 
-def faces_part(psi, links, where, t_outer, t_inner, z_outer, z_inner):
+def faces_part(psi, links, where, z_outer, z_inner, t_outer, t_inner):
     by_parity(where[0], functools.partial(z_faces, psi, links), (z_inner, z_outer))
     by_parity(where[1], functools.partial(t_faces, psi, links), (t_inner, t_outer))
 
@@ -262,7 +262,7 @@
         out[t, z, key[0], key[1], key[2]] = total[key]
 
 
-def halo_part(acc, links, where, t_outer, t_inner, z_outer, z_inner, out):
+def halo_part(acc, links, where, z_outer, z_inner, t_outer, t_inner, out):
     by_parity(where[0], functools.partial(z_halo, acc, links, out), (z_inner, z_outer))
     by_parity(where[1], functools.partial(t_halo, links, where, out), (t_inner, t_outer))
 
@@ -493,7 +493,7 @@
     spinor_type = jax.ShapeDtypeStruct(source.shape, F32)
     z_face = jax.ShapeDtypeStruct((slices, 2, 2, 3, columns, sites), BF16)
     t_face = jax.ShapeDtypeStruct((layers, 2, 2, 3, columns, sites), BF16)
-    faces = (t_face, t_face, z_face, z_face)
+    faces = (z_face, z_face, t_face, t_face)
     link_rows = jax.ShapeDtypeStruct((slices, layers, 108, sites), F32)
     clover_rows = jax.ShapeDtypeStruct((slices, layers, 216, sites), F32)
     row_count = slices * 2 * eigen_count // 128
@@ -503,12 +503,12 @@
         pairs = [(i % count, (i + 1) % count) for i in range(offset, count + offset, 2)]
         return lax.ppermute(value, axis, pairs + [(b, a) for a, b in pairs])
 
-    def exchanged(t_outer, t_inner, z_outer, z_inner):
+    def exchanged(z_outer, z_inner, t_outer, t_inner):
         return (
+            swapped(z_outer, "space", 1),
+            swapped(z_inner, "space", 0),
             swapped(t_outer, "tm", 1),
             swapped(t_inner, "tm", 0),
-            swapped(z_outer, "space", 1),
-            swapped(z_inner, "space", 0),
         )
 
     gauge = jnp.transpose(gauge_links, (0, 1, 2, 4, 5, 3, 6))

time: 118 us -> 114 us (0.966)
  waiting for transfers between devices: 8.45 us -> 0.08 us
  blocking collectives: 30.8 us -> 34.5 us
    ppermute x16, waiting for transfers between devices: 8.45 us -> 0.08 us  [swapped(): return lax.ppermute(value, axis, pairs + [(b, a) for a, b in pairs])]
    all_to_all x1, blocking collectives: 16.2 us -> 19.1 us  [on_device(): shares = lax.all_to_all(partial_sums, 'space', 0, 0, tiled=True)]
  transfers between devices with their start and end apart: 16 -> 16, of which waited for: 5 -> 0; matrix products, arithmetic and copies ran while one was open for 0% -> 0% of each run, Pallas kernels for 7% -> 6%
where the time goes in v5:
time: 114 us; the launch traced here: 113 us
  starting transfers between devices  64.4 us (56%)
  blocking collectives  34.5 us (30%)
  Pallas kernels  13.4 us (12%)
    ppermute x16, starting transfers between devices, swapped(): return lax.ppermute(value, axis, pairs + [(b, a) for a, b in pairs])  64.4 us
    all_to_all x1, blocking collectives, on_device(): shares = lax.all_to_all(partial_sums, 'space', 0, 0, tiled=True)  19.1 us
    all_to_all x1, blocking collectives, on_device(): mixed = lax.all_to_all(mixed, 'space', 0, 0, tiled=True)  15.5 us
    pallas_call x4, Pallas kernels, local(): call(local_kernel, 3, spinor_type, flops=1 << 26, name='local')  7.04 us
  transfers between devices with their start and end apart: 16, of which 0 were waited for; matrix products, arithmetic and copies ran while one was open for 0% of the time, Pallas kernels for 6%

profile of v5, /device:TPU:1, one launch (start us, length us, event | category | flops | bytes accessed | tf_op | source)
XLA Modules:
  0.0 112.7 jit_solution(16893834800525122411)
XLA Ops:
  0.0 1.3 %entry.1 = (f32[2,2,4,2,3,16,128]{6,5,4,3,2,1,0:T(8,128)S(1)}, f32[2,2,108,128]{3,2,1,0:T(8,128)S(1)}, bf16[2,2,2,3,16,128]{5,4,3,2,1,0:T(8,128)(2,1)S(1)}, bf16...) custom-call(bf16[2,2,4,2,3,16,128]{6,5,4,3,2,1,0:T(8,128)(2,1)} %sou, ...), custom_call_target="tpu_custom_call" | custom-call | flops 4194304 | bytes 2097152 | tf_op jit(solution)/shard_map/entry/pallas_call | solution.py:517
  1.3 9.9 %collective-permute-start = (bf16[2,2,2,3,16,128]{5,4,3,2,1,0:T(8,128)(2,1)S(1)}, bf16[2,2,2,3,16,128]{5,4,3,2,1,0:T(8,128)(2,1)S(1)}, u32[]{:S(2)}, u32[]{:S(2)}) collective-permute-start(bf16[2,2,2,3,16,128]{5,4,3,2,1,0:T(8,128)(2,1)S(1)} %get-tuple-element.30), channel_id=1, source_target_pairs={{8,16},{24,32},{40,48},{56,64},{72,80},{88,96},{104,112},{120,128}... | collective-permute-start | bytes 294920 | tf_op jit(solution)/shard_map/ppermute | solution.py:504
  11.3 1.9 %collective-permute-start.1 = (bf16[2,2,2,3,16,128]{5,4,3,2,1,0:T(8,128)(2,1)S(1)}, bf16[2,2,2,3,16,128]{5,4,3,2,1,0:T(8,128)(2,1)S(1)}, u32[]{:S(2)}, u32[]{:S(2)}) collective-permute-start(bf16[2,2,2,3,16,128]{5,4,3,2,1,0:T(8,128)(2,1)S(1)} %get-tuple-element.31), channel_id=1, source_target_pairs={{0,8},{16,24},{32,40},{48,56},{64,72},{80,88},{96,104},{112,120},{... | collective-permute-start | bytes 294920 | tf_op jit(solution)/shard_map/ppermute | solution.py:504
  13.2 6.6 %collective-permute-start.2 = (bf16[2,2,2,3,16,128]{5,4,3,2,1,0:T(8,128)(2,1)S(1)}, bf16[2,2,2,3,16,128]{5,4,3,2,1,0:T(8,128)(2,1)S(1)}, u32[]{:S(2)}, u32[]{:S(2)}) collective-permute-start(bf16[2,2,2,3,16,128]{5,4,3,2,1,0:T(8,128)(2,1)S(1)} %get-tuple-element.32), channel_id=1, source_target_pairs={{1,2},{3,4},{5,6},{7,0},{2,1},{4,3},{6,5},{0,7},{9,10},{11,12},{13... | collective-permute-start | bytes 294920 | tf_op jit(solution)/shard_map/ppermute | solution.py:504
  19.9 5.4 %collective-permute-start.3 = (bf16[2,2,2,3,16,128]{5,4,3,2,1,0:T(8,128)(2,1)S(1)}, bf16[2,2,2,3,16,128]{5,4,3,2,1,0:T(8,128)(2,1)S(1)}, u32[]{:S(2)}, u32[]{:S(2)}) collective-permute-start(bf16[2,2,2,3,16,128]{5,4,3,2,1,0:T(8,128)(2,1)S(1)} %get-tuple-element.33), channel_id=1, source_target_pairs={{0,1},{2,3},{4,5},{6,7},{1,0},{3,2},{5,4},{7,6},{8,9},{10,11},{12,... | collective-permute-start | bytes 294920 | tf_op jit(solution)/shard_map/ppermute | solution.py:504
  25.3 0.2 clover_rows.1.clover
  25.5 1.8 %local.4.acc = f32[2,2,4,2,3,16,128]{6,5,4,3,2,1,0:T(8,128)S(1)} custom-call(f32[2,2,4,2,3,16,128]{6,5,4,3,2,1,0:T(8,128)S(1)} %get-tuple-element.27.psi, f32[2,2,108,128]{3,2,1,0:T(8,128)S(1)} %get-tuple-element.28.links, f32[2,2,216,128]{3,2,1,0:T(8,128)S(1)} %clover_rows.1.clover), custom_call_target="tpu_custom_call" | custom-call | flops 67108864 | bytes 2097152 | tf_op jit(solution)/shard_map/local/pallas_call | solution.py:533
  27.3 0.5 middle.2
  27.8 4.0 %collective-permute-start.4 = (bf16[2,2,2,3,16,128]{5,4,3,2,1,0:T(8,128)(2,1)S(1)}, bf16[2,2,2,3,16,128]{5,4,3,2,1,0:T(8,128)(2,1)S(1)}, u32[]{:S(2)}, u32[]{:S(2)}) collective-permute-start(bf16[2,2,2,3,16,128]{5,4,3,2,1,0:T(8,128)(2,1)S(1)} %get-tuple-element.35), channel_id=1, source_target_pairs={{8,16},{24,32},{40,48},{56,64},{72,80},{88,96},{104,112},{120,128}... | collective-permute-start | bytes 294920 | tf_op jit(solution)/shard_map/ppermute | solution.py:504
  31.9 1.9 %collective-permute-start.5 = (bf16[2,2,2,3,16,128]{5,4,3,2,1,0:T(8,128)(2,1)S(1)}, bf16[2,2,2,3,16,128]{5,4,3,2,1,0:T(8,128)(2,1)S(1)}, u32[]{:S(2)}, u32[]{:S(2)}) collective-permute-start(bf16[2,2,2,3,16,128]{5,4,3,2,1,0:T(8,128)(2,1)S(1)} %get-tuple-element.36), channel_id=1, source_target_pairs={{0,8},{16,24},{32,40},{48,56},{64,72},{80,88},{96,104},{112,120},{... | collective-permute-start | bytes 294920 | tf_op jit(solution)/shard_map/ppermute | solution.py:504
  33.8 3.6 %collective-permute-start.6 = (bf16[2,2,2,3,16,128]{5,4,3,2,1,0:T(8,128)(2,1)S(1)}, bf16[2,2,2,3,16,128]{5,4,3,2,1,0:T(8,128)(2,1)S(1)}, u32[]{:S(2)}, u32[]{:S(2)}) collective-permute-start(bf16[2,2,2,3,16,128]{5,4,3,2,1,0:T(8,128)(2,1)S(1)} %get-tuple-element.37), channel_id=1, source_target_pairs={{1,2},{3,4},{5,6},{7,0},{2,1},{4,3},{6,5},{0,7},{9,10},{11,12},{13... | collective-permute-start | bytes 294920 | tf_op jit(solution)/shard_map/ppermute | solution.py:504
  37.4 2.8 %collective-permute-start.7 = (bf16[2,2,2,3,16,128]{5,4,3,2,1,0:T(8,128)(2,1)S(1)}, bf16[2,2,2,3,16,128]{5,4,3,2,1,0:T(8,128)(2,1)S(1)}, u32[]{:S(2)}, u32[]{:S(2)}) collective-permute-start(bf16[2,2,2,3,16,128]{5,4,3,2,1,0:T(8,128)(2,1)S(1)} %get-tuple-element.38), channel_id=1, source_target_pairs={{0,1},{2,3},{4,5},{6,7},{1,0},{3,2},{5,4},{7,6},{8,9},{10,11},{12,... | collective-permute-start | bytes 294920 | tf_op jit(solution)/shard_map/ppermute | solution.py:504
  40.1 1.8 %local.5.acc = f32[2,2,4,2,3,16,128]{6,5,4,3,2,1,0:T(8,128)S(1)} custom-call(f32[2,2,4,2,3,16,128]{6,5,4,3,2,1,0:T(8,128)S(1)} %get-tuple-element.34.psi, f32[2,2,108,128]{3,2,1,0:T(8,128)S(1)} %get-tuple-element.28.links, f32[2,2,216,128]{3,2,1,0:T(8,128)S(1)} %clover_rows.1.clover), custom_call_target="tpu_custom_call" | custom-call | flops 67108864 | bytes 2097152 | tf_op jit(solution)/shard_map/local/pallas_call | solution.py:533
  41.9 0.0 copy-start.1
  41.9 0.0 collective-permute-done.6.refs_2_
  42.0 1.0 coefficients.1
  43.0 19.1 %all_to_all.10.shares = f32[64,8,128]{2,1,0:T(8,128)S(1)} all-to-all(f32[64,8,128]{2,1,0:T(8,128)S(1)} %coefficients.1), channel_id=1, replica_groups=mesh['space'=64,'tm'=8] {'space'}, dimensions={0} | all-to-all | bytes 524288 | tf_op jit(solution)/shard_map/all_to_all | solution.py:555
  62.0 0.7 mix.1
  62.7 15.5 %all_to_all.11.mixed = bf16[64,8,128]{2,1,0:T(8,128)(2,1)S(1)} all-to-all(bf16[64,8,128]{2,1,0:T(8,128)(2,1)S(1)} %mix.1), channel_id=1, replica_groups=mesh['space'=64,'tm'=8] {'space'}, dimensions={0} | all-to-all | bytes 262144 | tf_op jit(solution)/shard_map/all_to_all | solution.py:562
  78.2 1.1 %expand.1 = (f32[2,2,4,2,3,16,128]{6,5,4,3,2,1,0:T(8,128)S(1)}, bf16[2,2,2,3,16,128]{5,4,3,2,1,0:T(8,128)(2,1)S(1)}, bf16[2,2,2,3,16,128]{5,4,3,2,1,0:T(8,128)(2...) custom-call(bf16[64,8,128]{2,1,0:T(8,128)(2,1)S(1)} %all_to_all.11.mixed, ...), custom_call_target="tpu_custom_call" | custom-call | flops 4194304 | bytes 2097152 | tf_op jit(solution)/shard_map/expand/pallas_call | solution.py:563
  79.3 3.7 %collective-permute-start.8 = (bf16[2,2,2,3,16,128]{5,4,3,2,1,0:T(8,128)(2,1)S(1)}, bf16[2,2,2,3,16,128]{5,4,3,2,1,0:T(8,128)(2,1)S(1)}, u32[]{:S(2)}, u32[]{:S(2)}) collective-permute-start(bf16[2,2,2,3,16,128]{5,4,3,2,1,0:T(8,128)(2,1)S(1)} %get-tuple-element.40), channel_id=1, source_target_pairs={{8,16},{24,32},{40,48},{56,64},{72,80},{88,96},{104,112},{120,128}... | collective-permute-start | bytes 294920 | tf_op jit(solution)/shard_map/ppermute | solution.py:504
  83.0 1.9 %collective-permute-start.9 = (bf16[2,2,2,3,16,128]{5,4,3,2,1,0:T(8,128)(2,1)S(1)}, bf16[2,2,2,3,16,128]{5,4,3,2,1,0:T(8,128)(2,1)S(1)}, u32[]{:S(2)}, u32[]{:S(2)}) collective-permute-start(bf16[2,2,2,3,16,128]{5,4,3,2,1,0:T(8,128)(2,1)S(1)} %get-tuple-element.41), channel_id=1, source_target_pairs={{0,8},{16,24},{32,40},{48,56},{64,72},{80,88},{96,104},{112,120},{... | collective-permute-start | bytes 294920 | tf_op jit(solution)/shard_map/ppermute | solution.py:504
  84.9 5.4 %collective-permute-start.10 = (bf16[2,2,2,3,16,128]{5,4,3,2,1,0:T(8,128)(2,1)S(1)}, bf16[2,2,2,3,16,128]{5,4,3,2,1,0:T(8,128)(2,1)S(1)}, u32[]{:S(2)}, u32[]{:S(2)}) collective-permute-start(bf16[2,2,2,3,16,128]{5,4,3,2,1,0:T(8,128)(2,1)S(1)} %get-tuple-element.42), channel_id=1, source_target_pairs={{1,2},{3,4},{5,6},{7,0},{2,1},{4,3},{6,5},{0,7},{9,10},{11,12},{13... | collective-permute-start | bytes 294920 | tf_op jit(solution)/shard_map/ppermute | solution.py:504
  90.3 1.9 %collective-permute-start.11 = (bf16[2,2,2,3,16,128]{5,4,3,2,1,0:T(8,128)(2,1)S(1)}, bf16[2,2,2,3,16,128]{5,4,3,2,1,0:T(8,128)(2,1)S(1)}, u32[]{:S(2)}, u32[]{:S(2)}) collective-permute-start(bf16[2,2,2,3,16,128]{5,4,3,2,1,0:T(8,128)(2,1)S(1)} %get-tuple-element.43), channel_id=1, source_target_pairs={{0,1},{2,3},{4,5},{6,7},{1,0},{3,2},{5,4},{7,6},{8,9},{10,11},{12,... | collective-permute-start | bytes 294920 | tf_op jit(solution)/shard_map/ppermute | solution.py:504
  92.2 1.8 %local.6.acc = f32[2,2,4,2,3,16,128]{6,5,4,3,2,1,0:T(8,128)S(1)} custom-call(f32[2,2,4,2,3,16,128]{6,5,4,3,2,1,0:T(8,128)S(1)} %get-tuple-element.39.psi, f32[2,2,108,128]{3,2,1,0:T(8,128)S(1)} %get-tuple-element.28.links, f32[2,2,216,128]{3,2,1,0:T(8,128)S(1)} %clover_rows.1.clover), custom_call_target="tpu_custom_call" | custom-call | flops 67108864 | bytes 2097152 | tf_op jit(solution)/shard_map/local/pallas_call | solution.py:533
  94.1 0.5 middle.3
  94.5 6.2 %collective-permute-start.12 = (bf16[2,2,2,3,16,128]{5,4,3,2,1,0:T(8,128)(2,1)S(1)}, bf16[2,2,2,3,16,128]{5,4,3,2,1,0:T(8,128)(2,1)S(1)}, u32[]{:S(2)}, u32[]{:S(2)}) collective-permute-start(bf16[2,2,2,3,16,128]{5,4,3,2,1,0:T(8,128)(2,1)S(1)} %get-tuple-element.45), channel_id=1, source_target_pairs={{8,16},{24,32},{40,48},{56,64},{72,80},{88,96},{104,112},{120,128}... | collective-permute-start | bytes 294920 | tf_op jit(solution)/shard_map/ppermute | solution.py:504
  100.8 1.9 %collective-permute-start.13 = (bf16[2,2,2,3,16,128]{5,4,3,2,1,0:T(8,128)(2,1)S(1)}, bf16[2,2,2,3,16,128]{5,4,3,2,1,0:T(8,128)(2,1)S(1)}, u32[]{:S(2)}, u32[]{:S(2)}) collective-permute-start(bf16[2,2,2,3,16,128]{5,4,3,2,1,0:T(8,128)(2,1)S(1)} %get-tuple-element.46), channel_id=1, source_target_pairs={{0,8},{16,24},{32,40},{48,56},{64,72},{80,88},{96,104},{112,120},{... | collective-permute-start | bytes 294920 | tf_op jit(solution)/shard_map/ppermute | solution.py:504
  102.7 4.4 %collective-permute-start.14 = (bf16[2,2,2,3,16,128]{5,4,3,2,1,0:T(8,128)(2,1)S(1)}, bf16[2,2,2,3,16,128]{5,4,3,2,1,0:T(8,128)(2,1)S(1)}, u32[]{:S(2)}, u32[]{:S(2)}) collective-permute-start(bf16[2,2,2,3,16,128]{5,4,3,2,1,0:T(8,128)(2,1)S(1)} %get-tuple-element.47), channel_id=1, source_target_pairs={{1,2},{3,4},{5,6},{7,0},{2,1},{4,3},{6,5},{0,7},{9,10},{11,12},{13... | collective-permute-start | bytes 294920 | tf_op jit(solution)/shard_map/ppermute | solution.py:504
  107.1 2.7 %collective-permute-start.15 = (bf16[2,2,2,3,16,128]{5,4,3,2,1,0:T(8,128)(2,1)S(1)}, bf16[2,2,2,3,16,128]{5,4,3,2,1,0:T(8,128)(2,1)S(1)}, u32[]{:S(2)}, u32[]{:S(2)}) collective-permute-start(bf16[2,2,2,3,16,128]{5,4,3,2,1,0:T(8,128)(2,1)S(1)} %get-tuple-element.48), channel_id=1, source_target_pairs={{0,1},{2,3},{4,5},{6,7},{1,0},{3,2},{5,4},{7,6},{8,9},{10,11},{12,... | collective-permute-start | bytes 294920 | tf_op jit(solution)/shard_map/ppermute | solution.py:504
  109.9 1.8 %local.7.acc = f32[2,2,4,2,3,16,128]{6,5,4,3,2,1,0:T(8,128)S(1)} custom-call(f32[2,2,4,2,3,16,128]{6,5,4,3,2,1,0:T(8,128)S(1)} %get-tuple-element.44.psi, f32[2,2,108,128]{3,2,1,0:T(8,128)S(1)} %get-tuple-element.28.links, f32[2,2,216,128]{3,2,1,0:T(8,128)S(1)} %clover_rows.1.clover), custom_call_target="tpu_custom_call" | custom-call | flops 67108864 | bytes 2097152 | tf_op jit(solution)/shard_map/local/pallas_call | solution.py:533
  111.7 1.1 last.1
  (18 shorter events, 0.0 us)
Async XLA Ops:
  1.3 26.0 %collective-permute-start = (bf16[2,2,2,3,16,128]{5,4,3,2,1,0:T(8,128)(2,1)S(1)}, bf16[2,2,2,3,16,128]{5,4,3,2,1,0:T(8,128)(2,1)S(1)}, u32[]{:S(2)}, u32[]{:S(2)}) collective-permute-start(bf16[2,2,2,3,16,128]{5,4,3,2,1,0:T(8,128)(2,1)S(1)} %get-tuple-element.30), channel_id=1, source_target_pairs={{8,16},{24,32},{40,48},{56,64},{72,80},{88,96},{104,112},{120,128}... | collective-permute-start | bytes 294920 | tf_op jit(solution)/shard_map/ppermute | solution.py:504
  11.3 16.0 %collective-permute-start.1 = (bf16[2,2,2,3,16,128]{5,4,3,2,1,0:T(8,128)(2,1)S(1)}, bf16[2,2,2,3,16,128]{5,4,3,2,1,0:T(8,128)(2,1)S(1)}, u32[]{:S(2)}, u32[]{:S(2)}) collective-permute-start(bf16[2,2,2,3,16,128]{5,4,3,2,1,0:T(8,128)(2,1)S(1)} %get-tuple-element.31), channel_id=1, source_target_pairs={{0,8},{16,24},{32,40},{48,56},{64,72},{80,88},{96,104},{112,120},{... | collective-permute-start | bytes 294920 | tf_op jit(solution)/shard_map/ppermute | solution.py:504
  13.2 14.1 %collective-permute-start.2 = (bf16[2,2,2,3,16,128]{5,4,3,2,1,0:T(8,128)(2,1)S(1)}, bf16[2,2,2,3,16,128]{5,4,3,2,1,0:T(8,128)(2,1)S(1)}, u32[]{:S(2)}, u32[]{:S(2)}) collective-permute-start(bf16[2,2,2,3,16,128]{5,4,3,2,1,0:T(8,128)(2,1)S(1)} %get-tuple-element.32), channel_id=1, source_target_pairs={{1,2},{3,4},{5,6},{7,0},{2,1},{4,3},{6,5},{0,7},{9,10},{11,12},{13... | collective-permute-start | bytes 294920 | tf_op jit(solution)/shard_map/ppermute | solution.py:504
  19.9 7.5 %collective-permute-start.3 = (bf16[2,2,2,3,16,128]{5,4,3,2,1,0:T(8,128)(2,1)S(1)}, bf16[2,2,2,3,16,128]{5,4,3,2,1,0:T(8,128)(2,1)S(1)}, u32[]{:S(2)}, u32[]{:S(2)}) collective-permute-start(bf16[2,2,2,3,16,128]{5,4,3,2,1,0:T(8,128)(2,1)S(1)} %get-tuple-element.33), channel_id=1, source_target_pairs={{0,1},{2,3},{4,5},{6,7},{1,0},{3,2},{5,4},{7,6},{8,9},{10,11},{12,... | collective-permute-start | bytes 294920 | tf_op jit(solution)/shard_map/ppermute | solution.py:504
  27.3 14.7 %copy-start = (bf16[2,2,2,3,256,128]{5,4,3,2,1,0:T(8,128)(2,1)S(1)}, bf16[2,2,2,3,256,128]{5,4,3,2,1,0:T(8,128)(2,1)}, u32[]{:S(2)}) copy-start(bf16[2,2,2,3,256,128]{5,4,3,2,1,0:T(8,128)(2,1)} %vectors.1) | copy-start | bytes 4718596
  27.8 14.1 %collective-permute-start.4 = (bf16[2,2,2,3,16,128]{5,4,3,2,1,0:T(8,128)(2,1)S(1)}, bf16[2,2,2,3,16,128]{5,4,3,2,1,0:T(8,128)(2,1)S(1)}, u32[]{:S(2)}, u32[]{:S(2)}) collective-permute-start(bf16[2,2,2,3,16,128]{5,4,3,2,1,0:T(8,128)(2,1)S(1)} %get-tuple-element.35), channel_id=1, source_target_pairs={{8,16},{24,32},{40,48},{56,64},{72,80},{88,96},{104,112},{120,128}... | collective-permute-start | bytes 294920 | tf_op jit(solution)/shard_map/ppermute | solution.py:504
  31.9 10.1 %collective-permute-start.5 = (bf16[2,2,2,3,16,128]{5,4,3,2,1,0:T(8,128)(2,1)S(1)}, bf16[2,2,2,3,16,128]{5,4,3,2,1,0:T(8,128)(2,1)S(1)}, u32[]{:S(2)}, u32[]{:S(2)}) collective-permute-start(bf16[2,2,2,3,16,128]{5,4,3,2,1,0:T(8,128)(2,1)S(1)} %get-tuple-element.36), channel_id=1, source_target_pairs={{0,8},{16,24},{32,40},{48,56},{64,72},{80,88},{96,104},{112,120},{... | collective-permute-start | bytes 294920 | tf_op jit(solution)/shard_map/ppermute | solution.py:504
  33.8 8.2 %collective-permute-start.6 = (bf16[2,2,2,3,16,128]{5,4,3,2,1,0:T(8,128)(2,1)S(1)}, bf16[2,2,2,3,16,128]{5,4,3,2,1,0:T(8,128)(2,1)S(1)}, u32[]{:S(2)}, u32[]{:S(2)}) collective-permute-start(bf16[2,2,2,3,16,128]{5,4,3,2,1,0:T(8,128)(2,1)S(1)} %get-tuple-element.37), channel_id=1, source_target_pairs={{1,2},{3,4},{5,6},{7,0},{2,1},{4,3},{6,5},{0,7},{9,10},{11,12},{13... | collective-permute-start | bytes 294920 | tf_op jit(solution)/shard_map/ppermute | solution.py:504
  37.4 4.6 %collective-permute-start.7 = (bf16[2,2,2,3,16,128]{5,4,3,2,1,0:T(8,128)(2,1)S(1)}, bf16[2,2,2,3,16,128]{5,4,3,2,1,0:T(8,128)(2,1)S(1)}, u32[]{:S(2)}, u32[]{:S(2)}) collective-permute-start(bf16[2,2,2,3,16,128]{5,4,3,2,1,0:T(8,128)(2,1)S(1)} %get-tuple-element.38), channel_id=1, source_target_pairs={{0,1},{2,3},{4,5},{6,7},{1,0},{3,2},{5,4},{7,6},{8,9},{10,11},{12,... | collective-permute-start | bytes 294920 | tf_op jit(solution)/shard_map/ppermute | solution.py:504
  41.9 20.1 %copy-start.1 = (bf16[2,2,256,256]{3,2,1,0:T(8,128)(2,1)S(1)}, bf16[2,2,256,256]{3,2,1,0:T(8,128)(2,1)}, u32[]{:S(2)}) copy-start(bf16[2,2,256,256]{3,2,1,0:T(8,128)(2,1)} %elemental.1) | copy-start | bytes 1572868
  79.3 14.7 %collective-permute-start.8 = (bf16[2,2,2,3,16,128]{5,4,3,2,1,0:T(8,128)(2,1)S(1)}, bf16[2,2,2,3,16,128]{5,4,3,2,1,0:T(8,128)(2,1)S(1)}, u32[]{:S(2)}, u32[]{:S(2)}) collective-permute-start(bf16[2,2,2,3,16,128]{5,4,3,2,1,0:T(8,128)(2,1)S(1)} %get-tuple-element.40), channel_id=1, source_target_pairs={{8,16},{24,32},{40,48},{56,64},{72,80},{88,96},{104,112},{120,128}... | collective-permute-start | bytes 294920 | tf_op jit(solution)/shard_map/ppermute | solution.py:504
  83.0 11.0 %collective-permute-start.9 = (bf16[2,2,2,3,16,128]{5,4,3,2,1,0:T(8,128)(2,1)S(1)}, bf16[2,2,2,3,16,128]{5,4,3,2,1,0:T(8,128)(2,1)S(1)}, u32[]{:S(2)}, u32[]{:S(2)}) collective-permute-start(bf16[2,2,2,3,16,128]{5,4,3,2,1,0:T(8,128)(2,1)S(1)} %get-tuple-element.41), channel_id=1, source_target_pairs={{0,8},{16,24},{32,40},{48,56},{64,72},{80,88},{96,104},{112,120},{... | collective-permute-start | bytes 294920 | tf_op jit(solution)/shard_map/ppermute | solution.py:504
  84.9 9.1 %collective-permute-start.10 = (bf16[2,2,2,3,16,128]{5,4,3,2,1,0:T(8,128)(2,1)S(1)}, bf16[2,2,2,3,16,128]{5,4,3,2,1,0:T(8,128)(2,1)S(1)}, u32[]{:S(2)}, u32[]{:S(2)}) collective-permute-start(bf16[2,2,2,3,16,128]{5,4,3,2,1,0:T(8,128)(2,1)S(1)} %get-tuple-element.42), channel_id=1, source_target_pairs={{1,2},{3,4},{5,6},{7,0},{2,1},{4,3},{6,5},{0,7},{9,10},{11,12},{13... | collective-permute-start | bytes 294920 | tf_op jit(solution)/shard_map/ppermute | solution.py:504
  90.3 3.7 %collective-permute-start.11 = (bf16[2,2,2,3,16,128]{5,4,3,2,1,0:T(8,128)(2,1)S(1)}, bf16[2,2,2,3,16,128]{5,4,3,2,1,0:T(8,128)(2,1)S(1)}, u32[]{:S(2)}, u32[]{:S(2)}) collective-permute-start(bf16[2,2,2,3,16,128]{5,4,3,2,1,0:T(8,128)(2,1)S(1)} %get-tuple-element.43), channel_id=1, source_target_pairs={{0,1},{2,3},{4,5},{6,7},{1,0},{3,2},{5,4},{7,6},{8,9},{10,11},{12,... | collective-permute-start | bytes 294920 | tf_op jit(solution)/shard_map/ppermute | solution.py:504
  94.5 17.1 %collective-permute-start.12 = (bf16[2,2,2,3,16,128]{5,4,3,2,1,0:T(8,128)(2,1)S(1)}, bf16[2,2,2,3,16,128]{5,4,3,2,1,0:T(8,128)(2,1)S(1)}, u32[]{:S(2)}, u32[]{:S(2)}) collective-permute-start(bf16[2,2,2,3,16,128]{5,4,3,2,1,0:T(8,128)(2,1)S(1)} %get-tuple-element.45), channel_id=1, source_target_pairs={{8,16},{24,32},{40,48},{56,64},{72,80},{88,96},{104,112},{120,128}... | collective-permute-start | bytes 294920 | tf_op jit(solution)/shard_map/ppermute | solution.py:504
  100.8 10.9 %collective-permute-start.13 = (bf16[2,2,2,3,16,128]{5,4,3,2,1,0:T(8,128)(2,1)S(1)}, bf16[2,2,2,3,16,128]{5,4,3,2,1,0:T(8,128)(2,1)S(1)}, u32[]{:S(2)}, u32[]{:S(2)}) collective-permute-start(bf16[2,2,2,3,16,128]{5,4,3,2,1,0:T(8,128)(2,1)S(1)} %get-tuple-element.46), channel_id=1, source_target_pairs={{0,8},{16,24},{32,40},{48,56},{64,72},{80,88},{96,104},{112,120},{... | collective-permute-start | bytes 294920 | tf_op jit(solution)/shard_map/ppermute | solution.py:504
  102.7 8.9 %collective-permute-start.14 = (bf16[2,2,2,3,16,128]{5,4,3,2,1,0:T(8,128)(2,1)S(1)}, bf16[2,2,2,3,16,128]{5,4,3,2,1,0:T(8,128)(2,1)S(1)}, u32[]{:S(2)}, u32[]{:S(2)}) collective-permute-start(bf16[2,2,2,3,16,128]{5,4,3,2,1,0:T(8,128)(2,1)S(1)} %get-tuple-element.47), channel_id=1, source_target_pairs={{1,2},{3,4},{5,6},{7,0},{2,1},{4,3},{6,5},{0,7},{9,10},{11,12},{13... | collective-permute-start | bytes 294920 | tf_op jit(solution)/shard_map/ppermute | solution.py:504
  107.1 4.5 %collective-permute-start.15 = (bf16[2,2,2,3,16,128]{5,4,3,2,1,0:T(8,128)(2,1)S(1)}, bf16[2,2,2,3,16,128]{5,4,3,2,1,0:T(8,128)(2,1)S(1)}, u32[]{:S(2)}, u32[]{:S(2)}) collective-permute-start(bf16[2,2,2,3,16,128]{5,4,3,2,1,0:T(8,128)(2,1)S(1)} %get-tuple-element.48), channel_id=1, source_target_pairs={{0,1},{2,3},{4,5},{6,7},{1,0},{3,2},{5,4},{7,6},{8,9},{10,11},{12,... | collective-permute-start | bytes 294920 | tf_op jit(solution)/shard_map/ppermute | solution.py:504

commit v6 on v5

--- a/solution.py
+++ b/solution.py
@@ -222,7 +222,7 @@
     pl.when(jnp.logical_not(odd))(lambda: function(pair[1], pair[0]))
 
 
-def faces_part(psi, links, where, z_outer, z_inner, t_outer, t_inner):
+def faces_part(psi, links, where, z_outer, t_outer, z_inner, t_inner):
     by_parity(where[0], functools.partial(z_faces, psi, links), (z_inner, z_outer))
     by_parity(where[1], functools.partial(t_faces, psi, links), (t_inner, t_outer))
 
@@ -262,7 +262,7 @@
         out[t, z, key[0], key[1], key[2]] = total[key]
 
 
-def halo_part(acc, links, where, z_outer, z_inner, t_outer, t_inner, out):
+def halo_part(acc, links, where, z_outer, t_outer, z_inner, t_inner, out):
     by_parity(where[0], functools.partial(z_halo, acc, links, out), (z_inner, z_outer))
     by_parity(where[1], functools.partial(t_halo, links, where, out), (t_inner, t_outer))
 
@@ -493,7 +493,7 @@
     spinor_type = jax.ShapeDtypeStruct(source.shape, F32)
     z_face = jax.ShapeDtypeStruct((slices, 2, 2, 3, columns, sites), BF16)
     t_face = jax.ShapeDtypeStruct((layers, 2, 2, 3, columns, sites), BF16)
-    faces = (z_face, z_face, t_face, t_face)
+    faces = (z_face, t_face, z_face, t_face)
     link_rows = jax.ShapeDtypeStruct((slices, layers, 108, sites), F32)
     clover_rows = jax.ShapeDtypeStruct((slices, layers, 216, sites), F32)
     row_count = slices * 2 * eigen_count // 128
@@ -503,11 +503,11 @@
         pairs = [(i % count, (i + 1) % count) for i in range(offset, count + offset, 2)]
         return lax.ppermute(value, axis, pairs + [(b, a) for a, b in pairs])
 
-    def exchanged(z_outer, z_inner, t_outer, t_inner):
+    def exchanged(z_outer, t_outer, z_inner, t_inner):
         return (
             swapped(z_outer, "space", 1),
+            swapped(t_outer, "tm", 1),
             swapped(z_inner, "space", 0),
-            swapped(t_outer, "tm", 1),
             swapped(t_inner, "tm", 0),
         )
 

time: 114 us -> 112 us (0.982)
  transfers between devices with their start and end apart: 16 -> 16, of which waited for: 0 -> 1; matrix products, arithmetic and copies ran while one was open for 0% -> 0% of each run, Pallas kernels for 6% -> 6%
where the time goes in v6:
time: 112 us
  starting transfers between devices  63.7 us (57%)
  blocking collectives  33.6 us (30%)
  Pallas kernels  13.4 us (12%)
    ppermute x16, starting transfers between devices, swapped(): return lax.ppermute(value, axis, pairs + [(b, a) for a, b in pairs])  63.7 us
    all_to_all x1, blocking collectives, on_device(): shares = lax.all_to_all(partial_sums, 'space', 0, 0, tiled=True)  18.2 us
    all_to_all x1, blocking collectives, on_device(): mixed = lax.all_to_all(mixed, 'space', 0, 0, tiled=True)  15.4 us
    pallas_call x4, Pallas kernels, local(): call(local_kernel, 3, spinor_type, flops=1 << 26, name='local')  7.04 us
  transfers between devices with their start and end apart: 16, of which 1 were waited for; matrix products, arithmetic and copies ran while one was open for 0% of the time, Pallas kernels for 6%

profile of v6, /device:TPU:1, one launch (start us, length us, event | category | flops | bytes accessed | tf_op | source)
XLA Modules:
  0.0 111.8 jit_solution(7080900562144277087)
XLA Ops:
  0.0 1.3 %entry.1 = (f32[2,2,4,2,3,16,128]{6,5,4,3,2,1,0:T(8,128)S(1)}, f32[2,2,108,128]{3,2,1,0:T(8,128)S(1)}, bf16[2,2,2,3,16,128]{5,4,3,2,1,0:T(8,128)(2,1)S(1)}, bf16...) custom-call(bf16[2,2,4,2,3,16,128]{6,5,4,3,2,1,0:T(8,128)(2,1)} %sou, ...), custom_call_target="tpu_custom_call" | custom-call | flops 4194304 | bytes 2097152 | tf_op jit(solution)/shard_map/entry/pallas_call | solution.py:517
  1.3 9.9 %collective-permute-start = (bf16[2,2,2,3,16,128]{5,4,3,2,1,0:T(8,128)(2,1)S(1)}, bf16[2,2,2,3,16,128]{5,4,3,2,1,0:T(8,128)(2,1)S(1)}, u32[]{:S(2)}, u32[]{:S(2)}) collective-permute-start(bf16[2,2,2,3,16,128]{5,4,3,2,1,0:T(8,128)(2,1)S(1)} %get-tuple-element.30), channel_id=1, source_target_pairs={{8,16},{24,32},{40,48},{56,64},{72,80},{88,96},{104,112},{120,128}... | collective-permute-start | bytes 294920 | tf_op jit(solution)/shard_map/ppermute | solution.py:504
  11.3 6.6 %collective-permute-start.1 = (bf16[2,2,2,3,16,128]{5,4,3,2,1,0:T(8,128)(2,1)S(1)}, bf16[2,2,2,3,16,128]{5,4,3,2,1,0:T(8,128)(2,1)S(1)}, u32[]{:S(2)}, u32[]{:S(2)}) collective-permute-start(bf16[2,2,2,3,16,128]{5,4,3,2,1,0:T(8,128)(2,1)S(1)} %get-tuple-element.31), channel_id=1, source_target_pairs={{1,2},{3,4},{5,6},{7,0},{2,1},{4,3},{6,5},{0,7},{9,10},{11,12},{13... | collective-permute-start | bytes 294920 | tf_op jit(solution)/shard_map/ppermute | solution.py:504
  17.9 1.9 %collective-permute-start.2 = (bf16[2,2,2,3,16,128]{5,4,3,2,1,0:T(8,128)(2,1)S(1)}, bf16[2,2,2,3,16,128]{5,4,3,2,1,0:T(8,128)(2,1)S(1)}, u32[]{:S(2)}, u32[]{:S(2)}) collective-permute-start(bf16[2,2,2,3,16,128]{5,4,3,2,1,0:T(8,128)(2,1)S(1)} %get-tuple-element.32), channel_id=1, source_target_pairs={{0,8},{16,24},{32,40},{48,56},{64,72},{80,88},{96,104},{112,120},{... | collective-permute-start | bytes 294920 | tf_op jit(solution)/shard_map/ppermute | solution.py:504
  19.9 5.4 %collective-permute-start.3 = (bf16[2,2,2,3,16,128]{5,4,3,2,1,0:T(8,128)(2,1)S(1)}, bf16[2,2,2,3,16,128]{5,4,3,2,1,0:T(8,128)(2,1)S(1)}, u32[]{:S(2)}, u32[]{:S(2)}) collective-permute-start(bf16[2,2,2,3,16,128]{5,4,3,2,1,0:T(8,128)(2,1)S(1)} %get-tuple-element.33), channel_id=1, source_target_pairs={{0,1},{2,3},{4,5},{6,7},{1,0},{3,2},{5,4},{7,6},{8,9},{10,11},{12,... | collective-permute-start | bytes 294920 | tf_op jit(solution)/shard_map/ppermute | solution.py:504
  25.3 0.2 clover_rows.1.clover
  25.5 1.8 %local.4.acc = f32[2,2,4,2,3,16,128]{6,5,4,3,2,1,0:T(8,128)S(1)} custom-call(f32[2,2,4,2,3,16,128]{6,5,4,3,2,1,0:T(8,128)S(1)} %get-tuple-element.27.psi, f32[2,2,108,128]{3,2,1,0:T(8,128)S(1)} %get-tuple-element.28.links, f32[2,2,216,128]{3,2,1,0:T(8,128)S(1)} %clover_rows.1.clover), custom_call_target="tpu_custom_call" | custom-call | flops 67108864 | bytes 2097152 | tf_op jit(solution)/shard_map/local/pallas_call | solution.py:533
  27.3 0.0 copy-start
  27.3 0.5 middle.2
  27.8 4.3 %collective-permute-start.4 = (bf16[2,2,2,3,16,128]{5,4,3,2,1,0:T(8,128)(2,1)S(1)}, bf16[2,2,2,3,16,128]{5,4,3,2,1,0:T(8,128)(2,1)S(1)}, u32[]{:S(2)}, u32[]{:S(2)}) collective-permute-start(bf16[2,2,2,3,16,128]{5,4,3,2,1,0:T(8,128)(2,1)S(1)} %get-tuple-element.35), channel_id=1, source_target_pairs={{8,16},{24,32},{40,48},{56,64},{72,80},{88,96},{104,112},{120,128}... | collective-permute-start | bytes 294920 | tf_op jit(solution)/shard_map/ppermute | solution.py:504
  32.1 3.0 %collective-permute-start.5 = (bf16[2,2,2,3,16,128]{5,4,3,2,1,0:T(8,128)(2,1)S(1)}, bf16[2,2,2,3,16,128]{5,4,3,2,1,0:T(8,128)(2,1)S(1)}, u32[]{:S(2)}, u32[]{:S(2)}) collective-permute-start(bf16[2,2,2,3,16,128]{5,4,3,2,1,0:T(8,128)(2,1)S(1)} %get-tuple-element.36), channel_id=1, source_target_pairs={{1,2},{3,4},{5,6},{7,0},{2,1},{4,3},{6,5},{0,7},{9,10},{11,12},{13... | collective-permute-start | bytes 294920 | tf_op jit(solution)/shard_map/ppermute | solution.py:504
  35.2 1.9 %collective-permute-start.6 = (bf16[2,2,2,3,16,128]{5,4,3,2,1,0:T(8,128)(2,1)S(1)}, bf16[2,2,2,3,16,128]{5,4,3,2,1,0:T(8,128)(2,1)S(1)}, u32[]{:S(2)}, u32[]{:S(2)}) collective-permute-start(bf16[2,2,2,3,16,128]{5,4,3,2,1,0:T(8,128)(2,1)S(1)} %get-tuple-element.37), channel_id=1, source_target_pairs={{0,8},{16,24},{32,40},{48,56},{64,72},{80,88},{96,104},{112,120},{... | collective-permute-start | bytes 294920 | tf_op jit(solution)/shard_map/ppermute | solution.py:504
  37.1 1.9 %collective-permute-start.7 = (bf16[2,2,2,3,16,128]{5,4,3,2,1,0:T(8,128)(2,1)S(1)}, bf16[2,2,2,3,16,128]{5,4,3,2,1,0:T(8,128)(2,1)S(1)}, u32[]{:S(2)}, u32[]{:S(2)}) collective-permute-start(bf16[2,2,2,3,16,128]{5,4,3,2,1,0:T(8,128)(2,1)S(1)} %get-tuple-element.38), channel_id=1, source_target_pairs={{0,1},{2,3},{4,5},{6,7},{1,0},{3,2},{5,4},{7,6},{8,9},{10,11},{12,... | collective-permute-start | bytes 294920 | tf_op jit(solution)/shard_map/ppermute | solution.py:504
  39.0 1.8 %local.5.acc = f32[2,2,4,2,3,16,128]{6,5,4,3,2,1,0:T(8,128)S(1)} custom-call(f32[2,2,4,2,3,16,128]{6,5,4,3,2,1,0:T(8,128)S(1)} %get-tuple-element.34.psi, f32[2,2,108,128]{3,2,1,0:T(8,128)S(1)} %get-tuple-element.28.links, f32[2,2,216,128]{3,2,1,0:T(8,128)S(1)} %clover_rows.1.clover), custom_call_target="tpu_custom_call" | custom-call | flops 67108864 | bytes 2097152 | tf_op jit(solution)/shard_map/local/pallas_call | solution.py:533
  40.8 0.7 collective-permute-done.6.refs_2_
  41.5 1.0 coefficients.1
  42.5 18.2 %all_to_all.10.shares = f32[64,8,128]{2,1,0:T(8,128)S(1)} all-to-all(f32[64,8,128]{2,1,0:T(8,128)S(1)} %coefficients.1), channel_id=1, replica_groups=mesh['space'=64,'tm'=8] {'space'}, dimensions={0} | all-to-all | bytes 524288 | tf_op jit(solution)/shard_map/all_to_all | solution.py:555
  60.8 0.7 mix.1
  61.4 15.4 %all_to_all.11.mixed = bf16[64,8,128]{2,1,0:T(8,128)(2,1)S(1)} all-to-all(bf16[64,8,128]{2,1,0:T(8,128)(2,1)S(1)} %mix.1), channel_id=1, replica_groups=mesh['space'=64,'tm'=8] {'space'}, dimensions={0} | all-to-all | bytes 262144 | tf_op jit(solution)/shard_map/all_to_all | solution.py:562
  76.8 1.1 %expand.1 = (f32[2,2,4,2,3,16,128]{6,5,4,3,2,1,0:T(8,128)S(1)}, bf16[2,2,2,3,16,128]{5,4,3,2,1,0:T(8,128)(2,1)S(1)}, bf16[2,2,2,3,16,128]{5,4,3,2,1,0:T(8,128)(2...) custom-call(bf16[64,8,128]{2,1,0:T(8,128)(2,1)S(1)} %all_to_all.11.mixed, ...), custom_call_target="tpu_custom_call" | custom-call | flops 4194304 | bytes 2097152 | tf_op jit(solution)/shard_map/expand/pallas_call | solution.py:563
  77.9 3.7 %collective-permute-start.8 = (bf16[2,2,2,3,16,128]{5,4,3,2,1,0:T(8,128)(2,1)S(1)}, bf16[2,2,2,3,16,128]{5,4,3,2,1,0:T(8,128)(2,1)S(1)}, u32[]{:S(2)}, u32[]{:S(2)}) collective-permute-start(bf16[2,2,2,3,16,128]{5,4,3,2,1,0:T(8,128)(2,1)S(1)} %get-tuple-element.40), channel_id=1, source_target_pairs={{8,16},{24,32},{40,48},{56,64},{72,80},{88,96},{104,112},{120,128}... | collective-permute-start | bytes 294920 | tf_op jit(solution)/shard_map/ppermute | solution.py:504
  81.6 6.5 %collective-permute-start.9 = (bf16[2,2,2,3,16,128]{5,4,3,2,1,0:T(8,128)(2,1)S(1)}, bf16[2,2,2,3,16,128]{5,4,3,2,1,0:T(8,128)(2,1)S(1)}, u32[]{:S(2)}, u32[]{:S(2)}) collective-permute-start(bf16[2,2,2,3,16,128]{5,4,3,2,1,0:T(8,128)(2,1)S(1)} %get-tuple-element.41), channel_id=1, source_target_pairs={{1,2},{3,4},{5,6},{7,0},{2,1},{4,3},{6,5},{0,7},{9,10},{11,12},{13... | collective-permute-start | bytes 294920 | tf_op jit(solution)/shard_map/ppermute | solution.py:504
  88.1 1.9 %collective-permute-start.10 = (bf16[2,2,2,3,16,128]{5,4,3,2,1,0:T(8,128)(2,1)S(1)}, bf16[2,2,2,3,16,128]{5,4,3,2,1,0:T(8,128)(2,1)S(1)}, u32[]{:S(2)}, u32[]{:S(2)}) collective-permute-start(bf16[2,2,2,3,16,128]{5,4,3,2,1,0:T(8,128)(2,1)S(1)} %get-tuple-element.42), channel_id=1, source_target_pairs={{0,8},{16,24},{32,40},{48,56},{64,72},{80,88},{96,104},{112,120},{... | collective-permute-start | bytes 294920 | tf_op jit(solution)/shard_map/ppermute | solution.py:504
  90.0 1.9 %collective-permute-start.11 = (bf16[2,2,2,3,16,128]{5,4,3,2,1,0:T(8,128)(2,1)S(1)}, bf16[2,2,2,3,16,128]{5,4,3,2,1,0:T(8,128)(2,1)S(1)}, u32[]{:S(2)}, u32[]{:S(2)}) collective-permute-start(bf16[2,2,2,3,16,128]{5,4,3,2,1,0:T(8,128)(2,1)S(1)} %get-tuple-element.43), channel_id=1, source_target_pairs={{0,1},{2,3},{4,5},{6,7},{1,0},{3,2},{5,4},{7,6},{8,9},{10,11},{12,... | collective-permute-start | bytes 294920 | tf_op jit(solution)/shard_map/ppermute | solution.py:504
  92.0 1.8 %local.6.acc = f32[2,2,4,2,3,16,128]{6,5,4,3,2,1,0:T(8,128)S(1)} custom-call(f32[2,2,4,2,3,16,128]{6,5,4,3,2,1,0:T(8,128)S(1)} %get-tuple-element.39.psi, f32[2,2,108,128]{3,2,1,0:T(8,128)S(1)} %get-tuple-element.28.links, f32[2,2,216,128]{3,2,1,0:T(8,128)S(1)} %clover_rows.1.clover), custom_call_target="tpu_custom_call" | custom-call | flops 67108864 | bytes 2097152 | tf_op jit(solution)/shard_map/local/pallas_call | solution.py:533
  93.8 0.5 middle.3
  94.3 6.2 %collective-permute-start.12 = (bf16[2,2,2,3,16,128]{5,4,3,2,1,0:T(8,128)(2,1)S(1)}, bf16[2,2,2,3,16,128]{5,4,3,2,1,0:T(8,128)(2,1)S(1)}, u32[]{:S(2)}, u32[]{:S(2)}) collective-permute-start(bf16[2,2,2,3,16,128]{5,4,3,2,1,0:T(8,128)(2,1)S(1)} %get-tuple-element.45), channel_id=1, source_target_pairs={{8,16},{24,32},{40,48},{56,64},{72,80},{88,96},{104,112},{120,128}... | collective-permute-start | bytes 294920 | tf_op jit(solution)/shard_map/ppermute | solution.py:504
  100.5 4.0 %collective-permute-start.13 = (bf16[2,2,2,3,16,128]{5,4,3,2,1,0:T(8,128)(2,1)S(1)}, bf16[2,2,2,3,16,128]{5,4,3,2,1,0:T(8,128)(2,1)S(1)}, u32[]{:S(2)}, u32[]{:S(2)}) collective-permute-start(bf16[2,2,2,3,16,128]{5,4,3,2,1,0:T(8,128)(2,1)S(1)} %get-tuple-element.46), channel_id=1, source_target_pairs={{1,2},{3,4},{5,6},{7,0},{2,1},{4,3},{6,5},{0,7},{9,10},{11,12},{13... | collective-permute-start | bytes 294920 | tf_op jit(solution)/shard_map/ppermute | solution.py:504
  104.5 1.9 %collective-permute-start.14 = (bf16[2,2,2,3,16,128]{5,4,3,2,1,0:T(8,128)(2,1)S(1)}, bf16[2,2,2,3,16,128]{5,4,3,2,1,0:T(8,128)(2,1)S(1)}, u32[]{:S(2)}, u32[]{:S(2)}) collective-permute-start(bf16[2,2,2,3,16,128]{5,4,3,2,1,0:T(8,128)(2,1)S(1)} %get-tuple-element.47), channel_id=1, source_target_pairs={{0,8},{16,24},{32,40},{48,56},{64,72},{80,88},{96,104},{112,120},{... | collective-permute-start | bytes 294920 | tf_op jit(solution)/shard_map/ppermute | solution.py:504
  106.4 2.5 %collective-permute-start.15 = (bf16[2,2,2,3,16,128]{5,4,3,2,1,0:T(8,128)(2,1)S(1)}, bf16[2,2,2,3,16,128]{5,4,3,2,1,0:T(8,128)(2,1)S(1)}, u32[]{:S(2)}, u32[]{:S(2)}) collective-permute-start(bf16[2,2,2,3,16,128]{5,4,3,2,1,0:T(8,128)(2,1)S(1)} %get-tuple-element.48), channel_id=1, source_target_pairs={{0,1},{2,3},{4,5},{6,7},{1,0},{3,2},{5,4},{7,6},{8,9},{10,11},{12,... | collective-permute-start | bytes 294920 | tf_op jit(solution)/shard_map/ppermute | solution.py:504
  108.9 1.8 %local.7.acc = f32[2,2,4,2,3,16,128]{6,5,4,3,2,1,0:T(8,128)S(1)} custom-call(f32[2,2,4,2,3,16,128]{6,5,4,3,2,1,0:T(8,128)S(1)} %get-tuple-element.44.psi, f32[2,2,108,128]{3,2,1,0:T(8,128)S(1)} %get-tuple-element.28.links, f32[2,2,216,128]{3,2,1,0:T(8,128)S(1)} %clover_rows.1.clover), custom_call_target="tpu_custom_call" | custom-call | flops 67108864 | bytes 2097152 | tf_op jit(solution)/shard_map/local/pallas_call | solution.py:533
  110.7 1.1 last.1
  (18 shorter events, 0.0 us)
Async XLA Ops:
  1.3 26.0 %collective-permute-start = (bf16[2,2,2,3,16,128]{5,4,3,2,1,0:T(8,128)(2,1)S(1)}, bf16[2,2,2,3,16,128]{5,4,3,2,1,0:T(8,128)(2,1)S(1)}, u32[]{:S(2)}, u32[]{:S(2)}) collective-permute-start(bf16[2,2,2,3,16,128]{5,4,3,2,1,0:T(8,128)(2,1)S(1)} %get-tuple-element.30), channel_id=1, source_target_pairs={{8,16},{24,32},{40,48},{56,64},{72,80},{88,96},{104,112},{120,128}... | collective-permute-start | bytes 294920 | tf_op jit(solution)/shard_map/ppermute | solution.py:504
  11.3 16.0 %collective-permute-start.1 = (bf16[2,2,2,3,16,128]{5,4,3,2,1,0:T(8,128)(2,1)S(1)}, bf16[2,2,2,3,16,128]{5,4,3,2,1,0:T(8,128)(2,1)S(1)}, u32[]{:S(2)}, u32[]{:S(2)}) collective-permute-start(bf16[2,2,2,3,16,128]{5,4,3,2,1,0:T(8,128)(2,1)S(1)} %get-tuple-element.31), channel_id=1, source_target_pairs={{1,2},{3,4},{5,6},{7,0},{2,1},{4,3},{6,5},{0,7},{9,10},{11,12},{13... | collective-permute-start | bytes 294920 | tf_op jit(solution)/shard_map/ppermute | solution.py:504
  17.9 9.4 %collective-permute-start.2 = (bf16[2,2,2,3,16,128]{5,4,3,2,1,0:T(8,128)(2,1)S(1)}, bf16[2,2,2,3,16,128]{5,4,3,2,1,0:T(8,128)(2,1)S(1)}, u32[]{:S(2)}, u32[]{:S(2)}) collective-permute-start(bf16[2,2,2,3,16,128]{5,4,3,2,1,0:T(8,128)(2,1)S(1)} %get-tuple-element.32), channel_id=1, source_target_pairs={{0,8},{16,24},{32,40},{48,56},{64,72},{80,88},{96,104},{112,120},{... | collective-permute-start | bytes 294920 | tf_op jit(solution)/shard_map/ppermute | solution.py:504
  19.9 7.5 %collective-permute-start.3 = (bf16[2,2,2,3,16,128]{5,4,3,2,1,0:T(8,128)(2,1)S(1)}, bf16[2,2,2,3,16,128]{5,4,3,2,1,0:T(8,128)(2,1)S(1)}, u32[]{:S(2)}, u32[]{:S(2)}) collective-permute-start(bf16[2,2,2,3,16,128]{5,4,3,2,1,0:T(8,128)(2,1)S(1)} %get-tuple-element.33), channel_id=1, source_target_pairs={{0,1},{2,3},{4,5},{6,7},{1,0},{3,2},{5,4},{7,6},{8,9},{10,11},{12,... | collective-permute-start | bytes 294920 | tf_op jit(solution)/shard_map/ppermute | solution.py:504
  27.3 14.3 %copy-start = (bf16[2,2,2,3,256,128]{5,4,3,2,1,0:T(8,128)(2,1)S(1)}, bf16[2,2,2,3,256,128]{5,4,3,2,1,0:T(8,128)(2,1)}, u32[]{:S(2)}) copy-start(bf16[2,2,2,3,256,128]{5,4,3,2,1,0:T(8,128)(2,1)} %vectors.1) | copy-start | bytes 4718596
  27.8 13.0 %collective-permute-start.4 = (bf16[2,2,2,3,16,128]{5,4,3,2,1,0:T(8,128)(2,1)S(1)}, bf16[2,2,2,3,16,128]{5,4,3,2,1,0:T(8,128)(2,1)S(1)}, u32[]{:S(2)}, u32[]{:S(2)}) collective-permute-start(bf16[2,2,2,3,16,128]{5,4,3,2,1,0:T(8,128)(2,1)S(1)} %get-tuple-element.35), channel_id=1, source_target_pairs={{8,16},{24,32},{40,48},{56,64},{72,80},{88,96},{104,112},{120,128}... | collective-permute-start | bytes 294920 | tf_op jit(solution)/shard_map/ppermute | solution.py:504
  32.1 8.7 %collective-permute-start.5 = (bf16[2,2,2,3,16,128]{5,4,3,2,1,0:T(8,128)(2,1)S(1)}, bf16[2,2,2,3,16,128]{5,4,3,2,1,0:T(8,128)(2,1)S(1)}, u32[]{:S(2)}, u32[]{:S(2)}) collective-permute-start(bf16[2,2,2,3,16,128]{5,4,3,2,1,0:T(8,128)(2,1)S(1)} %get-tuple-element.36), channel_id=1, source_target_pairs={{1,2},{3,4},{5,6},{7,0},{2,1},{4,3},{6,5},{0,7},{9,10},{11,12},{13... | collective-permute-start | bytes 294920 | tf_op jit(solution)/shard_map/ppermute | solution.py:504
  35.2 6.4 %collective-permute-start.6 = (bf16[2,2,2,3,16,128]{5,4,3,2,1,0:T(8,128)(2,1)S(1)}, bf16[2,2,2,3,16,128]{5,4,3,2,1,0:T(8,128)(2,1)S(1)}, u32[]{:S(2)}, u32[]{:S(2)}) collective-permute-start(bf16[2,2,2,3,16,128]{5,4,3,2,1,0:T(8,128)(2,1)S(1)} %get-tuple-element.37), channel_id=1, source_target_pairs={{0,8},{16,24},{32,40},{48,56},{64,72},{80,88},{96,104},{112,120},{... | collective-permute-start | bytes 294920 | tf_op jit(solution)/shard_map/ppermute | solution.py:504
  37.1 4.5 %collective-permute-start.7 = (bf16[2,2,2,3,16,128]{5,4,3,2,1,0:T(8,128)(2,1)S(1)}, bf16[2,2,2,3,16,128]{5,4,3,2,1,0:T(8,128)(2,1)S(1)}, u32[]{:S(2)}, u32[]{:S(2)}) collective-permute-start(bf16[2,2,2,3,16,128]{5,4,3,2,1,0:T(8,128)(2,1)S(1)} %get-tuple-element.38), channel_id=1, source_target_pairs={{0,1},{2,3},{4,5},{6,7},{1,0},{3,2},{5,4},{7,6},{8,9},{10,11},{12,... | collective-permute-start | bytes 294920 | tf_op jit(solution)/shard_map/ppermute | solution.py:504
  40.8 20.0 %copy-start.1 = (bf16[2,2,256,256]{3,2,1,0:T(8,128)(2,1)S(1)}, bf16[2,2,256,256]{3,2,1,0:T(8,128)(2,1)}, u32[]{:S(2)}) copy-start(bf16[2,2,256,256]{3,2,1,0:T(8,128)(2,1)} %elemental.1) | copy-start | bytes 1572868
  77.9 15.8 %collective-permute-start.8 = (bf16[2,2,2,3,16,128]{5,4,3,2,1,0:T(8,128)(2,1)S(1)}, bf16[2,2,2,3,16,128]{5,4,3,2,1,0:T(8,128)(2,1)S(1)}, u32[]{:S(2)}, u32[]{:S(2)}) collective-permute-start(bf16[2,2,2,3,16,128]{5,4,3,2,1,0:T(8,128)(2,1)S(1)} %get-tuple-element.40), channel_id=1, source_target_pairs={{8,16},{24,32},{40,48},{56,64},{72,80},{88,96},{104,112},{120,128}... | collective-permute-start | bytes 294920 | tf_op jit(solution)/shard_map/ppermute | solution.py:504
  81.6 12.1 %collective-permute-start.9 = (bf16[2,2,2,3,16,128]{5,4,3,2,1,0:T(8,128)(2,1)S(1)}, bf16[2,2,2,3,16,128]{5,4,3,2,1,0:T(8,128)(2,1)S(1)}, u32[]{:S(2)}, u32[]{:S(2)}) collective-permute-start(bf16[2,2,2,3,16,128]{5,4,3,2,1,0:T(8,128)(2,1)S(1)} %get-tuple-element.41), channel_id=1, source_target_pairs={{1,2},{3,4},{5,6},{7,0},{2,1},{4,3},{6,5},{0,7},{9,10},{11,12},{13... | collective-permute-start | bytes 294920 | tf_op jit(solution)/shard_map/ppermute | solution.py:504
  88.1 5.6 %collective-permute-start.10 = (bf16[2,2,2,3,16,128]{5,4,3,2,1,0:T(8,128)(2,1)S(1)}, bf16[2,2,2,3,16,128]{5,4,3,2,1,0:T(8,128)(2,1)S(1)}, u32[]{:S(2)}, u32[]{:S(2)}) collective-permute-start(bf16[2,2,2,3,16,128]{5,4,3,2,1,0:T(8,128)(2,1)S(1)} %get-tuple-element.42), channel_id=1, source_target_pairs={{0,8},{16,24},{32,40},{48,56},{64,72},{80,88},{96,104},{112,120},{... | collective-permute-start | bytes 294920 | tf_op jit(solution)/shard_map/ppermute | solution.py:504
  90.0 3.7 %collective-permute-start.11 = (bf16[2,2,2,3,16,128]{5,4,3,2,1,0:T(8,128)(2,1)S(1)}, bf16[2,2,2,3,16,128]{5,4,3,2,1,0:T(8,128)(2,1)S(1)}, u32[]{:S(2)}, u32[]{:S(2)}) collective-permute-start(bf16[2,2,2,3,16,128]{5,4,3,2,1,0:T(8,128)(2,1)S(1)} %get-tuple-element.43), channel_id=1, source_target_pairs={{0,1},{2,3},{4,5},{6,7},{1,0},{3,2},{5,4},{7,6},{8,9},{10,11},{12,... | collective-permute-start | bytes 294920 | tf_op jit(solution)/shard_map/ppermute | solution.py:504
  94.3 16.4 %collective-permute-start.12 = (bf16[2,2,2,3,16,128]{5,4,3,2,1,0:T(8,128)(2,1)S(1)}, bf16[2,2,2,3,16,128]{5,4,3,2,1,0:T(8,128)(2,1)S(1)}, u32[]{:S(2)}, u32[]{:S(2)}) collective-permute-start(bf16[2,2,2,3,16,128]{5,4,3,2,1,0:T(8,128)(2,1)S(1)} %get-tuple-element.45), channel_id=1, source_target_pairs={{8,16},{24,32},{40,48},{56,64},{72,80},{88,96},{104,112},{120,128}... | collective-permute-start | bytes 294920 | tf_op jit(solution)/shard_map/ppermute | solution.py:504
  100.5 10.2 %collective-permute-start.13 = (bf16[2,2,2,3,16,128]{5,4,3,2,1,0:T(8,128)(2,1)S(1)}, bf16[2,2,2,3,16,128]{5,4,3,2,1,0:T(8,128)(2,1)S(1)}, u32[]{:S(2)}, u32[]{:S(2)}) collective-permute-start(bf16[2,2,2,3,16,128]{5,4,3,2,1,0:T(8,128)(2,1)S(1)} %get-tuple-element.46), channel_id=1, source_target_pairs={{1,2},{3,4},{5,6},{7,0},{2,1},{4,3},{6,5},{0,7},{9,10},{11,12},{13... | collective-permute-start | bytes 294920 | tf_op jit(solution)/shard_map/ppermute | solution.py:504
  104.5 6.2 %collective-permute-start.14 = (bf16[2,2,2,3,16,128]{5,4,3,2,1,0:T(8,128)(2,1)S(1)}, bf16[2,2,2,3,16,128]{5,4,3,2,1,0:T(8,128)(2,1)S(1)}, u32[]{:S(2)}, u32[]{:S(2)}) collective-permute-start(bf16[2,2,2,3,16,128]{5,4,3,2,1,0:T(8,128)(2,1)S(1)} %get-tuple-element.47), channel_id=1, source_target_pairs={{0,8},{16,24},{32,40},{48,56},{64,72},{80,88},{96,104},{112,120},{... | collective-permute-start | bytes 294920 | tf_op jit(solution)/shard_map/ppermute | solution.py:504
  106.4 4.3 %collective-permute-start.15 = (bf16[2,2,2,3,16,128]{5,4,3,2,1,0:T(8,128)(2,1)S(1)}, bf16[2,2,2,3,16,128]{5,4,3,2,1,0:T(8,128)(2,1)S(1)}, u32[]{:S(2)}, u32[]{:S(2)}) collective-permute-start(bf16[2,2,2,3,16,128]{5,4,3,2,1,0:T(8,128)(2,1)S(1)} %get-tuple-element.48), channel_id=1, source_target_pairs={{0,1},{2,3},{4,5},{6,7},{1,0},{3,2},{5,4},{7,6},{8,9},{10,11},{12,... | collective-permute-start | bytes 294920 | tf_op jit(solution)/shard_map/ppermute | solution.py:504
